TPU v7x, 32 devices: a whole 2x2x4 slice. The times are simulated.
32 devices in a mesh: ka: 8 (over z, y), cfg: 4 (over x, core).
Axes of the slice: x: 2, y: 2, z: 4, core: 2. Of those that a mesh axis runs over, the one named last changes fastest.
Arguments:
- medium_t: float32 [2, 2, 16, 16, 16], replicated, may hold values from -6 to 6
- structure: float32 [2, 2, 16, 16, 4096], P(None, None, None, None, ('ka', 'cfg')), may hold values from -0.12 to 0.12
- kmap: int32 [4096], P(('ka', 'cfg')), may hold values from 0 to 15, as said below
- occupation: int32 [32, 16], P(('ka', 'cfg')), may hold values from 0 to 1
- cfg_weight: float32 [32], P(('ka', 'cfg')), may hold values from 1 to 30
- shift_a: float32 [2, 2, 16, 16], replicated, may hold values from -0.18 to 0.18
- shift_b: float32 [2, 2, 16, 16], replicated, may hold values from -0.18 to 0.18
Outputs:
- coarse_tau: float32 [2, 2, 16, 16, 16], replicated
- avg_tau: float32 [2, 2, 256, 256], P(None, None, 'cfg')
- correction: float32 [2, 2, 4096], P(None, None, ('ka', 'cfg'))
Inputs may be any that keep to these rules, and one draw needn't show every extreme that they name: `kmap`: every cluster momentum is named by exactly 4096 / 16 k-points.
All inputs are finite; a program needn't handle non-finite values.
Results may differ from a plain program's by a relative error of at most 0.00015.
Values sent between devices are 32-bit elements; how exact they have to be, the bound alone decides.
No kernel may reach another device: no remote copies, remote signals or barrier semaphores. Data moves between devices by JAX's collectives and lax.ppermute only.
A program may use at most 128 MiB of HBM per device.

v0:
```python
import functools
import math

import jax
import jax.numpy as jnp
import numpy as np
from jax import lax
from jax.experimental import pallas as pl
from jax.experimental.pallas import tpu as pltpu
from jax.sharding import PartitionSpec as P

ENERGIES = 2
F32 = jnp.float32
BF16 = jnp.bfloat16
PAD_ROWS = 8
KERNEL_VMEM = 20 << 20


def site_geometry(count_sites):
    places = np.arange(count_sites)
    half_n = count_sites // 2
    cell = places % half_n
    site_xyz = np.stack([cell // 4, cell // 2 % 2, cell % 2], axis=1).astype(np.float64)
    site_xyz = site_xyz + 0.5 * (places >= half_n)[:, None]
    mom_hkl = np.stack([places // 4, places // 2 % 2, places % 2], axis=1).astype(np.float64)
    angles = math.pi * (mom_hkl[:, None, :] * site_xyz[None, :, :]).sum(axis=2)
    place_diff = np.zeros((count_sites, count_sites), np.int32)
    for i in range(count_sites):
        for j in range(count_sites):
            gap = (site_xyz[i] - site_xyz[j]) % 2.0
            place_diff[i, j] = int(np.argmin(np.abs(site_xyz % 2.0 - gap).sum(axis=1)))
    return angles, place_diff


def phase_constants(count_sites, chans):
    angles, place_diff = site_geometry(count_sites)
    cos_ms = np.rint(np.cos(angles))
    sin_ms = np.rint(np.sin(angles))
    eye = np.eye(chans)
    fwd = np.stack([np.kron(cos_ms, eye), np.kron(-sin_ms, eye)]) / count_sites
    back = np.stack([np.kron(cos_ms.T, eye), np.kron(sin_ms.T, eye)]) / count_sites
    rows = np.stack([np.repeat(cos_ms.T, chans, axis=1), np.repeat(sin_ms.T, chans, axis=1)])
    return (
        fwd.astype(np.float32),
        back.astype(np.float32),
        rows.astype(np.float32),
        place_diff,
    )


def iota(shape, dim):
    return lax.broadcasted_iota(jnp.int32, shape, dim)


def split(value, pieces):
    out = []
    for step in range(pieces):
        part = value.astype(BF16)
        out.append(part)
        if step + 1 < pieces:
            value = value - part.astype(F32)
    return out


def mm(left, right):
    return jnp.dot(left, right, preferred_element_type=F32)


def mm_nt(left, right):
    return lax.dot_general(left, right, (((1,), (1,)), ((), ())), preferred_element_type=F32)


def mm_exact(left, right_bf16, pieces=3):
    parts = split(left, pieces)
    total = mm(parts[-1], right_bf16)
    for part in parts[-2::-1]:
        total = total + mm(part, right_bf16)
    return total


def mm3(left, right):
    left_hi, left_lo = split(left, 2)
    right_hi, right_lo = split(right, 2)
    return mm(left_hi, right_lo) + mm(left_lo, right_hi) + mm(left_hi, right_hi)


def mm_high(left, right):
    return jnp.dot(left, right, preferred_element_type=F32, precision=lax.Precision.HIGHEST)


def cmul(left, right, mul=mm3):
    rows = left[0].shape[0]
    both = jnp.concatenate(left, axis=0)
    by_real = mul(both, right[0])
    by_imag = mul(both, right[1])
    return (by_real[:rows] - by_imag[rows:], by_imag[:rows] + by_real[rows:])


def cadd(*terms):
    real, imag = terms[0]
    for term in terms[1:]:
        real, imag = real + term[0], imag + term[1]
    return (real, imag)


def cscale(value, factor):
    return (value[0] * factor, value[1] * factor)


def block_diag(row, chans):
    width = row.shape[1]
    tiled = jnp.concatenate([row] * (width // chans), axis=0)
    keep = iota((width, width), 0) // chans == iota((width, width), 1) // chans
    return jnp.where(keep, tiled, 0.0)


def batch_mul(left, right, write, chans):
    group = 4

    def body(step, carry):
        base = step * (group * chans)
        sums = [[None] * 3 for _ in range(group)]
        for b in range(chans):
            rights = [right[part, b * chans : (b + 1) * chans, :] for part in range(3)]
            for g in range(group):
                for part in range(3):
                    lane = left[part, pl.ds(base + (g * chans + b), 1), :]
                    term = lane * rights[part]
                    old = sums[g][part]
                    sums[g][part] = term if old is None else old + term
        for g in range(group):
            both, twice, cross = sums[g]
            write(base + g * chans, both - twice, cross - both - twice)
        return carry

    lax.fori_loop(0, chans // group, body, 0)


def put3(ref, base, count, real, imag):
    rows = pl.ds(pl.multiple_of(base, count), count)
    ref[0, rows, :] = real
    ref[1, rows, :] = imag
    ref[2, rows, :] = real + imag


def first_kernel(
    cfg_at, medium, structure, kmap, occupation, weight,
    keep, send, z_first, z_second, y_first, y_second, y_row, y_s, g_s, f_s, part_s,
):
    chans = structure.shape[2]
    count_k = structure.shape[4]
    count_m = medium.shape[3]
    width = count_m * chans
    flat = chans * chans
    momenta = kmap[...]
    onehot = (momenta == iota((count_m, count_k), 0)).astype(BF16)
    wide = (momenta == iota((width, count_k), 0) // chans).astype(BF16)
    same = iota((flat, width), 0) % chans == iota((flat, width), 1) % chans
    lanes_of = (iota((count_m, width), 0) == iota((count_m, width), 1) // chans).astype(BF16)

    def fold(value):
        return jnp.sum(jnp.where(same, value, 0.0).reshape(chans, chans, width), axis=1)

    for energy, (z_out, y_out) in enumerate(((z_first, y_first), (z_second, y_second))):
        for part in range(2):
            med = medium[energy, part]
            y_row[energy, part] = fold(mm_exact(med, lanes_of))
            value = mm_exact(med, onehot)
            y_s[part] = value
            y_out[part] = value
            g_s[part] = structure[energy, part].reshape(flat, count_k)
        y_s[2] = y_s[0] + y_s[1]
        g_s[2] = g_s[0] + g_s[1]

        def write_f(base, real, imag):
            put3(f_s, base, chans, real, imag)

        batch_mul(y_s, g_s, write_f, chans)

        def write_z(base, real, imag, z_out=z_out):
            rows = pl.ds(pl.multiple_of(base, chans), chans)
            z_out[0, rows, :] = real + f_s[0, rows, :]
            z_out[1, rows, :] = imag + f_s[1, rows, :]

        batch_mul(f_s, f_s, write_z, chans)
        for part in range(2):
            parts = split(z_out[part], 3)
            total = mm_nt(parts[2], wide) + mm_nt(parts[1], wide) + mm_nt(parts[0], wide)
            part_s[energy, part * chans : (part + 1) * chans, :] = fold(total)

    sites = occupation.shape[1]
    pairs = sites * sites
    from_l = (iota((sites, pairs), 0) == iota((sites, pairs), 1) // sites).astype(BF16)
    from_j = (iota((sites, pairs), 0) == iota((sites, pairs), 1) % sites).astype(BF16)
    diag = iota((sites, sites), 0) == iota((sites, sites), 1)
    triple = jnp.zeros((sites, pairs), F32)
    weight_sum = jnp.zeros((1, 1), F32)
    for g in range(occupation.shape[0]):
        filled = occupation[g : g + 1, :].astype(F32)
        square = jnp.broadcast_to(filled, (sites, sites))
        column = jnp.sum(jnp.where(diag, square, 0.0), axis=1, keepdims=True)
        row_l = mm(square.astype(BF16), from_l)
        row_j = mm(square.astype(BF16), from_j)
        scale = weight[0:1, g : g + 1]
        triple = triple + column * (row_l * row_j) * scale
        weight_sum = weight_sum + scale
    own = cfg_at[0] % 2
    half = 2 * chans
    keep[0:half, :] = part_s[own]
    send[0:half, :] = part_s[1 - own]
    for ref in (keep, send):
        ref[half : half + sites, :] = triple
        ref[half + sites : half + sites + PAD_ROWS, :] = jnp.broadcast_to(
            weight_sum, (PAD_ROWS, pairs)
        )


def square_kernel(y_in, z_in, out, y_s, z_s, t_s):
    flat = out.shape[1]
    chans = math.isqrt(flat)
    for part in range(2):
        y_s[part] = y_in[part]
        z_s[part] = z_in[part]
    y_s[2] = y_in[0] + y_in[1]
    z_s[2] = z_in[0] + z_in[1]

    def write_t(base, real, imag):
        rows = pl.ds(pl.multiple_of(base, chans), chans)
        put3(t_s, base, chans, real + y_s[0, rows, :], imag + y_s[1, rows, :])

    batch_mul(z_s, y_s, write_t, chans)

    def write_o(base, real, imag):
        rows = pl.ds(pl.multiple_of(base, chans), chans)
        out[0, rows, :] = real
        out[1, rows, :] = imag

    batch_mul(t_s, t_s, write_o, chans)


def cluster_kernel(
    per_moment, own_rows,
    cfg_at, diff_tab, summed, y_row, shift_a, shift_b, fwd, back, phases,
    keep, send, lhs_s, site_s, corr_s, p_s, t3_s, a_s, n_s,
):
    own = cfg_at[0] % 2
    chans = shift_a.shape[2]
    width = summed.shape[1]
    sites = phases.shape[1]
    own_sites = own_rows // chans
    rows_n = 2 * own_rows
    own_start = cfg_at[0] * own_sites
    other_start = (cfg_at[0] + 1 - 2 * own) * own_sites
    cols = (slice(0, chans), slice(chans, 2 * chans))

    y_val = (y_row[own, 0], y_row[own, 1])
    z_val = (summed[cols[0], :], summed[cols[1], :])
    y_diag = tuple(block_diag(v, chans) for v in y_val)
    coarse = cadd(y_val, cscale(cmul(z_val, y_diag), 1.0 / per_moment))

    base_t = (shift_b[own, 0], shift_b[own, 1])
    step_t = (shift_a[own, 0] - base_t[0], shift_a[own, 1] - base_t[1])

    def left_small(small, value):
        stack = jnp.concatenate(small, axis=0)
        by_real = mm_high(stack, value[0])
        by_imag = mm_high(stack, value[1])
        return (by_real[cols[0]] - by_imag[cols[1]], by_imag[cols[0]] + by_real[cols[1]])

    b_diag = tuple(block_diag(v, chans) for v in left_small(base_t, coarse))
    series = [coarse]
    for _ in range(3):
        series.append(cscale(cmul(series[-1], b_diag), -1.0))
    kern = [left_small(step_t, series[n]) for n in range(3)]
    whole = cadd(*series)

    for i in range(sites):
        phase = (phases[0, i : i + 1, :], phases[1, i : i + 1, :])
        for n, (real, imag) in enumerate(kern):
            start = n * width + i * chans
            lhs_s[0, start : start + chans, :] = phase[0] * real - phase[1] * imag
            lhs_s[1, start : start + chans, :] = phase[0] * imag + phase[1] * real

    base = 3 * width
    for i in range(2 * own_sites):
        site = own_start + i if i < own_sites else other_start + (i - own_sites)
        phase = (phases[0, pl.ds(site, 1), :], phases[1, pl.ds(site, 1), :])
        for n, (real, imag) in enumerate([whole] + series[:3]):
            start = base + n * rows_n + i * chans
            lhs_s[0, start : start + chans, :] = phase[0] * real - phase[1] * imag
            lhs_s[1, start : start + chans, :] = phase[0] * imag + phase[1] * real
    fwd_val = (fwd[0], fwd[1])

    for start in range(0, base + 4 * rows_n, width):
        rows = slice(start, start + width)
        out = cmul(
            (lhs_s[0, rows, :], lhs_s[1, rows, :]),
            fwd_val,
            functools.partial(mm_exact, pieces=2),
        )
        site_s[0, rows, :] = out[0]
        site_s[1, rows, :] = out[1]

    norm = 1.0 / summed[2 * chans + sites : 2 * chans + sites + 1, :]
    triple = summed[2 * chans : 2 * chans + sites, :] * norm
    lane_l = iota((sites, width), 1) // sites
    lane_j = iota((sites, width), 1) % sites
    row_i = iota((sites, width), 0)
    pair = jnp.where(lane_l == row_i, triple, 0.0)
    single = jnp.sum(jnp.where(lane_j == row_i, pair, 0.0), axis=0, keepdims=True)
    stack = jnp.concatenate(
        [block_diag(triple, sites), pair, jnp.broadcast_to(single, (PAD_ROWS, width))], axis=0
    )
    spread_j = (
        iota((width, width), 0) % sites == iota((width, width), 1) // chans
    ).astype(BF16)
    corr_s[...] = mm_exact(stack, spread_j)

    hi_lo = []
    for part in range(2):
        hi, lo = split(site_s[part, 0:width, 0:chans], 2)
        hi_lo += [hi.astype(F32), hi.astype(F32), lo.astype(F32)]
    for n, piece in enumerate(hi_lo):
        a_s[:, n * chans : (n + 1) * chans] = piece
    a_val = a_s[:, 0 : 6 * chans].astype(BF16)
    t3_s[...] = jnp.zeros_like(t3_s)

    together = p_s.shape[0]

    def triple_step(step, carry):
        for t in range(together):
            at = step * together + t
            rows = pl.ds(pl.multiple_of(at * chans, chans), chans)
            real_hi, real_lo = split(site_s[0, rows, :], 2)
            imag_hi, imag_lo = split(site_s[1, rows, :], 2)
            right_real = jnp.concatenate(
                [real_hi, real_lo, real_hi, -imag_hi, -imag_lo, -imag_hi], axis=0
            )
            right_imag = jnp.concatenate(
                [imag_hi, imag_lo, imag_hi, real_hi, real_lo, real_hi], axis=0
            )
            p_s[t, 0] = mm(a_val, right_real)
            p_s[t, 1] = mm(a_val, right_imag)
        for i in range(sites):
            here = slice(i * chans, (i + 1) * chans)
            total = [t3_s[0, here, :], t3_s[1, here, :]]
            for t in range(together):
                at = step * together + t
                source = pl.ds(pl.multiple_of(diff_tab[i, at] * chans, chans), chans)
                scale = corr_s[pl.ds(at * sites + i, 1), :]
                for part in range(2):
                    total[part] = total[part] + scale * p_s[t, part, source, :]
            for part in range(2):
                t3_s[part, here, :] = total[part]
        return carry

    lax.fori_loop(0, sites // together, triple_step, 0)

    occupied = corr_s[width + sites : width + sites + 1, :]

    def middle(i, carry):
        rows = pl.ds(pl.multiple_of(i * chans, chans), chans)
        after = pl.ds(pl.multiple_of(width + i * chans, chans), chans)
        pair_row = corr_s[pl.ds(width + i, 1), :]
        on_diag = iota((chans, width), 0) + i * chans == iota((chans, width), 1)
        first = jnp.where(on_diag, occupied, 0.0)
        for part in range(2):
            lead = pair_row * site_s[part, rows, :]
            if part == 0:
                lead = lead - first
            n_s[part, after, :] = lead
            n_s[part, rows, :] = lead + pair_row * site_s[part, after, :] - t3_s[part, rows, :]
        return carry

    lax.fori_loop(0, sites, middle, 0)

    def site_rows(n):
        start = base + n * rows_n
        return (site_s[0, start : start + rows_n, :], site_s[1, start : start + rows_n, :])

    def kernel_of(n):
        rows = slice(n * width, (n + 1) * width)
        return (site_s[0, rows, :], site_s[1, rows, :])

    mid = [(n_s[0, n * width : (n + 1) * width, :], n_s[1, n * width : (n + 1) * width, :]) for n in range(2)]
    lead_rows = [site_rows(n) for n in range(4)]
    minus = -occupied
    q_zero = cadd(cmul(lead_rows[1], mid[0]), cmul(lead_rows[2], mid[1]), cscale(lead_rows[3], minus))
    q_one = cadd(cmul(lead_rows[1], mid[1]), cscale(lead_rows[2], minus))
    q_two = cscale(lead_rows[1], minus)
    result = cadd(
        lead_rows[0],
        cmul(q_zero, kernel_of(0)),
        cmul(q_one, kernel_of(1)),
        cmul(q_two, kernel_of(2)),
    )

    back_val = (back[0], back[1])
    means = []
    for n in range(2):
        moved = cmul(mid[n], back_val, functools.partial(mm_exact, pieces=2))
        lhs_s[0, n * width : (n + 1) * width, :] = moved[0]
        lhs_s[1, n * width : (n + 1) * width, :] = moved[1]

        def gather(i, carry):
            rows = pl.ds(pl.multiple_of(n * width + i * chans, chans), chans)
            phase = (phases[0, pl.ds(i, 1), :], phases[1, pl.ds(i, 1), :])
            real, imag = lhs_s[0, rows, :], lhs_s[1, rows, :]
            return (
                carry[0] + phase[0] * real + phase[1] * imag,
                carry[1] + phase[0] * imag - phase[1] * real,
            )

        zero = jnp.zeros((chans, width), F32)
        means.append(lax.fori_loop(0, sites, gather, (zero, zero)))
    mean_diag = [tuple(block_diag(v, chans) for v in pair_val) for pair_val in means]
    kern_diag = [tuple(block_diag(v, chans) for v in pair_val) for pair_val in kern]
    filled = -jnp.mean(occupied, axis=1, keepdims=True)
    u_zero = cadd(
        cmul(series[0], mean_diag[0]), cmul(series[1], mean_diag[1]), cscale(series[2], filled)
    )
    u_one = cadd(cmul(series[0], mean_diag[1]), cscale(series[1], filled))
    u_two = cscale(series[0], filled)
    change = cadd(
        series[1],
        series[2],
        series[3],
        cmul(u_zero, kern_diag[0]),
        cmul(u_one, kern_diag[1]),
        cmul(u_two, kern_diag[2]),
    )
    for ref, start in ((keep, 0), (send, own_rows)):
        for part in range(2):
            ref[part * own_rows : (part + 1) * own_rows, :] = result[part][start : start + own_rows]
            for n, value in enumerate((change, coarse)):
                at = 2 * own_rows + (2 * n + part) * chans
                ref[at : at + chans, :] = value[part]


def last_kernel(
    own_rows, cfg_at, kept, got, kmap, square_first, square_second, avg, coarse, correction, d_s
):
    own = cfg_at[0] % 2
    chans = (kept.shape[0] - 2 * own_rows) // 4
    width = kept.shape[1]
    flat = coarse.shape[2]
    count_m = coarse.shape[3]
    count_k = kmap.shape[1]
    onehot = kmap[...] == iota((count_m, count_k), 0)
    spread_b = (iota((chans, flat), 0) == iota((chans, flat), 1) % chans).astype(BF16)
    same_b = iota((width, flat), 0) % chans == iota((width, flat), 1) // chans
    pick_m = (iota((width, count_m), 0) // chans == iota((width, count_m), 1)).astype(BF16)
    same_c = iota((flat, width), 0) % chans == iota((flat, width), 1) % chans
    for ref, energy in ((kept, own), (got, 1 - own)):
        moved = []
        for part in range(2):
            avg[energy, part] = ref[part * own_rows : (part + 1) * own_rows, :]
            at = 2 * own_rows + part * chans
            turned = mm_exact(ref[at : at + chans, :].T, spread_b)
            turned = jnp.where(same_b, turned, 0.0).reshape(count_m, chans, flat)
            moved.append(jnp.sum(turned, axis=1))
            at = 2 * own_rows + (2 + part) * chans
            row = ref[at : at + chans, :]
            tall = jnp.broadcast_to(row[:, None, :], (chans, chans, width)).reshape(flat, width)
            coarse[energy, part] = mm_exact(jnp.where(same_c, tall, 0.0), pick_m)
        d_s[energy] = jnp.concatenate(moved, axis=0)
    for energy, square in enumerate((square_first, square_second)):
        both = d_s[energy]
        by_real = mm3(both, square[0])
        by_imag = mm3(both, square[1])
        real = by_real[:count_m] - by_imag[count_m:]
        imag = by_imag[:count_m] + by_real[count_m:]
        correction[energy, 0:1, :] = jnp.sum(jnp.where(onehot, real, 0.0), axis=0, keepdims=True)
        correction[energy, 1:2, :] = jnp.sum(jnp.where(onehot, imag, 0.0), axis=0, keepdims=True)


def shape_of(*extent):
    return jax.ShapeDtypeStruct(extent, F32)


SMEM_SPEC = pl.BlockSpec(memory_space=pltpu.SMEM)
VMEM_SPEC = pl.BlockSpec(memory_space=pltpu.VMEM)


def call(body, outs, scratch, scalars, args, cost):
    return pl.pallas_call(
        body,
        out_shape=outs,
        in_specs=[SMEM_SPEC] * scalars + [VMEM_SPEC] * (len(args) - scalars),
        out_specs=jax.tree.map(lambda _: VMEM_SPEC, outs),
        scratch_shapes=scratch,
        compiler_params=pltpu.CompilerParams(vmem_limit_bytes=KERNEL_VMEM),
        cost_estimate=pl.CostEstimate(flops=cost, bytes_accessed=cost // 64, transcendentals=0),
    )(*args)


def exchange_stages(ka_size, cfg_size):
    total = ka_size * cfg_size
    bits = []
    step = 2
    while step < total:
        bits.append(step)
        step *= 2
    stages = []
    for at in range(0, len(bits), 2):
        group = bits[at : at + 2]
        stages.append(group if len(group) == 1 else [group[0], group[1], group[0] + group[1]])
    return stages


def swap(value, mask, total):
    return lax.ppermute(value, ("ka", "cfg"), [(i, i ^ mask) for i in range(total)])


def step(medium_t, structure, kmap, occupation, cfg_weight, shift_a, shift_b):
    ka_size, cfg_size = lax.axis_size("ka"), lax.axis_size("cfg")
    total = ka_size * cfg_size
    sites = occupation.shape[1]
    chans, count_m = medium_t.shape[2], medium_t.shape[4]
    count_k = kmap.shape[0]
    flat = chans * chans
    width = count_m * chans
    per_moment = count_k * total // count_m
    own_sites = sites // cfg_size
    own_rows = own_sites * chans
    chip_rows = 2 * own_rows
    sum_rows = 2 * chans + sites + PAD_ROWS
    fwd, back, phases, place_diff = phase_constants(sites, chans)

    cfg_at = lax.axis_index("cfg").astype(jnp.int32).reshape(1)
    phases = jnp.asarray(phases)
    kmap_row = kmap.reshape(1, count_k)

    keep, send, *z_y, y_row = call(
        first_kernel,
        (
            shape_of(sum_rows, width),
            shape_of(sum_rows, width),
            *[shape_of(2, flat, count_k)] * (2 * ENERGIES),
            shape_of(ENERGIES, 2, chans, width),
        ),
        [pltpu.VMEM((3, flat, count_k), F32)] * 3 + [pltpu.VMEM((ENERGIES, 2 * chans, width), F32)],
        1,
        (
            cfg_at,
            medium_t.reshape(ENERGIES, 2, flat, count_m),
            structure,
            kmap_row,
            occupation,
            cfg_weight.reshape(1, -1),
        ),
        1 << 24,
    )
    summed = keep + swap(send, 1, total)
    squares = []
    for energy in range(ENERGIES):
        squares.append(
            call(
                square_kernel,
                shape_of(2, flat, count_k),
                [pltpu.VMEM((3, flat, count_k), F32)] * 3,
                0,
                (z_y[ENERGIES + energy], z_y[energy]),
                1 << 24,
            )
        )
    for stage in exchange_stages(ka_size, cfg_size):
        arrived = []
        for mask in stage:
            arrived.append(swap(summed, mask, total))
        for value in arrived:
            summed = summed + value
    out_rows = 2 * own_rows + 4 * chans
    lhs_rows = 3 * width + 4 * chip_rows
    kept, sent = call(
        functools.partial(cluster_kernel, per_moment, own_rows),
        (shape_of(out_rows, width), shape_of(out_rows, width)),
        [
            pltpu.VMEM((2, lhs_rows, width), F32),
            pltpu.VMEM((2, lhs_rows, width), F32),
            pltpu.VMEM((width + sites + PAD_ROWS, width), F32),
            pltpu.VMEM((4, 2, width, width), F32),
            pltpu.VMEM((2, width, width), F32),
            pltpu.VMEM((width, 128), F32),
            pltpu.VMEM((2, 2 * width, width), F32),
        ],
        2,
        (
            cfg_at,
            jnp.asarray(place_diff),
            summed,
            y_row,
            shift_a,
            shift_b,
            jnp.asarray(fwd, BF16),
            jnp.asarray(back, BF16),
            phases,
        ),
        1 << 26,
    )
    got = swap(sent, 1, total)
    avg, coarse, correction = call(
        functools.partial(last_kernel, own_rows),
        (
            shape_of(ENERGIES, 2, own_rows, width),
            shape_of(ENERGIES, 2, flat, count_m),
            shape_of(ENERGIES, 2, count_k),
        ),
        [pltpu.VMEM((ENERGIES, 2 * count_m, flat), F32)],
        1,
        (cfg_at, kept, got, kmap_row, *squares),
        1 << 22,
    )
    return (coarse.reshape(ENERGIES, 2, chans, chans, count_m), avg, correction)


def solution(mesh):
    placed = (
        P(),
        P(None, None, None, None, ("ka", "cfg")),
        P(("ka", "cfg")),
        P(("ka", "cfg"), None),
        P(("ka", "cfg")),
        P(),
        P(),
    )
    return jax.shard_map(
        step,
        mesh=mesh,
        in_specs=placed,
        out_specs=(P(), P(None, None, "cfg", None), P(None, None, ("ka", "cfg"))),
        check_vma=False,
    )
```

profile of v0, /device:TPU:0, one launch (start us, length us, event | category | flops | bytes accessed | tf_op | source)
XLA Modules:
  0.0 42.6 jit_solution(503400332901246172)
XLA Ops:
  1.3 0.6 %copy-done.8 = s32[128]{0:T(128)S(1)} copy-done((s32[128]{0:T(128)S(1)}, s32[128]{0:T(128)}, u32[]{:S(2)}) %copy-start.8) | copy-done | bytes 536
  1.9 0.0 copy-done.9
  2.0 1.0 %copy-done = f32[2,2,16,16,16]{4,3,2,1,0:T(8,128)S(1)} copy-done((f32[2,2,16,16,16]{4,3,2,1,0:T(8,128)S(1)}, f32[2,2,16,16,16]{4,3,2,1,0:T(8,128)}, u32[]{:S(2)}) %copy-start) | copy-done | bytes 65560
  3.0 1.0 %copy-done.1 = f32[2,2,16,16,128]{4,3,2,1,0:T(8,128)S(1)} copy-done((f32[2,2,16,16,128]{4,3,2,1,0:T(8,128)S(1)}, f32[2,2,16,16,128]{4,3,2,1,0:T(8,128)}, u32[]{:S(2)}) %copy-start.1) | copy-done | bytes 524312
  4.0 3.8 %shard_map.130 = (f32[56,256]{1,0:T(8,128)S(1)}, f32[56,256]{1,0:T(8,128)S(1)}, f32[2,256,128]{2,1,0:T(8,128)S(1)}, f32[2,256,128]{2,1,0:T(8,128)S(1)}, f32[2,25...) custom-call(s32[1]{0:T(128)} %bitcast.cfg_at, f32[2,2,256,16]{3,2,1,0:T(8,128)S(1)} %bitcast.6, ...), custom_call_target="tpu_custom_call" | custom-call | flops 16777216 | bytes 262144 | tf_op jit(solution)/shard_map/pallas_call | solution.py:486
  7.8 0.5 %collective-permute-start = (f32[56,256]{1,0:T(8,128)S(1)}, f32[56,256]{1,0:T(8,128)S(1)}, u32[]{:S(2)}, u32[]{:S(2)}) collective-permute-start(f32[56,256]{1,0:T(8,128)S(1)} %get-tuple-element.16), channel_id=1, source_target_pairs={{0,1},{1,0},{2,3},{3,2},{4,5},{5,4},{6,7},{7,6},{8,9},{9,8},{10,11... | collective-permute-start | bytes 172040 | tf_op jit(solution)/shard_map/ppermute | solution.py:512
  8.4 0.9 %collective-permute-done = f32[56,256]{1,0:T(8,128)S(1)} collective-permute-done((f32[56,256]{1,0:T(8,128)S(1)}, f32[56,256]{1,0:T(8,128)S(1)}, u32[]{:S(2)}, u32[]{:S(2)}) %collective-permute-start) | collective-permute-done | bytes 57376 | tf_op jit(solution)/shard_map/ppermute | solution.py:512
  9.3 0.0 copy-start.2
  9.3 0.0 copy-start.3
  9.3 3.9 %collective-permute-start.3 = (f32[56,256]{1,0:T(8,128)S(1)}, f32[56,256]{1,0:T(8,128)S(1)}, u32[]{:S(2)}, u32[]{:S(2)}) collective-permute-start(f32[56,256]{1,0:T(8,128)S(1)} %add.21), channel_id=1, source_target_pairs={{0,6},{1,7},{2,4},{3,5},{4,2},{5,3},{6,0},{7,1},{8,14},{9,15},{10,... | collective-permute-start | bytes 172040 | tf_op jit(solution)/shard_map/ppermute | solution.py:512
  13.2 0.5 %collective-permute-start.2 = (f32[56,256]{1,0:T(8,128)S(1)}, f32[56,256]{1,0:T(8,128)S(1)}, u32[]{:S(2)}, u32[]{:S(2)}) collective-permute-start(f32[56,256]{1,0:T(8,128)S(1)} %add.21), channel_id=1, source_target_pairs={{0,4},{1,5},{2,6},{3,7},{4,0},{5,1},{6,2},{7,3},{8,12},{9,13},{10,... | collective-permute-start | bytes 172040 | tf_op jit(solution)/shard_map/ppermute | solution.py:512
  13.6 0.1 collective-permute-start.1
  13.8 1.6 %collective-permute-done.3 = f32[56,256]{1,0:T(8,128)S(1)} collective-permute-done((f32[56,256]{1,0:T(8,128)S(1)}, f32[56,256]{1,0:T(8,128)S(1)}, u32[]{:S(2)}, u32[]{:S(2)}) %collective-permute-start.3) | collective-permute-done | bytes 57376 | tf_op jit(solution)/shard_map/ppermute | solution.py:512
  15.4 1.9 %collective-permute-done.2 = f32[56,256]{1,0:T(8,128)S(1)} collective-permute-done((f32[56,256]{1,0:T(8,128)S(1)}, f32[56,256]{1,0:T(8,128)S(1)}, u32[]{:S(2)}, u32[]{:S(2)}) %collective-permute-start.2) | collective-permute-done | bytes 57376 | tf_op jit(solution)/shard_map/ppermute | solution.py:512
  17.3 0.5 %collective-permute-done.1 = f32[56,256]{1,0:T(8,128)S(1)} collective-permute-done((f32[56,256]{1,0:T(8,128)S(1)}, f32[56,256]{1,0:T(8,128)S(1)}, u32[]{:S(2)}, u32[]{:S(2)}) %collective-permute-start.1) | collective-permute-done | bytes 57376 | tf_op jit(solution)/shard_map/ppermute | solution.py:512
  17.9 3.7 %collective-permute-start.6 = (f32[56,256]{1,0:T(8,128)S(1)}, f32[56,256]{1,0:T(8,128)S(1)}, u32[]{:S(2)}, u32[]{:S(2)}) collective-permute-start(f32[56,256]{1,0:T(8,128)S(1)} %add_add_fusion.1), channel_id=1, source_target_pairs={{0,24},{1,25},{2,26},{3,27},{4,28},{5,29},{6,30},{7,31},{8,16},{9,... | collective-permute-start | bytes 172040 | tf_op jit(solution)/shard_map/ppermute | solution.py:512
  21.6 0.8 %collective-permute-start.4 = (f32[56,256]{1,0:T(8,128)S(1)}, f32[56,256]{1,0:T(8,128)S(1)}, u32[]{:S(2)}, u32[]{:S(2)}) collective-permute-start(f32[56,256]{1,0:T(8,128)S(1)} %add_add_fusion.1), channel_id=1, source_target_pairs={{0,8},{1,9},{2,10},{3,11},{4,12},{5,13},{6,14},{7,15},{8,0},{9,1},... | collective-permute-start | bytes 172040 | tf_op jit(solution)/shard_map/ppermute | solution.py:512
  22.3 1.7 %collective-permute-done.6 = f32[56,256]{1,0:T(8,128)S(1)} collective-permute-done((f32[56,256]{1,0:T(8,128)S(1)}, f32[56,256]{1,0:T(8,128)S(1)}, u32[]{:S(2)}, u32[]{:S(2)}) %collective-permute-start.6) | collective-permute-done | bytes 57376 | tf_op jit(solution)/shard_map/ppermute | solution.py:512
  24.0 2.6 %collective-permute-done.5 = f32[56,256]{1,0:T(8,128)S(1)} collective-permute-done((f32[56,256]{1,0:T(8,128)S(1)}, f32[56,256]{1,0:T(8,128)S(1)}, u32[]{:S(2)}, u32[]{:S(2)}) %collective-permute-start.5) | collective-permute-done | bytes 57376 | tf_op jit(solution)/shard_map/ppermute | solution.py:512
  26.7 11.5 %shard_map.131 = (f32[192,256]{1,0:T(8,128)S(1)}, f32[192,256]{1,0:T(8,128)S(1)}) custom-call(s32[1]{0:T(128)} %bitcast.cfg_at, s32[16,16]{1,0:T(8,128)S(1)} %copy-done.7, f32[56,256]{1,0:T(8,128)S(1)} %add_add_fusion.summed, f32[2,2,16,256]{3,2,1,0:T(8,128)S(1)} %get-tuple-element.17.y_row, f32[2,2,16,16]{3,2,1,0:T(8,128)S(1)} %copy-done.4, ...), custom_call_target="tpu_custom_call" | custom-call | flops 67108864 | bytes 1048576 | tf_op jit(solution)/shard_map/pallas_call | solution.py:486
  38.2 0.1 collective-permute-start.7
  38.3 1.2 %shard_map.132.square_first = f32[2,256,128]{2,1,0:T(8,128)S(1)} custom-call(f32[2,256,128]{2,1,0:T(8,128)S(1)} %get-tuple-element.20.y_in, f32[2,256,128]{2,1,0:T(8,128)S(1)} %get-tuple-element.21.z_in), custom_call_target="tpu_custom_call" | custom-call | flops 16777216 | bytes 262144 | tf_op jit(solution)/shard_map/pallas_call | solution.py:486
  39.4 1.1 %shard_map.133.square_second = f32[2,256,128]{2,1,0:T(8,128)S(1)} custom-call(f32[2,256,128]{2,1,0:T(8,128)S(1)} %get-tuple-element.22.y_in, f32[2,256,128]{2,1,0:T(8,128)S(1)} %get-tuple-element.23.z_in), custom_call_target="tpu_custom_call" | custom-call | flops 16777216 | bytes 262144 | tf_op jit(solution)/shard_map/pallas_call | solution.py:486
  40.6 2.0 %shard_map.134 = (f32[2,2,64,256]{3,2,1,0:T(8,128)}, f32[2,2,256,16]{3,2,1,0:T(8,128)}, f32[2,2,128]{2,1,0:T(2,128)}) custom-call(s32[1]{0:T(128)} %bitcast.cfg_at, f32[192,256]{1,0:T(8,128)S(1)} %get-tuple-element.18.kept, f32[192,256]{1,0:T(8,128)S(1)} %collective-permute-done.7.got, s32[1,128]{1,0:T(1,128)S(1)} %bitcast.8, ...), custom_call_target="tpu_custom_call" | custom-call | flops 4194304 | bytes 65536 | tf_op jit(solution)/shard_map/pallas_call | solution.py:486
  (20 shorter events, 0.1 us)
Async XLA Ops:
  1.3 0.7 %copy-start.8 = (s32[128]{0:T(128)S(1)}, s32[128]{0:T(128)}, u32[]{:S(2)}) copy-start(s32[128]{0:T(128)} %param.13) | copy-start | bytes 1540
  1.3 0.7 %copy-start.9 = (s32[1,16]{1,0:T(1,128)S(1)}, s32[1,16]{1,0:T(1,128)}, u32[]{:S(2)}) copy-start(s32[1,16]{1,0:T(1,128)} %occupation.1) | copy-start | bytes 196
  2.0 1.0 %copy-start = (f32[2,2,16,16,16]{4,3,2,1,0:T(8,128)S(1)}, f32[2,2,16,16,16]{4,3,2,1,0:T(8,128)}, u32[]{:S(2)}) copy-start(f32[2,2,16,16,16]{4,3,2,1,0:T(8,128)} %param.11) | copy-start | bytes 196612
  3.0 1.0 %copy-start.1 = (f32[2,2,16,16,128]{4,3,2,1,0:T(8,128)S(1)}, f32[2,2,16,16,128]{4,3,2,1,0:T(8,128)}, u32[]{:S(2)}) copy-start(f32[2,2,16,16,128]{4,3,2,1,0:T(8,128)} %structure.1) | copy-start | bytes 1572868
  7.8 1.4 %collective-permute-start = (f32[56,256]{1,0:T(8,128)S(1)}, f32[56,256]{1,0:T(8,128)S(1)}, u32[]{:S(2)}, u32[]{:S(2)}) collective-permute-start(f32[56,256]{1,0:T(8,128)S(1)} %get-tuple-element.16), channel_id=1, source_target_pairs={{0,1},{1,0},{2,3},{3,2},{4,5},{5,4},{6,7},{7,6},{8,9},{9,8},{10,11... | collective-permute-start | bytes 172040 | tf_op jit(solution)/shard_map/ppermute | solution.py:512
  9.3 17.4 %copy-start.5 = (f32[2,2,16,16]{3,2,1,0:T(8,128)S(1)}, f32[2,2,16,16]{3,2,1,0:T(8,128)}, u32[]{:S(2)}) copy-start(f32[2,2,16,16]{3,2,1,0:T(8,128)} %shift_b.1) | copy-start | bytes 12292
  9.3 17.4 %copy-start.6 = (f32[2,16,256]{2,1,0:T(8,128)S(1)}, f32[2,16,256]{2,1,0:T(8,128)}, u32[]{:S(2)}) copy-start(f32[2,16,256]{2,1,0:T(8,128)} %constant.12.clone.phases) | copy-start | bytes 98308
  9.3 17.4 %copy-start.2 = (bf16[2,256,256]{2,1,0:T(8,128)(2,1)S(1)}, bf16[2,256,256]{2,1,0:T(8,128)(2,1)}, u32[]{:S(2)}) copy-start(bf16[2,256,256]{2,1,0:T(8,128)(2,1)} %constant.15.clone.back) | copy-start | bytes 786436
  9.3 17.4 %copy-start.3 = (bf16[2,256,256]{2,1,0:T(8,128)(2,1)S(1)}, bf16[2,256,256]{2,1,0:T(8,128)(2,1)}, u32[]{:S(2)}) copy-start(bf16[2,256,256]{2,1,0:T(8,128)(2,1)} %constant.14.clone.fwd) | copy-start | bytes 786436
  9.3 6.1 %collective-permute-start.3 = (f32[56,256]{1,0:T(8,128)S(1)}, f32[56,256]{1,0:T(8,128)S(1)}, u32[]{:S(2)}, u32[]{:S(2)}) collective-permute-start(f32[56,256]{1,0:T(8,128)S(1)} %add.21), channel_id=1, source_target_pairs={{0,6},{1,7},{2,4},{3,5},{4,2},{5,3},{6,0},{7,1},{8,14},{9,15},{10,... | collective-permute-start | bytes 172040 | tf_op jit(solution)/shard_map/ppermute | solution.py:512
  13.2 4.2 %collective-permute-start.2 = (f32[56,256]{1,0:T(8,128)S(1)}, f32[56,256]{1,0:T(8,128)S(1)}, u32[]{:S(2)}, u32[]{:S(2)}) collective-permute-start(f32[56,256]{1,0:T(8,128)S(1)} %add.21), channel_id=1, source_target_pairs={{0,4},{1,5},{2,6},{3,7},{4,0},{5,1},{6,2},{7,3},{8,12},{9,13},{10,... | collective-permute-start | bytes 172040 | tf_op jit(solution)/shard_map/ppermute | solution.py:512
  13.6 4.2 %collective-permute-start.1 = (f32[56,256]{1,0:T(8,128)S(1)}, f32[56,256]{1,0:T(8,128)S(1)}, u32[]{:S(2)}, u32[]{:S(2)}) collective-permute-start(f32[56,256]{1,0:T(8,128)S(1)} %add.21), channel_id=1, source_target_pairs={{0,2},{1,3},{2,0},{3,1},{4,6},{5,7},{6,4},{7,5},{8,10},{9,11},{10,... | collective-permute-start | bytes 172040 | tf_op jit(solution)/shard_map/ppermute | solution.py:512
  17.8 8.8 %copy-start.4 = (f32[2,2,16,16]{3,2,1,0:T(8,128)S(1)}, f32[2,2,16,16]{3,2,1,0:T(8,128)}, u32[]{:S(2)}) copy-start(f32[2,2,16,16]{3,2,1,0:T(8,128)} %shift_a.1) | copy-start | bytes 12292
  17.9 8.8 %copy-start.7 = (s32[16,16]{1,0:T(8,128)S(1)}, s32[16,16]{1,0:T(8,128)}, u32[]{:S(2)}) copy-start(s32[16,16]{1,0:T(8,128)} %constant.13.clone.diff_tab) | copy-start | bytes 3076
  17.9 6.1 %collective-permute-start.6 = (f32[56,256]{1,0:T(8,128)S(1)}, f32[56,256]{1,0:T(8,128)S(1)}, u32[]{:S(2)}, u32[]{:S(2)}) collective-permute-start(f32[56,256]{1,0:T(8,128)S(1)} %add_add_fusion.1), channel_id=1, source_target_pairs={{0,24},{1,25},{2,26},{3,27},{4,28},{5,29},{6,30},{7,31},{8,16},{9,... | collective-permute-start | bytes 172040 | tf_op jit(solution)/shard_map/ppermute | solution.py:512
  21.5 5.1 %collective-permute-start.5 = (f32[56,256]{1,0:T(8,128)S(1)}, f32[56,256]{1,0:T(8,128)S(1)}, u32[]{:S(2)}, u32[]{:S(2)}) collective-permute-start(f32[56,256]{1,0:T(8,128)S(1)} %add_add_fusion.1), channel_id=1, source_target_pairs={{0,16},{1,17},{2,18},{3,19},{4,20},{5,21},{6,22},{7,23},{8,24},{9,... | collective-permute-start | bytes 172040 | tf_op jit(solution)/shard_map/ppermute | solution.py:512
  21.6 5.1 %collective-permute-start.4 = (f32[56,256]{1,0:T(8,128)S(1)}, f32[56,256]{1,0:T(8,128)S(1)}, u32[]{:S(2)}, u32[]{:S(2)}) collective-permute-start(f32[56,256]{1,0:T(8,128)S(1)} %add_add_fusion.1), channel_id=1, source_target_pairs={{0,8},{1,9},{2,10},{3,11},{4,12},{5,13},{6,14},{7,15},{8,0},{9,1},... | collective-permute-start | bytes 172040 | tf_op jit(solution)/shard_map/ppermute | solution.py:512
  38.2 2.4 %collective-permute-start.7 = (f32[192,256]{1,0:T(8,128)S(1)}, f32[192,256]{1,0:T(8,128)S(1)}, u32[]{:S(2)}, u32[]{:S(2)}) collective-permute-start(f32[192,256]{1,0:T(8,128)S(1)} %get-tuple-element.19), channel_id=1, source_target_pairs={{0,1},{1,0},{2,3},{3,2},{4,5},{5,4},{6,7},{7,6},{8,9},{9,8},{10,11... | collective-permute-start | bytes 589832 | tf_op jit(solution)/shard_map/ppermute | solution.py:512
where the time goes:
time: 42.9 us; the launch traced here: 42.6 us
  Pallas kernels  19.6 us (46%)
  starting transfers between devices  9.56 us (22%)
  waiting for transfers between devices  9.23 us (22%)
  local copies, waits for them, and re-layouts  2.77 us (6%)
  between operations  1.41 us (3%)
    pallas_call x5, Pallas kernels, call(): pl.pallas_call(body, out_shape=outs, in_specs=[SMEM_SPEC] * scalars + [VM...  19.6 us
    ppermute x8, starting transfers between devices, swap(): lax.ppermute(value, ('ka', 'cfg'), [(i, i ^ mask) for i in range(total)])  9.56 us
    ppermute x8, waiting for transfers between devices, swap(): lax.ppermute(value, ('ka', 'cfg'), [(i, i ^ mask) for i in range(total)])  9.23 us
    unnamed x20, local copies, waits for them, and re-layouts  2.77 us
  transfers between devices with their start and end apart: 8, of which 6 were waited for; matrix products, arithmetic and copies ran while one was open for 0% of the time, Pallas kernels for 5%

commit v1 on v0

--- a/solution.py
+++ b/solution.py
@@ -239,9 +239,9 @@
 
 
 def cluster_kernel(
-    per_moment, own_rows,
-    cfg_at, diff_tab, summed, y_row, shift_a, shift_b, fwd, back, phases,
-    keep, send, lhs_s, site_s, corr_s, p_s, t3_s, a_s, n_s,
+    per_moment, own_rows, place_diff,
+    cfg_at, summed, y_row, shift_a, shift_b, fwd, back, phases,
+    keep, send, lhs_s, site_s, corr_s, p_s, a_s, n_s,
 ):
     own = cfg_at[0] % 2
     chans = shift_a.shape[2]
@@ -261,17 +261,31 @@
     base_t = (shift_b[own, 0], shift_b[own, 1])
     step_t = (shift_a[own, 0] - base_t[0], shift_a[own, 1] - base_t[1])
 
-    def left_small(small, value):
-        stack = jnp.concatenate(small, axis=0)
-        by_real = mm_high(stack, value[0])
-        by_imag = mm_high(stack, value[1])
-        return (by_real[cols[0]] - by_imag[cols[1]], by_imag[cols[0]] + by_real[cols[1]])
-
-    b_diag = tuple(block_diag(v, chans) for v in left_small(base_t, coarse))
-    series = [coarse]
-    for _ in range(3):
-        series.append(cscale(cmul(series[-1], b_diag), -1.0))
-    kern = [left_small(step_t, series[n]) for n in range(3)]
+    stack = jnp.concatenate(base_t + step_t, axis=0)
+    by_real = mm_high(stack, coarse[0])
+    by_imag = mm_high(stack, coarse[1])
+
+    def small_part(at):
+        here, after = slice(at * chans, (at + 1) * chans), slice((at + 1) * chans, (at + 2) * chans)
+        return (by_real[here] - by_imag[after], by_imag[here] + by_real[after])
+
+    def rows_by(rows, diag):
+        count = len(rows)
+        out = cmul(
+            tuple(jnp.concatenate([row[part] for row in rows], axis=0) for part in range(2)), diag
+        )
+        return [
+            tuple(out[part][n * chans : (n + 1) * chans] for part in range(2)) for n in range(count)
+        ]
+
+    power, lead_kern = small_part(0), small_part(2)
+    power_diag = tuple(block_diag(v, chans) for v in power)
+    first, first_kern, power = rows_by([coarse, lead_kern, power], power_diag)
+    first, first_kern = cscale(first, -1.0), cscale(first_kern, -1.0)
+    power_diag = tuple(block_diag(v, chans) for v in power)
+    second, third, second_kern = rows_by([coarse, first, lead_kern], power_diag)
+    series = [coarse, first, second, third]
+    kern = [lead_kern, first_kern, second_kern]
     whole = cadd(*series)
 
     for i in range(sites):
@@ -323,56 +337,38 @@
     for n, piece in enumerate(hi_lo):
         a_s[:, n * chans : (n + 1) * chans] = piece
     a_val = a_s[:, 0 : 6 * chans].astype(BF16)
-    t3_s[...] = jnp.zeros_like(t3_s)
-
-    together = p_s.shape[0]
-
-    def triple_step(step, carry):
-        for t in range(together):
-            at = step * together + t
-            rows = pl.ds(pl.multiple_of(at * chans, chans), chans)
-            real_hi, real_lo = split(site_s[0, rows, :], 2)
-            imag_hi, imag_lo = split(site_s[1, rows, :], 2)
-            right_real = jnp.concatenate(
-                [real_hi, real_lo, real_hi, -imag_hi, -imag_lo, -imag_hi], axis=0
-            )
-            right_imag = jnp.concatenate(
-                [imag_hi, imag_lo, imag_hi, real_hi, real_lo, real_hi], axis=0
-            )
-            p_s[t, 0] = mm(a_val, right_real)
-            p_s[t, 1] = mm(a_val, right_imag)
-        for i in range(sites):
-            here = slice(i * chans, (i + 1) * chans)
-            total = [t3_s[0, here, :], t3_s[1, here, :]]
-            for t in range(together):
-                at = step * together + t
-                source = pl.ds(pl.multiple_of(diff_tab[i, at] * chans, chans), chans)
-                scale = corr_s[pl.ds(at * sites + i, 1), :]
-                for part in range(2):
-                    total[part] = total[part] + scale * p_s[t, part, source, :]
-            for part in range(2):
-                t3_s[part, here, :] = total[part]
-        return carry
-
-    lax.fori_loop(0, sites // together, triple_step, 0)
+    for at in range(sites):
+        rows = slice(at * chans, (at + 1) * chans)
+        real_hi, real_lo = split(site_s[0, rows, :], 2)
+        imag_hi, imag_lo = split(site_s[1, rows, :], 2)
+        right_real = jnp.concatenate(
+            [real_hi, real_lo, real_hi, -imag_hi, -imag_lo, -imag_hi], axis=0
+        )
+        right_imag = jnp.concatenate(
+            [imag_hi, imag_lo, imag_hi, real_hi, real_lo, real_hi], axis=0
+        )
+        p_s[at, 0] = mm(a_val, right_real)
+        p_s[at, 1] = mm(a_val, right_imag)
 
     occupied = corr_s[width + sites : width + sites + 1, :]
 
-    def middle(i, carry):
-        rows = pl.ds(pl.multiple_of(i * chans, chans), chans)
-        after = pl.ds(pl.multiple_of(width + i * chans, chans), chans)
-        pair_row = corr_s[pl.ds(width + i, 1), :]
+    for i in range(sites):
+        rows = slice(i * chans, (i + 1) * chans)
+        after = slice(width + i * chans, width + (i + 1) * chans)
+        pair_row = corr_s[width + i : width + i + 1, :]
         on_diag = iota((chans, width), 0) + i * chans == iota((chans, width), 1)
-        first = jnp.where(on_diag, occupied, 0.0)
         for part in range(2):
+            total = None
+            for at in range(sites):
+                gap = int(place_diff[i, at])
+                scale = corr_s[at * sites + i : at * sites + i + 1, :]
+                term = scale * p_s[at, part, gap * chans : (gap + 1) * chans, :]
+                total = term if total is None else total + term
             lead = pair_row * site_s[part, rows, :]
             if part == 0:
-                lead = lead - first
+                lead = lead - jnp.where(on_diag, occupied, 0.0)
             n_s[part, after, :] = lead
-            n_s[part, rows, :] = lead + pair_row * site_s[part, after, :] - t3_s[part, rows, :]
-        return carry
-
-    lax.fori_loop(0, sites, middle, 0)
+            n_s[part, rows, :] = lead + pair_row * site_s[part, after, :] - total
 
     def site_rows(n):
         start = base + n * rows_n
@@ -399,20 +395,14 @@
     means = []
     for n in range(2):
         moved = cmul(mid[n], back_val, functools.partial(mm_exact, pieces=2))
-        lhs_s[0, n * width : (n + 1) * width, :] = moved[0]
-        lhs_s[1, n * width : (n + 1) * width, :] = moved[1]
-
-        def gather(i, carry):
-            rows = pl.ds(pl.multiple_of(n * width + i * chans, chans), chans)
-            phase = (phases[0, pl.ds(i, 1), :], phases[1, pl.ds(i, 1), :])
-            real, imag = lhs_s[0, rows, :], lhs_s[1, rows, :]
-            return (
-                carry[0] + phase[0] * real + phase[1] * imag,
-                carry[1] + phase[0] * imag - phase[1] * real,
-            )
-
-        zero = jnp.zeros((chans, width), F32)
-        means.append(lax.fori_loop(0, sites, gather, (zero, zero)))
+        total = None
+        for i in range(sites):
+            rows = slice(i * chans, (i + 1) * chans)
+            phase = (phases[0, i : i + 1, :], phases[1, i : i + 1, :])
+            real, imag = moved[0][rows], moved[1][rows]
+            term = (phase[0] * real + phase[1] * imag, phase[0] * imag - phase[1] * real)
+            total = term if total is None else cadd(total, term)
+        means.append(total)
     mean_diag = [tuple(block_diag(v, chans) for v in pair_val) for pair_val in means]
     kern_diag = [tuple(block_diag(v, chans) for v in pair_val) for pair_val in kern]
     filled = -jnp.mean(occupied, axis=1, keepdims=True)
@@ -573,21 +563,19 @@
     out_rows = 2 * own_rows + 4 * chans
     lhs_rows = 3 * width + 4 * chip_rows
     kept, sent = call(
-        functools.partial(cluster_kernel, per_moment, own_rows),
+        functools.partial(cluster_kernel, per_moment, own_rows, place_diff),
         (shape_of(out_rows, width), shape_of(out_rows, width)),
         [
             pltpu.VMEM((2, lhs_rows, width), F32),
             pltpu.VMEM((2, lhs_rows, width), F32),
             pltpu.VMEM((width + sites + PAD_ROWS, width), F32),
-            pltpu.VMEM((4, 2, width, width), F32),
-            pltpu.VMEM((2, width, width), F32),
+            pltpu.VMEM((sites, 2, width, width), F32),
             pltpu.VMEM((width, 128), F32),
             pltpu.VMEM((2, 2 * width, width), F32),
         ],
-        2,
+        1,
         (
             cfg_at,
-            jnp.asarray(place_diff),
             summed,
             y_row,
             shift_a,

time: 42.9 us -> 38.1 us (0.89)
  Pallas kernels: 19.6 us -> 15 us
    pallas_call x5, Pallas kernels: 19.6 us -> 15 us  [call(): pl.pallas_call(body, out_shape=outs, in_specs=[SMEM_SPEC] * scalars + [VM...]
    unnamed x20 -> x18, local copies, waits for them, and re-layouts: 2.77 us -> 2.77 us
  transfers between devices with their start and end apart: 8 -> 8, of which waited for: 6 -> 6; matrix products, arithmetic and copies ran while one was open for 0% -> 0% of each run, Pallas kernels for 5% -> 6%
where the time goes in v1:
time: 38.1 us; the launch traced here: 37.9 us
  Pallas kernels  15 us (39%)
  starting transfers between devices  9.53 us (25%)
  waiting for transfers between devices  9.22 us (24%)
  local copies, waits for them, and re-layouts  2.77 us (7%)
  between operations  1.4 us (4%)
    pallas_call x5, Pallas kernels, call(): pl.pallas_call(body, out_shape=outs, in_specs=[SMEM_SPEC] * scalars + [VM...  15 us
    ppermute x8, starting transfers between devices, swap(): lax.ppermute(value, ('ka', 'cfg'), [(i, i ^ mask) for i in range(total)])  9.53 us
    ppermute x8, waiting for transfers between devices, swap(): lax.ppermute(value, ('ka', 'cfg'), [(i, i ^ mask) for i in range(total)])  9.22 us
    unnamed x18, local copies, waits for them, and re-layouts  2.77 us
  transfers between devices with their start and end apart: 8, of which 6 were waited for; matrix products, arithmetic and copies ran while one was open for 0% of the time, Pallas kernels for 6%

profile of v1, /device:TPU:0, one launch (start us, length us, event | category | flops | bytes accessed | tf_op | source)
XLA Modules:
  0.0 37.9 jit_solution(18314728394214591421)
XLA Ops:
  1.3 0.6 %copy-done.7 = s32[128]{0:T(128)S(1)} copy-done((s32[128]{0:T(128)S(1)}, s32[128]{0:T(128)}, u32[]{:S(2)}) %copy-start.7) | copy-done | bytes 536
  1.9 0.0 copy-done.8
  2.0 1.0 %copy-done = f32[2,2,16,16,16]{4,3,2,1,0:T(8,128)S(1)} copy-done((f32[2,2,16,16,16]{4,3,2,1,0:T(8,128)S(1)}, f32[2,2,16,16,16]{4,3,2,1,0:T(8,128)}, u32[]{:S(2)}) %copy-start) | copy-done | bytes 65560
  3.0 1.0 %copy-done.1 = f32[2,2,16,16,128]{4,3,2,1,0:T(8,128)S(1)} copy-done((f32[2,2,16,16,128]{4,3,2,1,0:T(8,128)S(1)}, f32[2,2,16,16,128]{4,3,2,1,0:T(8,128)}, u32[]{:S(2)}) %copy-start.1) | copy-done | bytes 524312
  4.0 3.8 %shard_map.121 = (f32[56,256]{1,0:T(8,128)S(1)}, f32[56,256]{1,0:T(8,128)S(1)}, f32[2,256,128]{2,1,0:T(8,128)S(1)}, f32[2,256,128]{2,1,0:T(8,128)S(1)}, f32[2,25...) custom-call(s32[1]{0:T(128)} %bitcast.cfg_at, f32[2,2,256,16]{3,2,1,0:T(8,128)S(1)} %bitcast.6, ...), custom_call_target="tpu_custom_call" | custom-call | flops 16777216 | bytes 262144 | tf_op jit(solution)/shard_map/pallas_call | solution.py:476
  7.8 0.6 %collective-permute-start = (f32[56,256]{1,0:T(8,128)S(1)}, f32[56,256]{1,0:T(8,128)S(1)}, u32[]{:S(2)}, u32[]{:S(2)}) collective-permute-start(f32[56,256]{1,0:T(8,128)S(1)} %get-tuple-element.16), channel_id=1, source_target_pairs={{0,1},{1,0},{2,3},{3,2},{4,5},{5,4},{6,7},{7,6},{8,9},{9,8},{10,11... | collective-permute-start | bytes 172040 | tf_op jit(solution)/shard_map/ppermute | solution.py:502
  8.4 0.9 %collective-permute-done = f32[56,256]{1,0:T(8,128)S(1)} collective-permute-done((f32[56,256]{1,0:T(8,128)S(1)}, f32[56,256]{1,0:T(8,128)S(1)}, u32[]{:S(2)}, u32[]{:S(2)}) %collective-permute-start) | collective-permute-done | bytes 57376 | tf_op jit(solution)/shard_map/ppermute | solution.py:502
  9.3 0.0 copy-start.2
  9.3 0.0 copy-start.3
  9.3 3.8 %collective-permute-start.3 = (f32[56,256]{1,0:T(8,128)S(1)}, f32[56,256]{1,0:T(8,128)S(1)}, u32[]{:S(2)}, u32[]{:S(2)}) collective-permute-start(f32[56,256]{1,0:T(8,128)S(1)} %add.21), channel_id=1, source_target_pairs={{0,6},{1,7},{2,4},{3,5},{4,2},{5,3},{6,0},{7,1},{8,14},{9,15},{10,... | collective-permute-start | bytes 172040 | tf_op jit(solution)/shard_map/ppermute | solution.py:502
  13.2 0.5 %collective-permute-start.2 = (f32[56,256]{1,0:T(8,128)S(1)}, f32[56,256]{1,0:T(8,128)S(1)}, u32[]{:S(2)}, u32[]{:S(2)}) collective-permute-start(f32[56,256]{1,0:T(8,128)S(1)} %add.21), channel_id=1, source_target_pairs={{0,4},{1,5},{2,6},{3,7},{4,0},{5,1},{6,2},{7,3},{8,12},{9,13},{10,... | collective-permute-start | bytes 172040 | tf_op jit(solution)/shard_map/ppermute | solution.py:502
  13.7 0.1 collective-permute-start.1
  13.8 1.6 %collective-permute-done.3 = f32[56,256]{1,0:T(8,128)S(1)} collective-permute-done((f32[56,256]{1,0:T(8,128)S(1)}, f32[56,256]{1,0:T(8,128)S(1)}, u32[]{:S(2)}, u32[]{:S(2)}) %collective-permute-start.3) | collective-permute-done | bytes 57376 | tf_op jit(solution)/shard_map/ppermute | solution.py:502
  15.4 1.9 %collective-permute-done.2 = f32[56,256]{1,0:T(8,128)S(1)} collective-permute-done((f32[56,256]{1,0:T(8,128)S(1)}, f32[56,256]{1,0:T(8,128)S(1)}, u32[]{:S(2)}, u32[]{:S(2)}) %collective-permute-start.2) | collective-permute-done | bytes 57376 | tf_op jit(solution)/shard_map/ppermute | solution.py:502
  17.3 0.5 %collective-permute-done.1 = f32[56,256]{1,0:T(8,128)S(1)} collective-permute-done((f32[56,256]{1,0:T(8,128)S(1)}, f32[56,256]{1,0:T(8,128)S(1)}, u32[]{:S(2)}, u32[]{:S(2)}) %collective-permute-start.1) | collective-permute-done | bytes 57376 | tf_op jit(solution)/shard_map/ppermute | solution.py:502
  17.9 3.7 %collective-permute-start.6 = (f32[56,256]{1,0:T(8,128)S(1)}, f32[56,256]{1,0:T(8,128)S(1)}, u32[]{:S(2)}, u32[]{:S(2)}) collective-permute-start(f32[56,256]{1,0:T(8,128)S(1)} %add_add_fusion.1), channel_id=1, source_target_pairs={{0,24},{1,25},{2,26},{3,27},{4,28},{5,29},{6,30},{7,31},{8,16},{9,... | collective-permute-start | bytes 172040 | tf_op jit(solution)/shard_map/ppermute | solution.py:502
  21.5 0.8 %collective-permute-start.4 = (f32[56,256]{1,0:T(8,128)S(1)}, f32[56,256]{1,0:T(8,128)S(1)}, u32[]{:S(2)}, u32[]{:S(2)}) collective-permute-start(f32[56,256]{1,0:T(8,128)S(1)} %add_add_fusion.1), channel_id=1, source_target_pairs={{0,8},{1,9},{2,10},{3,11},{4,12},{5,13},{6,14},{7,15},{8,0},{9,1},... | collective-permute-start | bytes 172040 | tf_op jit(solution)/shard_map/ppermute | solution.py:502
  22.3 1.7 %collective-permute-done.6 = f32[56,256]{1,0:T(8,128)S(1)} collective-permute-done((f32[56,256]{1,0:T(8,128)S(1)}, f32[56,256]{1,0:T(8,128)S(1)}, u32[]{:S(2)}, u32[]{:S(2)}) %collective-permute-start.6) | collective-permute-done | bytes 57376 | tf_op jit(solution)/shard_map/ppermute | solution.py:502
  24.0 2.6 %collective-permute-done.5 = f32[56,256]{1,0:T(8,128)S(1)} collective-permute-done((f32[56,256]{1,0:T(8,128)S(1)}, f32[56,256]{1,0:T(8,128)S(1)}, u32[]{:S(2)}, u32[]{:S(2)}) %collective-permute-start.5) | collective-permute-done | bytes 57376 | tf_op jit(solution)/shard_map/ppermute | solution.py:502
  26.7 6.8 %shard_map.122 = (f32[192,256]{1,0:T(8,128)S(1)}, f32[192,256]{1,0:T(8,128)S(1)}) custom-call(s32[1]{0:T(128)} %bitcast.cfg_at, f32[56,256]{1,0:T(8,128)S(1)} %add_add_fusion.summed, f32[2,2,16,256]{3,2,1,0:T(8,128)S(1)} %get-tuple-element.17.y_row, f32[2,2,16,16]{3,2,1,0:T(8,128)S(1)} %copy-done.4, f32[2,2,16,16]{3,2,1,0:T(8,128)S(1)} %copy-done.5, ...), custom_call_target="tpu_custom_call" | custom-call | flops 67108864 | bytes 1048576 | tf_op jit(solution)/shard_map/pallas_call | solution.py:476
  33.5 0.0 collective-permute-start.7
  33.6 1.2 %shard_map.123.square_first = f32[2,256,128]{2,1,0:T(8,128)S(1)} custom-call(f32[2,256,128]{2,1,0:T(8,128)S(1)} %get-tuple-element.20.y_in, f32[2,256,128]{2,1,0:T(8,128)S(1)} %get-tuple-element.21.z_in), custom_call_target="tpu_custom_call" | custom-call | flops 16777216 | bytes 262144 | tf_op jit(solution)/shard_map/pallas_call | solution.py:476
  34.7 1.1 %shard_map.124.square_second = f32[2,256,128]{2,1,0:T(8,128)S(1)} custom-call(f32[2,256,128]{2,1,0:T(8,128)S(1)} %get-tuple-element.22.y_in, f32[2,256,128]{2,1,0:T(8,128)S(1)} %get-tuple-element.23.z_in), custom_call_target="tpu_custom_call" | custom-call | flops 16777216 | bytes 262144 | tf_op jit(solution)/shard_map/pallas_call | solution.py:476
  35.9 2.0 %shard_map.125 = (f32[2,2,64,256]{3,2,1,0:T(8,128)}, f32[2,2,256,16]{3,2,1,0:T(8,128)}, f32[2,2,128]{2,1,0:T(2,128)}) custom-call(s32[1]{0:T(128)} %bitcast.cfg_at, f32[192,256]{1,0:T(8,128)S(1)} %get-tuple-element.18.kept, f32[192,256]{1,0:T(8,128)S(1)} %collective-permute-done.7.got, s32[1,128]{1,0:T(1,128)S(1)} %bitcast.8, ...), custom_call_target="tpu_custom_call" | custom-call | flops 4194304 | bytes 65536 | tf_op jit(solution)/shard_map/pallas_call | solution.py:476
  (18 shorter events, 0.1 us)
Async XLA Ops:
  1.3 0.7 %copy-start.7 = (s32[128]{0:T(128)S(1)}, s32[128]{0:T(128)}, u32[]{:S(2)}) copy-start(s32[128]{0:T(128)} %param.12) | copy-start | bytes 1540
  1.3 0.7 %copy-start.8 = (s32[1,16]{1,0:T(1,128)S(1)}, s32[1,16]{1,0:T(1,128)}, u32[]{:S(2)}) copy-start(s32[1,16]{1,0:T(1,128)} %occupation.1) | copy-start | bytes 196
  2.0 1.0 %copy-start = (f32[2,2,16,16,16]{4,3,2,1,0:T(8,128)S(1)}, f32[2,2,16,16,16]{4,3,2,1,0:T(8,128)}, u32[]{:S(2)}) copy-start(f32[2,2,16,16,16]{4,3,2,1,0:T(8,128)} %param.10) | copy-start | bytes 196612
  3.0 1.0 %copy-start.1 = (f32[2,2,16,16,128]{4,3,2,1,0:T(8,128)S(1)}, f32[2,2,16,16,128]{4,3,2,1,0:T(8,128)}, u32[]{:S(2)}) copy-start(f32[2,2,16,16,128]{4,3,2,1,0:T(8,128)} %structure.1) | copy-start | bytes 1572868
  7.8 1.4 %collective-permute-start = (f32[56,256]{1,0:T(8,128)S(1)}, f32[56,256]{1,0:T(8,128)S(1)}, u32[]{:S(2)}, u32[]{:S(2)}) collective-permute-start(f32[56,256]{1,0:T(8,128)S(1)} %get-tuple-element.16), channel_id=1, source_target_pairs={{0,1},{1,0},{2,3},{3,2},{4,5},{5,4},{6,7},{7,6},{8,9},{9,8},{10,11... | collective-permute-start | bytes 172040 | tf_op jit(solution)/shard_map/ppermute | solution.py:502
  9.3 17.4 %copy-start.5 = (f32[2,2,16,16]{3,2,1,0:T(8,128)S(1)}, f32[2,2,16,16]{3,2,1,0:T(8,128)}, u32[]{:S(2)}) copy-start(f32[2,2,16,16]{3,2,1,0:T(8,128)} %shift_b.1) | copy-start | bytes 12292
  9.3 17.4 %copy-start.6 = (f32[2,16,256]{2,1,0:T(8,128)S(1)}, f32[2,16,256]{2,1,0:T(8,128)}, u32[]{:S(2)}) copy-start(f32[2,16,256]{2,1,0:T(8,128)} %constant.10.clone.phases) | copy-start | bytes 98308
  9.3 17.4 %copy-start.2 = (bf16[2,256,256]{2,1,0:T(8,128)(2,1)S(1)}, bf16[2,256,256]{2,1,0:T(8,128)(2,1)}, u32[]{:S(2)}) copy-start(bf16[2,256,256]{2,1,0:T(8,128)(2,1)} %constant.12.clone.back) | copy-start | bytes 786436
  9.3 17.4 %copy-start.3 = (bf16[2,256,256]{2,1,0:T(8,128)(2,1)S(1)}, bf16[2,256,256]{2,1,0:T(8,128)(2,1)}, u32[]{:S(2)}) copy-start(bf16[2,256,256]{2,1,0:T(8,128)(2,1)} %constant.11.clone.fwd) | copy-start | bytes 786436
  9.3 6.1 %collective-permute-start.3 = (f32[56,256]{1,0:T(8,128)S(1)}, f32[56,256]{1,0:T(8,128)S(1)}, u32[]{:S(2)}, u32[]{:S(2)}) collective-permute-start(f32[56,256]{1,0:T(8,128)S(1)} %add.21), channel_id=1, source_target_pairs={{0,6},{1,7},{2,4},{3,5},{4,2},{5,3},{6,0},{7,1},{8,14},{9,15},{10,... | collective-permute-start | bytes 172040 | tf_op jit(solution)/shard_map/ppermute | solution.py:502
  13.2 4.2 %collective-permute-start.2 = (f32[56,256]{1,0:T(8,128)S(1)}, f32[56,256]{1,0:T(8,128)S(1)}, u32[]{:S(2)}, u32[]{:S(2)}) collective-permute-start(f32[56,256]{1,0:T(8,128)S(1)} %add.21), channel_id=1, source_target_pairs={{0,4},{1,5},{2,6},{3,7},{4,0},{5,1},{6,2},{7,3},{8,12},{9,13},{10,... | collective-permute-start | bytes 172040 | tf_op jit(solution)/shard_map/ppermute | solution.py:502
  13.7 4.2 %collective-permute-start.1 = (f32[56,256]{1,0:T(8,128)S(1)}, f32[56,256]{1,0:T(8,128)S(1)}, u32[]{:S(2)}, u32[]{:S(2)}) collective-permute-start(f32[56,256]{1,0:T(8,128)S(1)} %add.21), channel_id=1, source_target_pairs={{0,2},{1,3},{2,0},{3,1},{4,6},{5,7},{6,4},{7,5},{8,10},{9,11},{10,... | collective-permute-start | bytes 172040 | tf_op jit(solution)/shard_map/ppermute | solution.py:502
  17.8 8.8 %copy-start.4 = (f32[2,2,16,16]{3,2,1,0:T(8,128)S(1)}, f32[2,2,16,16]{3,2,1,0:T(8,128)}, u32[]{:S(2)}) copy-start(f32[2,2,16,16]{3,2,1,0:T(8,128)} %shift_a.1) | copy-start | bytes 12292
  17.9 6.1 %collective-permute-start.6 = (f32[56,256]{1,0:T(8,128)S(1)}, f32[56,256]{1,0:T(8,128)S(1)}, u32[]{:S(2)}, u32[]{:S(2)}) collective-permute-start(f32[56,256]{1,0:T(8,128)S(1)} %add_add_fusion.1), channel_id=1, source_target_pairs={{0,24},{1,25},{2,26},{3,27},{4,28},{5,29},{6,30},{7,31},{8,16},{9,... | collective-permute-start | bytes 172040 | tf_op jit(solution)/shard_map/ppermute | solution.py:502
  21.5 5.1 %collective-permute-start.5 = (f32[56,256]{1,0:T(8,128)S(1)}, f32[56,256]{1,0:T(8,128)S(1)}, u32[]{:S(2)}, u32[]{:S(2)}) collective-permute-start(f32[56,256]{1,0:T(8,128)S(1)} %add_add_fusion.1), channel_id=1, source_target_pairs={{0,16},{1,17},{2,18},{3,19},{4,20},{5,21},{6,22},{7,23},{8,24},{9,... | collective-permute-start | bytes 172040 | tf_op jit(solution)/shard_map/ppermute | solution.py:502
  21.5 5.1 %collective-permute-start.4 = (f32[56,256]{1,0:T(8,128)S(1)}, f32[56,256]{1,0:T(8,128)S(1)}, u32[]{:S(2)}, u32[]{:S(2)}) collective-permute-start(f32[56,256]{1,0:T(8,128)S(1)} %add_add_fusion.1), channel_id=1, source_target_pairs={{0,8},{1,9},{2,10},{3,11},{4,12},{5,13},{6,14},{7,15},{8,0},{9,1},... | collective-permute-start | bytes 172040 | tf_op jit(solution)/shard_map/ppermute | solution.py:502
  33.5 2.3 %collective-permute-start.7 = (f32[192,256]{1,0:T(8,128)S(1)}, f32[192,256]{1,0:T(8,128)S(1)}, u32[]{:S(2)}, u32[]{:S(2)}) collective-permute-start(f32[192,256]{1,0:T(8,128)S(1)} %get-tuple-element.19), channel_id=1, source_target_pairs={{0,1},{1,0},{2,3},{3,2},{4,5},{5,4},{6,7},{7,6},{8,9},{9,8},{10,11... | collective-permute-start | bytes 589832 | tf_op jit(solution)/shard_map/ppermute | solution.py:502

commit v2 on v1

--- a/solution.py
+++ b/solution.py
@@ -13,6 +13,7 @@
 F32 = jnp.float32
 BF16 = jnp.bfloat16
 PAD_ROWS = 8
+SLOT = 32
 KERNEL_VMEM = 20 << 20
 
 
@@ -143,76 +144,98 @@
     ref[2, rows, :] = real + imag
 
 
-def first_kernel(
-    cfg_at, medium, structure, kmap, occupation, weight,
-    keep, send, z_first, z_second, y_first, y_second, y_row, y_s, g_s, f_s, part_s,
-):
-    chans = structure.shape[2]
-    count_k = structure.shape[4]
-    count_m = medium.shape[3]
-    width = count_m * chans
-    flat = chans * chans
-    momenta = kmap[...]
-    onehot = (momenta == iota((count_m, count_k), 0)).astype(BF16)
-    wide = (momenta == iota((width, count_k), 0) // chans).astype(BF16)
+def kpoint_energy(medium, kmap, packed, z_out, y_out, y_s, g_s, f_s):
+    flat, count_m = medium[0].shape
+    count_k = kmap.shape[1]
+    chans = math.isqrt(flat)
+    width = packed.shape[1]
+    onehot = (kmap == iota((count_m, count_k), 0)).astype(BF16)
+    wide = (kmap == iota((width, count_k), 0) // chans).astype(BF16)
     same = iota((flat, width), 0) % chans == iota((flat, width), 1) % chans
-    lanes_of = (iota((count_m, width), 0) == iota((count_m, width), 1) // chans).astype(BF16)
 
     def fold(value):
         return jnp.sum(jnp.where(same, value, 0.0).reshape(chans, chans, width), axis=1)
 
-    for energy, (z_out, y_out) in enumerate(((z_first, y_first), (z_second, y_second))):
-        for part in range(2):
-            med = medium[energy, part]
-            y_row[energy, part] = fold(mm_exact(med, lanes_of))
-            value = mm_exact(med, onehot)
-            y_s[part] = value
-            y_out[part] = value
-            g_s[part] = structure[energy, part].reshape(flat, count_k)
-        y_s[2] = y_s[0] + y_s[1]
-        g_s[2] = g_s[0] + g_s[1]
-
-        def write_f(base, real, imag):
-            put3(f_s, base, chans, real, imag)
-
-        batch_mul(y_s, g_s, write_f, chans)
-
-        def write_z(base, real, imag, z_out=z_out):
-            rows = pl.ds(pl.multiple_of(base, chans), chans)
-            z_out[0, rows, :] = real + f_s[0, rows, :]
-            z_out[1, rows, :] = imag + f_s[1, rows, :]
-
-        batch_mul(f_s, f_s, write_z, chans)
-        for part in range(2):
-            parts = split(z_out[part], 3)
-            total = mm_nt(parts[2], wide) + mm_nt(parts[1], wide) + mm_nt(parts[0], wide)
-            part_s[energy, part * chans : (part + 1) * chans, :] = fold(total)
-
-    sites = occupation.shape[1]
-    pairs = sites * sites
-    from_l = (iota((sites, pairs), 0) == iota((sites, pairs), 1) // sites).astype(BF16)
-    from_j = (iota((sites, pairs), 0) == iota((sites, pairs), 1) % sites).astype(BF16)
-    diag = iota((sites, sites), 0) == iota((sites, sites), 1)
-    triple = jnp.zeros((sites, pairs), F32)
-    weight_sum = jnp.zeros((1, 1), F32)
-    for g in range(occupation.shape[0]):
-        filled = occupation[g : g + 1, :].astype(F32)
-        square = jnp.broadcast_to(filled, (sites, sites))
-        column = jnp.sum(jnp.where(diag, square, 0.0), axis=1, keepdims=True)
-        row_l = mm(square.astype(BF16), from_l)
-        row_j = mm(square.astype(BF16), from_j)
-        scale = weight[0:1, g : g + 1]
-        triple = triple + column * (row_l * row_j) * scale
-        weight_sum = weight_sum + scale
-    own = cfg_at[0] % 2
-    half = 2 * chans
-    keep[0:half, :] = part_s[own]
-    send[0:half, :] = part_s[1 - own]
-    for ref in (keep, send):
-        ref[half : half + sites, :] = triple
-        ref[half + sites : half + sites + PAD_ROWS, :] = jnp.broadcast_to(
-            weight_sum, (PAD_ROWS, pairs)
+    for part in range(2):
+        value = mm_exact(medium[part], onehot)
+        y_s[part] = value
+        y_out[part] = value
+    y_s[2] = y_s[0] + y_s[1]
+    g_s[2] = g_s[0] + g_s[1]
+    batch_mul(y_s, g_s, lambda base, real, imag: put3(f_s, base, chans, real, imag), chans)
+
+    def write_z(base, real, imag):
+        rows = pl.ds(pl.multiple_of(base, chans), chans)
+        z_out[0, rows, :] = real + f_s[0, rows, :]
+        z_out[1, rows, :] = imag + f_s[1, rows, :]
+
+    batch_mul(f_s, f_s, write_z, chans)
+    for part in range(2):
+        parts = split(z_out[part], 3)
+        total = mm_nt(parts[2], wide) + mm_nt(parts[1], wide) + mm_nt(parts[0], wide)
+        packed[part * chans : (part + 1) * chans, :] = fold(total)
+
+    return fold
+
+
+def occupation_slots(place, occupation, weight, rows, width):
+    count, sites = occupation.shape
+    lane = iota((sites, width), 1) % SLOT
+    to_slot = (iota((sites, width), 0) == lane).astype(BF16)
+    slots = jnp.zeros((rows, width), F32)
+    for g in range(count):
+        filled = jnp.broadcast_to(occupation[g : g + 1, :].astype(BF16), (sites, sites))
+        line = mm(filled, to_slot)[0:1] + jnp.where(lane[0:1] == sites, weight[g], 0.0)
+        at = place * count + g
+        per_row = width // SLOT
+        here = (iota((rows, width), 0) == at // per_row) & (
+            iota((rows, width), 1) // SLOT == at % per_row
         )
+        slots = slots + jnp.where(here, line, 0.0)
+    return slots
+
+
+def send_kernel(
+    place, weight, medium, structure, kmap, occupation,
+    packed, z_out, y_out, medium_own, structure_own, kmap_own,
+    y_s, g_s, f_s, medium_s, occupation_s, sems,
+):
+    own = place[0] % 2
+    copies = [
+        (kmap, kmap_own),
+        (medium.at[1 - own], medium_s),
+        (structure.at[1 - own, 0], g_s.at[0]),
+        (structure.at[1 - own, 1], g_s.at[1]),
+        (occupation, occupation_s),
+        (medium.at[own], medium_own),
+        (structure.at[own], structure_own),
+    ]
+    copies = [pltpu.make_async_copy(src, dst, sems.at[n]) for n, (src, dst) in enumerate(copies)]
+    for copy in copies:
+        copy.start()
+    for copy in copies[:5]:
+        copy.wait()
+    medium_val = (medium_s[0], medium_s[1])
+    kpoint_energy(medium_val, kmap_own[...], packed, z_out, y_out, y_s, g_s, f_s)
+    half = 2 * math.isqrt(medium_s.shape[1])
+    packed[half:, :] = occupation_slots(
+        place[0], occupation_s[...], weight, packed.shape[0] - half, packed.shape[1]
+    )
+    for copy in copies[5:]:
+        copy.wait()
+
+
+def keep_kernel(sent, medium, structure, kmap, packed, z_out, y_out, y_row, y_s, g_s, f_s):
+    for part in range(2):
+        g_s[part] = structure[part]
+    medium_val = (medium[0], medium[1])
+    fold = kpoint_energy(medium_val, kmap[...], packed, z_out, y_out, y_s, g_s, f_s)
+    half = 2 * y_row.shape[1]
+    packed[half:, :] = sent[half:, :]
+    count_m, width = medium.shape[2], packed.shape[1]
+    lanes_of = (iota((count_m, width), 0) == iota((count_m, width), 1) * count_m // width).astype(BF16)
+    for part in range(2):
+        y_row[part] = fold(mm_exact(medium_val[part], lanes_of))
 
 
 def square_kernel(y_in, z_in, out, y_s, z_s, t_s):
@@ -253,7 +276,7 @@
     other_start = (cfg_at[0] + 1 - 2 * own) * own_sites
     cols = (slice(0, chans), slice(chans, 2 * chans))
 
-    y_val = (y_row[own, 0], y_row[own, 1])
+    y_val = (y_row[0], y_row[1])
     z_val = (summed[cols[0], :], summed[cols[1], :])
     y_diag = tuple(block_diag(v, chans) for v in y_val)
     coarse = cadd(y_val, cscale(cmul(z_val, y_diag), 1.0 / per_moment))
@@ -315,8 +338,23 @@
         site_s[0, rows, :] = out[0]
         site_s[1, rows, :] = out[1]
 
-    norm = 1.0 / summed[2 * chans + sites : 2 * chans + sites + 1, :]
-    triple = summed[2 * chans : 2 * chans + sites, :] * norm
+    slots = summed[2 * chans :, :]
+    groups = width // SLOT
+    slot_of = iota(slots.shape, 1) // SLOT
+    unpacked = jnp.concatenate([jnp.where(slot_of == n, slots, 0.0) for n in range(groups)], axis=0)
+    place_in = iota((width, width), 0) % SLOT
+    col = iota((width, width), 1)
+    row_l = mm(unpacked.astype(BF16), (place_in == col // sites).astype(BF16))
+    row_j = mm(unpacked.astype(BF16), (place_in == col % sites).astype(BF16))
+    sites_in = (iota((sites, width), 1) % SLOT == iota((sites, width), 0)).astype(BF16)
+    filled_t = mm_nt(sites_in, unpacked.astype(BF16)).astype(BF16)
+    weights = jnp.sum(
+        jnp.where(iota(unpacked.shape, 1) % SLOT == sites, unpacked, 0.0), axis=1, keepdims=True
+    )
+    norm = 1.0 / jnp.sum(weights, axis=0, keepdims=True)
+    pieces = split(weights * (row_l * row_j), 3)
+    triple = mm(filled_t, pieces[2]) + mm(filled_t, pieces[1]) + mm(filled_t, pieces[0])
+    triple = triple * norm
     lane_l = iota((sites, width), 1) // sites
     lane_j = iota((sites, width), 1) % sites
     row_i = iota((sites, width), 0)
@@ -428,7 +466,7 @@
 
 
 def last_kernel(
-    own_rows, cfg_at, kept, got, kmap, square_first, square_second, avg, coarse, correction, d_s
+    own_rows, cfg_at, kept, got, kmap, square_own, square_other, avg, coarse, correction
 ):
     own = cfg_at[0] % 2
     chans = (kept.shape[0] - 2 * own_rows) // 4
@@ -441,7 +479,7 @@
     same_b = iota((width, flat), 0) % chans == iota((width, flat), 1) // chans
     pick_m = (iota((width, count_m), 0) // chans == iota((width, count_m), 1)).astype(BF16)
     same_c = iota((flat, width), 0) % chans == iota((flat, width), 1) % chans
-    for ref, energy in ((kept, own), (got, 1 - own)):
+    for at_slot, (ref, energy) in enumerate(((kept, own), (got, 1 - own))):
         moved = []
         for part in range(2):
             avg[energy, part] = ref[part * own_rows : (part + 1) * own_rows, :]
@@ -453,9 +491,8 @@
             row = ref[at : at + chans, :]
             tall = jnp.broadcast_to(row[:, None, :], (chans, chans, width)).reshape(flat, width)
             coarse[energy, part] = mm_exact(jnp.where(same_c, tall, 0.0), pick_m)
-        d_s[energy] = jnp.concatenate(moved, axis=0)
-    for energy, square in enumerate((square_first, square_second)):
-        both = d_s[energy]
+        both = jnp.concatenate(moved, axis=0)
+        square = (square_own, square_other)[at_slot]
         by_real = mm3(both, square[0])
         by_imag = mm3(both, square[1])
         real = by_real[:count_m] - by_imag[count_m:]
@@ -472,11 +509,11 @@
 VMEM_SPEC = pl.BlockSpec(memory_space=pltpu.VMEM)
 
 
-def call(body, outs, scratch, scalars, args, cost):
+def call(body, outs, scratch, scalars, args, cost, spec=None):
     return pl.pallas_call(
         body,
         out_shape=outs,
-        in_specs=[SMEM_SPEC] * scalars + [VMEM_SPEC] * (len(args) - scalars),
+        in_specs=[SMEM_SPEC] * scalars + [spec or VMEM_SPEC] * (len(args) - scalars),
         out_specs=jax.tree.map(lambda _: VMEM_SPEC, outs),
         scratch_shapes=scratch,
         compiler_params=pltpu.CompilerParams(vmem_limit_bytes=KERNEL_VMEM),
@@ -505,6 +542,7 @@
 def step(medium_t, structure, kmap, occupation, cfg_weight, shift_a, shift_b):
     ka_size, cfg_size = lax.axis_size("ka"), lax.axis_size("cfg")
     total = ka_size * cfg_size
+    count_cfg = occupation.shape[0] * total
     sites = occupation.shape[1]
     chans, count_m = medium_t.shape[2], medium_t.shape[4]
     count_k = kmap.shape[0]
@@ -514,34 +552,57 @@
     own_sites = sites // cfg_size
     own_rows = own_sites * chans
     chip_rows = 2 * own_rows
-    sum_rows = 2 * chans + sites + PAD_ROWS
+    slot_rows = -(-count_cfg * SLOT // width)
+    sum_rows = 2 * chans + -(-slot_rows // 8) * 8
     fwd, back, phases, place_diff = phase_constants(sites, chans)
 
     cfg_at = lax.axis_index("cfg").astype(jnp.int32).reshape(1)
     phases = jnp.asarray(phases)
     kmap_row = kmap.reshape(1, count_k)
 
-    keep, send, *z_y, y_row = call(
-        first_kernel,
-        (
-            shape_of(sum_rows, width),
-            shape_of(sum_rows, width),
-            *[shape_of(2, flat, count_k)] * (2 * ENERGIES),
-            shape_of(ENERGIES, 2, chans, width),
-        ),
-        [pltpu.VMEM((3, flat, count_k), F32)] * 3 + [pltpu.VMEM((ENERGIES, 2 * chans, width), F32)],
-        1,
-        (
-            cfg_at,
-            medium_t.reshape(ENERGIES, 2, flat, count_m),
-            structure,
-            kmap_row,
-            occupation,
-            cfg_weight.reshape(1, -1),
-        ),
-        1 << 24,
-    )
-    summed = keep + swap(send, 1, total)
+    place = lax.axis_index(("ka", "cfg")).astype(jnp.int32).reshape(1)
+    inputs = (
+        place,
+        cfg_weight,
+        medium_t.reshape(ENERGIES, 2, flat, count_m),
+        structure.reshape(ENERGIES, 2, flat, count_k),
+        kmap_row,
+        occupation,
+    )
+    inputs = inputs[:2] + tuple(
+        pltpu.with_memory_space_constraint(value, pltpu.HBM) for value in inputs[2:]
+    )
+    outs = (
+        shape_of(sum_rows, width),
+        shape_of(2, flat, count_k),
+        shape_of(2, flat, count_k),
+    )
+    own_outs = (
+        shape_of(2, flat, count_m),
+        shape_of(2, flat, count_k),
+        jax.ShapeDtypeStruct((1, count_k), jnp.int32),
+    )
+    work = [pltpu.VMEM((3, flat, count_k), F32)] * 3
+    local = [
+        pltpu.VMEM((2, flat, count_m), F32),
+        pltpu.VMEM(occupation.shape, jnp.int32),
+        pltpu.SemaphoreType.DMA((7,)),
+    ]
+    send, z_other, y_other, *own = call(
+        send_kernel,
+        outs + own_outs,
+        work + local,
+        2,
+        inputs,
+        1 << 23,
+        spec=pl.BlockSpec(memory_space=pltpu.HBM),
+    )
+    arrived = swap(send, 1, total)
+    keep, z_own, y_own, y_row = call(
+        keep_kernel, outs + (shape_of(2, chans, width),), work, 0, (send, *own), 1 << 23
+    )
+    summed = keep + arrived
+    y_z = ((y_own, z_own), (y_other, z_other))
     squares = []
     for energy in range(ENERGIES):
         squares.append(
@@ -550,7 +611,7 @@
                 shape_of(2, flat, count_k),
                 [pltpu.VMEM((3, flat, count_k), F32)] * 3,
                 0,
-                (z_y[ENERGIES + energy], z_y[energy]),
+                y_z[energy],
                 1 << 24,
             )
         )
@@ -594,7 +655,7 @@
             shape_of(ENERGIES, 2, flat, count_m),
             shape_of(ENERGIES, 2, count_k),
         ),
-        [pltpu.VMEM((ENERGIES, 2 * count_m, flat), F32)],
+        [],
         1,
         (cfg_at, kept, got, kmap_row, *squares),
         1 << 22,

time: 38.1 us -> 38.4 us (level)
  local copies, waits for them, and re-layouts: 2.77 us -> 0.66 us
  Pallas kernels: 15 us -> 16.5 us
  waiting for transfers between devices: 9.22 us -> 10.5 us
    unnamed x18 -> x12, local copies, waits for them, and re-layouts: 2.77 us -> 0.66 us
    pallas_call x5 -> x6, Pallas kernels: 15 us -> 16.5 us  [call(): pl.pallas_call(body, out_shape=outs, in_specs=[SMEM_SPEC] * scalars + [sp...]
    ppermute x8, waiting for transfers between devices: 9.22 us -> 10.5 us  [swap(): lax.ppermute(value, ('ka', 'cfg'), [(i, i ^ mask) for i in range(total)])]
  transfers between devices with their start and end apart: 8 -> 8, of which waited for: 6 -> 5; matrix products, arithmetic and copies ran while one was open for 0% -> 0% of each run, Pallas kernels for 6% -> 11%
where the time goes in v2:
time: 38.4 us; the launch traced here: 38.3 us
  Pallas kernels  16.5 us (43%)
  waiting for transfers between devices  10.5 us (27%)
  starting transfers between devices  9.18 us (24%)
  between operations  1.41 us (4%)
  local copies, waits for them, and re-layouts  0.66 us (2%)
    pallas_call x6, Pallas kernels, call(): pl.pallas_call(body, out_shape=outs, in_specs=[SMEM_SPEC] * scalars + [sp...  16.5 us
    ppermute x8, waiting for transfers between devices, swap(): lax.ppermute(value, ('ka', 'cfg'), [(i, i ^ mask) for i in range(total)])  10.5 us
    ppermute x8, starting transfers between devices, swap(): lax.ppermute(value, ('ka', 'cfg'), [(i, i ^ mask) for i in range(total)])  9.18 us
  transfers between devices with their start and end apart: 8, of which 5 were waited for; matrix products, arithmetic and copies ran while one was open for 0% of the time, Pallas kernels for 11%

profile of v2, /device:TPU:0, one launch (start us, length us, event | category | flops | bytes accessed | tf_op | source)
XLA Modules:
  0.0 38.3 jit_solution(5511456592335253130)
XLA Ops:
  1.3 2.9 %shard_map.121 = (f32[40,256]{1,0:T(8,128)S(1)}, f32[2,256,128]{2,1,0:T(8,128)S(1)}, f32[2,256,128]{2,1,0:T(8,128)S(1)}, f32[2,256,16]{2,1,0:T(8,128)S(1)}, f32[...) custom-call(s32[1]{0:T(128)} %bitcast.1.place, f32[1]{0:T(128)S(6)} %copy.13.weight, f32[2,2,256,16]{3,2,1,0:T(8,128)} %bitcast.8, ...), custom_call_target="tpu_custom_call" | custom-call | flops 8388608 | bytes 131072 | tf_op jit(solution)/shard_map/pallas_call | solution.py:513
  4.2 0.6 %collective-permute-start = (f32[40,256]{1,0:T(8,128)S(1)}, f32[40,256]{1,0:T(8,128)S(1)}, u32[]{:S(2)}, u32[]{:S(2)}) collective-permute-start(f32[40,256]{1,0:T(8,128)S(1)} %get-tuple-element.18.sent), channel_id=1, source_target_pairs={{0,1},{1,0},{2,3},{3,2},{4,5},{5,4},{6,7},{7,6},{8,9},{9,8},{10,11... | collective-permute-start | bytes 122888 | tf_op jit(solution)/shard_map/ppermute | solution.py:539
  4.8 2.0 %shard_map.122 = (f32[40,256]{1,0:T(8,128)S(1)}, f32[2,256,128]{2,1,0:T(8,128)S(1)}, f32[2,256,128]{2,1,0:T(8,128)S(1)}, f32[2,16,256]{2,1,0:T(8,128)S(1)}) custom-call(f32[40,256]{1,0:T(8,128)S(1)} %get-tuple-element.18.sent, f32[2,256,16]{2,1,0:T(8,128)S(1)} %get-tuple-element.19.medium, f32[2,256,128]{2,1,0:T(8,128)S(1)} %get-tuple-element.20.structure, ...), custom_call_target="tpu_custom_call" | custom-call | flops 8388608 | bytes 131072 | tf_op jit(solution)/shard_map/pallas_call | solution.py:513
  6.8 0.0 copy-start
  6.8 0.0 copy-start.1
  6.8 2.6 %collective-permute-start.1 = (f32[40,256]{1,0:T(8,128)S(1)}, f32[40,256]{1,0:T(8,128)S(1)}, u32[]{:S(2)}, u32[]{:S(2)}) collective-permute-start(f32[40,256]{1,0:T(8,128)S(1)} %add.25), channel_id=1, source_target_pairs={{0,2},{1,3},{2,0},{3,1},{4,6},{5,7},{6,4},{7,5},{8,10},{9,11},{10,... | collective-permute-start | bytes 122888 | tf_op jit(solution)/shard_map/ppermute | solution.py:539
  9.4 1.5 %collective-permute-start.2 = (f32[40,256]{1,0:T(8,128)S(1)}, f32[40,256]{1,0:T(8,128)S(1)}, u32[]{:S(2)}, u32[]{:S(2)}) collective-permute-start(f32[40,256]{1,0:T(8,128)S(1)} %add.25), channel_id=1, source_target_pairs={{0,4},{1,5},{2,6},{3,7},{4,0},{5,1},{6,2},{7,3},{8,12},{9,13},{10,... | collective-permute-start | bytes 122888 | tf_op jit(solution)/shard_map/ppermute | solution.py:539
  10.9 0.0 collective-permute-start.3
  11.0 0.6 %collective-permute-done.1 = f32[40,256]{1,0:T(8,128)S(1)} collective-permute-done((f32[40,256]{1,0:T(8,128)S(1)}, f32[40,256]{1,0:T(8,128)S(1)}, u32[]{:S(2)}, u32[]{:S(2)}) %collective-permute-start.1) | collective-permute-done | bytes 40992 | tf_op jit(solution)/shard_map/ppermute | solution.py:539
  11.6 1.8 %collective-permute-done.2 = f32[40,256]{1,0:T(8,128)S(1)} collective-permute-done((f32[40,256]{1,0:T(8,128)S(1)}, f32[40,256]{1,0:T(8,128)S(1)}, u32[]{:S(2)}, u32[]{:S(2)}) %collective-permute-start.2) | collective-permute-done | bytes 40992 | tf_op jit(solution)/shard_map/ppermute | solution.py:539
  13.4 2.4 %collective-permute-done.3 = f32[40,256]{1,0:T(8,128)S(1)} collective-permute-done((f32[40,256]{1,0:T(8,128)S(1)}, f32[40,256]{1,0:T(8,128)S(1)}, u32[]{:S(2)}, u32[]{:S(2)}) %collective-permute-start.3) | collective-permute-done | bytes 40992 | tf_op jit(solution)/shard_map/ppermute | solution.py:539
  15.9 1.6 %collective-permute-start.4 = (f32[40,256]{1,0:T(8,128)S(1)}, f32[40,256]{1,0:T(8,128)S(1)}, u32[]{:S(2)}, u32[]{:S(2)}) collective-permute-start(f32[40,256]{1,0:T(8,128)S(1)} %add_add_fusion.1), channel_id=1, source_target_pairs={{0,8},{1,9},{2,10},{3,11},{4,12},{5,13},{6,14},{7,15},{8,0},{9,1},... | collective-permute-start | bytes 122888 | tf_op jit(solution)/shard_map/ppermute | solution.py:539
  17.5 2.6 %collective-permute-start.5 = (f32[40,256]{1,0:T(8,128)S(1)}, f32[40,256]{1,0:T(8,128)S(1)}, u32[]{:S(2)}, u32[]{:S(2)}) collective-permute-start(f32[40,256]{1,0:T(8,128)S(1)} %add_add_fusion.1), channel_id=1, source_target_pairs={{0,16},{1,17},{2,18},{3,19},{4,20},{5,21},{6,22},{7,23},{8,24},{9,... | collective-permute-start | bytes 122888 | tf_op jit(solution)/shard_map/ppermute | solution.py:539
  20.1 0.2 collective-permute-start.6
  20.3 0.0 collective-permute-done.4
  20.3 3.0 %collective-permute-done.5 = f32[40,256]{1,0:T(8,128)S(1)} collective-permute-done((f32[40,256]{1,0:T(8,128)S(1)}, f32[40,256]{1,0:T(8,128)S(1)}, u32[]{:S(2)}, u32[]{:S(2)}) %collective-permute-start.5) | collective-permute-done | bytes 40992 | tf_op jit(solution)/shard_map/ppermute | solution.py:539
  23.3 2.6 %collective-permute-done.6 = f32[40,256]{1,0:T(8,128)S(1)} collective-permute-done((f32[40,256]{1,0:T(8,128)S(1)}, f32[40,256]{1,0:T(8,128)S(1)}, u32[]{:S(2)}, u32[]{:S(2)}) %collective-permute-start.6) | collective-permute-done | bytes 40992 | tf_op jit(solution)/shard_map/ppermute | solution.py:539
  26.0 7.2 %shard_map.123 = (f32[192,256]{1,0:T(8,128)S(1)}, f32[192,256]{1,0:T(8,128)S(1)}) custom-call(s32[1]{0:T(128)} %bitcast.cfg_at, f32[40,256]{1,0:T(8,128)S(1)} %add_add_fusion.summed, f32[2,16,256]{2,1,0:T(8,128)S(1)} %get-tuple-element.23.y_row, f32[2,2,16,16]{3,2,1,0:T(8,128)S(1)} %copy-done.2, f32[2,2,16,16]{3,2,1,0:T(8,128)S(1)} %copy-done.3, ...), custom_call_target="tpu_custom_call" | custom-call | flops 67108864 | bytes 1048576 | tf_op jit(solution)/shard_map/pallas_call | solution.py:513
  33.1 0.0 collective-permute-start.7
  33.2 1.2 %shard_map.124.square_own = f32[2,256,128]{2,1,0:T(8,128)S(1)} custom-call(f32[2,256,128]{2,1,0:T(8,128)S(1)} %get-tuple-element.26.y_in, f32[2,256,128]{2,1,0:T(8,128)S(1)} %get-tuple-element.27.z_in), custom_call_target="tpu_custom_call" | custom-call | flops 16777216 | bytes 262144 | tf_op jit(solution)/shard_map/pallas_call | solution.py:513
  34.3 1.1 %shard_map.125.square_other = f32[2,256,128]{2,1,0:T(8,128)S(1)} custom-call(f32[2,256,128]{2,1,0:T(8,128)S(1)} %get-tuple-element.28.y_in, f32[2,256,128]{2,1,0:T(8,128)S(1)} %get-tuple-element.29.z_in), custom_call_target="tpu_custom_call" | custom-call | flops 16777216 | bytes 262144 | tf_op jit(solution)/shard_map/pallas_call | solution.py:513
  35.5 0.0 copy-start.5
  35.5 0.6 %copy-done.5 = s32[128]{0:T(128)S(1)} copy-done((s32[128]{0:T(128)S(1)}, s32[128]{0:T(128)}, u32[]{:S(2)}) %copy-start.5) | copy-done | bytes 536
  36.1 2.1 %shard_map.126 = (f32[2,2,64,256]{3,2,1,0:T(8,128)}, f32[2,2,256,16]{3,2,1,0:T(8,128)}, f32[2,2,128]{2,1,0:T(2,128)}) custom-call(s32[1]{0:T(128)} %bitcast.cfg_at, f32[192,256]{1,0:T(8,128)S(1)} %get-tuple-element.24.kept, f32[192,256]{1,0:T(8,128)S(1)} %collective-permute-done.7.got, s32[1,128]{1,0:T(1,128)S(1)} %bitcast.7, ...), custom_call_target="tpu_custom_call" | custom-call | flops 4194304 | bytes 65536 | tf_op jit(solution)/shard_map/pallas_call | solution.py:513
  (13 shorter events, 0.1 us)
Async XLA Ops:
  4.2 2.6 %collective-permute-start = (f32[40,256]{1,0:T(8,128)S(1)}, f32[40,256]{1,0:T(8,128)S(1)}, u32[]{:S(2)}, u32[]{:S(2)}) collective-permute-start(f32[40,256]{1,0:T(8,128)S(1)} %get-tuple-element.18.sent), channel_id=1, source_target_pairs={{0,1},{1,0},{2,3},{3,2},{4,5},{5,4},{6,7},{7,6},{8,9},{9,8},{10,11... | collective-permute-start | bytes 122888 | tf_op jit(solution)/shard_map/ppermute | solution.py:539
  4.8 21.1 %copy-start.2 = (f32[2,2,16,16]{3,2,1,0:T(8,128)S(1)}, f32[2,2,16,16]{3,2,1,0:T(8,128)}, u32[]{:S(2)}) copy-start(f32[2,2,16,16]{3,2,1,0:T(8,128)} %shift_a.1) | copy-start | bytes 12292
  4.8 21.2 %copy-start.3 = (f32[2,2,16,16]{3,2,1,0:T(8,128)S(1)}, f32[2,2,16,16]{3,2,1,0:T(8,128)}, u32[]{:S(2)}) copy-start(f32[2,2,16,16]{3,2,1,0:T(8,128)} %shift_b.1) | copy-start | bytes 12292
  4.8 21.2 %copy-start.4 = (f32[2,16,256]{2,1,0:T(8,128)S(1)}, f32[2,16,256]{2,1,0:T(8,128)}, u32[]{:S(2)}) copy-start(f32[2,16,256]{2,1,0:T(8,128)} %constant.17.clone.phases) | copy-start | bytes 98308
  6.8 19.1 %copy-start = (bf16[2,256,256]{2,1,0:T(8,128)(2,1)S(1)}, bf16[2,256,256]{2,1,0:T(8,128)(2,1)}, u32[]{:S(2)}) copy-start(bf16[2,256,256]{2,1,0:T(8,128)(2,1)} %constant.18.clone.fwd) | copy-start | bytes 786436
  6.8 19.1 %copy-start.1 = (bf16[2,256,256]{2,1,0:T(8,128)(2,1)S(1)}, bf16[2,256,256]{2,1,0:T(8,128)(2,1)}, u32[]{:S(2)}) copy-start(bf16[2,256,256]{2,1,0:T(8,128)(2,1)} %constant.19.clone.back) | copy-start | bytes 786436
  6.8 4.8 %collective-permute-start.1 = (f32[40,256]{1,0:T(8,128)S(1)}, f32[40,256]{1,0:T(8,128)S(1)}, u32[]{:S(2)}, u32[]{:S(2)}) collective-permute-start(f32[40,256]{1,0:T(8,128)S(1)} %add.25), channel_id=1, source_target_pairs={{0,2},{1,3},{2,0},{3,1},{4,6},{5,7},{6,4},{7,5},{8,10},{9,11},{10,... | collective-permute-start | bytes 122888 | tf_op jit(solution)/shard_map/ppermute | solution.py:539
  9.4 4.0 %collective-permute-start.2 = (f32[40,256]{1,0:T(8,128)S(1)}, f32[40,256]{1,0:T(8,128)S(1)}, u32[]{:S(2)}, u32[]{:S(2)}) collective-permute-start(f32[40,256]{1,0:T(8,128)S(1)} %add.25), channel_id=1, source_target_pairs={{0,4},{1,5},{2,6},{3,7},{4,0},{5,1},{6,2},{7,3},{8,12},{9,13},{10,... | collective-permute-start | bytes 122888 | tf_op jit(solution)/shard_map/ppermute | solution.py:539
  10.9 4.9 %collective-permute-start.3 = (f32[40,256]{1,0:T(8,128)S(1)}, f32[40,256]{1,0:T(8,128)S(1)}, u32[]{:S(2)}, u32[]{:S(2)}) collective-permute-start(f32[40,256]{1,0:T(8,128)S(1)} %add.25), channel_id=1, source_target_pairs={{0,6},{1,7},{2,4},{3,5},{4,2},{5,3},{6,0},{7,1},{8,14},{9,15},{10,... | collective-permute-start | bytes 122888 | tf_op jit(solution)/shard_map/ppermute | solution.py:539
  15.9 4.5 %collective-permute-start.4 = (f32[40,256]{1,0:T(8,128)S(1)}, f32[40,256]{1,0:T(8,128)S(1)}, u32[]{:S(2)}, u32[]{:S(2)}) collective-permute-start(f32[40,256]{1,0:T(8,128)S(1)} %add_add_fusion.1), channel_id=1, source_target_pairs={{0,8},{1,9},{2,10},{3,11},{4,12},{5,13},{6,14},{7,15},{8,0},{9,1},... | collective-permute-start | bytes 122888 | tf_op jit(solution)/shard_map/ppermute | solution.py:539
  17.5 5.8 %collective-permute-start.5 = (f32[40,256]{1,0:T(8,128)S(1)}, f32[40,256]{1,0:T(8,128)S(1)}, u32[]{:S(2)}, u32[]{:S(2)}) collective-permute-start(f32[40,256]{1,0:T(8,128)S(1)} %add_add_fusion.1), channel_id=1, source_target_pairs={{0,16},{1,17},{2,18},{3,19},{4,20},{5,21},{6,22},{7,23},{8,24},{9,... | collective-permute-start | bytes 122888 | tf_op jit(solution)/shard_map/ppermute | solution.py:539
  20.1 5.8 %collective-permute-start.6 = (f32[40,256]{1,0:T(8,128)S(1)}, f32[40,256]{1,0:T(8,128)S(1)}, u32[]{:S(2)}, u32[]{:S(2)}) collective-permute-start(f32[40,256]{1,0:T(8,128)S(1)} %add_add_fusion.1), channel_id=1, source_target_pairs={{0,24},{1,25},{2,26},{3,27},{4,28},{5,29},{6,30},{7,31},{8,16},{9,... | collective-permute-start | bytes 122888 | tf_op jit(solution)/shard_map/ppermute | solution.py:539
  33.1 2.4 %collective-permute-start.7 = (f32[192,256]{1,0:T(8,128)S(1)}, f32[192,256]{1,0:T(8,128)S(1)}, u32[]{:S(2)}, u32[]{:S(2)}) collective-permute-start(f32[192,256]{1,0:T(8,128)S(1)} %get-tuple-element.25), channel_id=1, source_target_pairs={{0,1},{1,0},{2,3},{3,2},{4,5},{5,4},{6,7},{7,6},{8,9},{9,8},{10,11... | collective-permute-start | bytes 589832 | tf_op jit(solution)/shard_map/ppermute | solution.py:539
  35.5 0.7 %copy-start.5 = (s32[128]{0:T(128)S(1)}, s32[128]{0:T(128)}, u32[]{:S(2)}) copy-start(s32[128]{0:T(128)} %param.12) | copy-start | bytes 1540

commit v3 on v2

--- a/solution.py
+++ b/solution.py
@@ -35,16 +35,16 @@
 
 def phase_constants(count_sites, chans):
     angles, place_diff = site_geometry(count_sites)
-    cos_ms = np.rint(np.cos(angles))
-    sin_ms = np.rint(np.sin(angles))
-    eye = np.eye(chans)
-    fwd = np.stack([np.kron(cos_ms, eye), np.kron(-sin_ms, eye)]) / count_sites
-    back = np.stack([np.kron(cos_ms.T, eye), np.kron(sin_ms.T, eye)]) / count_sites
-    rows = np.stack([np.repeat(cos_ms.T, chans, axis=1), np.repeat(sin_ms.T, chans, axis=1)])
+    cells = count_sites // 2
+    signs = np.rint(np.cos(angles[:, :cells]))
+    turn = angles[:, cells]
+    to_cells = np.kron(signs, np.eye(chans)) / count_sites
+    turns = np.stack([np.rint(np.cos(turn)), np.rint(np.sin(turn))])
+    turns = np.repeat(turns, chans, axis=1)
     return (
-        fwd.astype(np.float32),
-        back.astype(np.float32),
-        rows.astype(np.float32),
+        jnp.asarray(to_cells, BF16),
+        jnp.asarray(to_cells.T, BF16),
+        jnp.asarray(np.concatenate([turns] * (chans // 2)), F32),
         place_diff,
     )
 
@@ -72,17 +72,29 @@
 
 
 def mm_exact(left, right_bf16, pieces=3):
-    parts = split(left, pieces)
-    total = mm(parts[-1], right_bf16)
-    for part in parts[-2::-1]:
-        total = total + mm(part, right_bf16)
+    rows = left.shape[0]
+    out = mm(jnp.concatenate(split(left, pieces), axis=0), right_bf16)
+    total = out[(pieces - 1) * rows :]
+    for at in range(pieces - 2, -1, -1):
+        total = total + out[at * rows : (at + 1) * rows]
     return total
 
 
 def mm3(left, right):
+    rows = left.shape[0]
     left_hi, left_lo = split(left, 2)
     right_hi, right_lo = split(right, 2)
-    return mm(left_hi, right_lo) + mm(left_lo, right_hi) + mm(left_hi, right_hi)
+    out = mm(jnp.concatenate([left_hi, left_lo], axis=0), right_hi)
+    return (mm(left_hi, right_lo) + out[rows:]) + out[:rows]
+
+
+def mm3_deep(left, right):
+    left_hi, left_lo = split(left, 2)
+    right_hi, right_lo = split(right, 2)
+    return mm(
+        jnp.concatenate([left_hi, left_lo, left_hi], axis=1),
+        jnp.concatenate([right_lo, right_hi, right_hi], axis=0),
+    )
 
 
 def mm_high(left, right):
@@ -95,6 +107,45 @@
     by_real = mul(both, right[0])
     by_imag = mul(both, right[1])
     return (by_real[:rows] - by_imag[rows:], by_imag[:rows] + by_real[rows:])
+
+
+def flip_cells(value, step):
+    lanes = value.shape[1]
+    ahead = pltpu.roll(value, step, 1)
+    if 2 * step == lanes:
+        return ahead
+    behind = pltpu.roll(value, lanes - step, 1)
+    return jnp.where(iota(value.shape, 1) // step % 2 == 1, ahead, behind)
+
+
+def cell_orders(value, chans):
+    count = value.shape[1] // chans
+    orders = {0: value}
+    at = 0
+    for step in range(1, count):
+        bit = count // 2
+        while step % 2 == 0:
+            step //= 2
+            bit //= 2
+        value = flip_cells(value, bit * chans)
+        at ^= bit
+        orders[at] = value
+    return [orders[n] for n in range(count)]
+
+
+def sum_cells(values, chans):
+    bit = len(values) // 2
+    while bit:
+        values = [values[n] + flip_cells(values[n + bit], bit * chans) for n in range(bit)]
+        bit //= 2
+    return values[0]
+
+
+def turned(value, turns, back=False):
+    cos_t, sin_t = turns[0:1], turns[1:2]
+    if back:
+        sin_t = -sin_t
+    return (cos_t * value[0] - sin_t * value[1], cos_t * value[1] + sin_t * value[0])
 
 
 def cadd(*terms):
@@ -263,13 +314,16 @@
 
 def cluster_kernel(
     per_moment, own_rows, place_diff,
-    cfg_at, summed, y_row, shift_a, shift_b, fwd, back, phases,
-    keep, send, lhs_s, site_s, corr_s, p_s, a_s, n_s,
+    cfg_at, summed, y_row, shift_a, shift_b, to_cells, from_cells, turn_rows,
+    keep, send, site_s, corr_s, p_s, a_s, n_s, c_s,
 ):
     own = cfg_at[0] % 2
     chans = shift_a.shape[2]
     width = summed.shape[1]
-    sites = phases.shape[1]
+    sites = width // turn_rows.shape[0]
+    cells = sites // 2
+    half = cells * chans
+    turns = turn_rows[0:2, :]
     own_sites = own_rows // chans
     rows_n = 2 * own_rows
     own_start = cfg_at[0] * own_sites
@@ -303,40 +357,96 @@
 
     power, lead_kern = small_part(0), small_part(2)
     power_diag = tuple(block_diag(v, chans) for v in power)
+    cell_map = to_cells[...]
+
+    def to_differences(values):
+        rows = []
+        for step in range(2):
+            for value in values:
+                for variant in (value, turned(value, turns)):
+                    rows += [split(part, 2)[step] for part in variant]
+        out = mm(jnp.concatenate(rows, axis=0), cell_map)
+        count = len(values) * 4 * chans
+        out = out[count:] + out[:count]
+        blocks = [out[n * chans : (n + 1) * chans] for n in range(4 * len(values))]
+        return [
+            [[blocks[4 * n + 2 * side + part] for part in range(2)] for side in range(2)]
+            for n in range(len(values))
+        ]
+
+    def kern_to_sites(n, sides):
+        start = n * width
+        for part in range(2):
+            lower = cell_orders(sides[0][part], chans)
+            upper = cell_orders(sides[1][part], chans)
+            for c in range(cells):
+                low = slice(start + c * chans, start + (c + 1) * chans)
+                high = slice(start + half + c * chans, start + half + (c + 1) * chans)
+                site_s[part, low, 0:half] = lower[c]
+                site_s[part, high, half:width] = lower[c]
+                site_s[part, high, 0:half] = upper[c]
+                site_s[part, low, half:width] = upper[c ^ (cells - 1)]
+
     first, first_kern, power = rows_by([coarse, lead_kern, power], power_diag)
     first, first_kern = cscale(first, -1.0), cscale(first_kern, -1.0)
     power_diag = tuple(block_diag(v, chans) for v in power)
+    (lead_sides,) = to_differences([lead_kern])
+    kern_to_sites(0, lead_sides)
     second, third, second_kern = rows_by([coarse, first, lead_kern], power_diag)
     series = [coarse, first, second, third]
     kern = [lead_kern, first_kern, second_kern]
     whole = cadd(*series)
 
-    for i in range(sites):
-        phase = (phases[0, i : i + 1, :], phases[1, i : i + 1, :])
-        for n, (real, imag) in enumerate(kern):
-            start = n * width + i * chans
-            lhs_s[0, start : start + chans, :] = phase[0] * real - phase[1] * imag
-            lhs_s[1, start : start + chans, :] = phase[0] * imag + phase[1] * real
-
+    hi_lo = []
+    for part in range(2):
+        hi, lo = split(site_s[part, 0:width, 0:chans], 2)
+        hi_lo += [hi.astype(F32), hi.astype(F32), lo.astype(F32)]
+    for n, piece in enumerate(hi_lo):
+        a_s[:, n * chans : (n + 1) * chans] = piece
+    a_val = a_s[:, 0 : 6 * chans].astype(BF16)
+    far = cells // 2
+    for c in range(far):
+        rows = slice(c * chans, (c + 1) * chans)
+        high = slice(half + c * chans, half + (c + 1) * chans)
+        pieces = []
+        for part in range(2):
+            line = jnp.concatenate([site_s[part, rows, 0:half], site_s[part, high, 0:half]], axis=1)
+            pieces += split(line, 2)
+        real_hi, real_lo, imag_hi, imag_lo = pieces
+        for part, right in enumerate(
+            (
+                [real_hi, real_lo, real_hi, -imag_hi, -imag_lo, -imag_hi],
+                [imag_hi, imag_lo, imag_hi, real_hi, real_lo, real_hi],
+            )
+        ):
+            out = mm(a_val, jnp.concatenate(right, axis=0))
+            for side in range(2):
+                value = out[:, side * half : (side + 1) * half]
+                p_s[c, side, part] = value
+                p_s[c + far, side, part] = flip_cells(value, half // 2)
+
+    others = [whole] + series[:3]
+    sides_of = to_differences(kern[1:] + others)
+    kern_to_sites(1, sides_of[0])
+    kern_to_sites(2, sides_of[1])
     base = 3 * width
-    for i in range(2 * own_sites):
-        site = own_start + i if i < own_sites else other_start + (i - own_sites)
-        phase = (phases[0, pl.ds(site, 1), :], phases[1, pl.ds(site, 1), :])
-        for n, (real, imag) in enumerate([whole] + series[:3]):
-            start = base + n * rows_n + i * chans
-            lhs_s[0, start : start + chans, :] = phase[0] * real - phase[1] * imag
-            lhs_s[1, start : start + chans, :] = phase[0] * imag + phase[1] * real
-    fwd_val = (fwd[0], fwd[1])
-
-    for start in range(0, base + 4 * rows_n, width):
-        rows = slice(start, start + width)
-        out = cmul(
-            (lhs_s[0, rows, :], lhs_s[1, rows, :]),
-            fwd_val,
-            functools.partial(mm_exact, pieces=2),
-        )
-        site_s[0, rows, :] = out[0]
-        site_s[1, rows, :] = out[1]
+    for n, sides in enumerate(sides_of[2:]):
+        for side in range(2):
+            for part in range(2):
+                for c, value in enumerate(cell_orders(sides[side][part], chans)):
+                    c_s[n, side, part, c] = value
+    for group, first_site in enumerate((own_start, other_start)):
+        for i in range(own_sites):
+            cell = (first_site + i) % cells
+            above = (first_site + i) // cells
+            turned_cell = above * cell + (1 - above) * (cells - 1 - cell)
+            for n in range(4):
+                start = base + n * rows_n + (group * own_sites + i) * chans
+                for part in range(2):
+                    site_s[part, start : start + chans, 0:half] = c_s[n, above, part, cell]
+                    site_s[part, start : start + chans, half:width] = c_s[
+                        n, 1 - above, part, turned_cell
+                    ]
 
     slots = summed[2 * chans :, :]
     groups = width // SLOT
@@ -368,26 +478,6 @@
     ).astype(BF16)
     corr_s[...] = mm_exact(stack, spread_j)
 
-    hi_lo = []
-    for part in range(2):
-        hi, lo = split(site_s[part, 0:width, 0:chans], 2)
-        hi_lo += [hi.astype(F32), hi.astype(F32), lo.astype(F32)]
-    for n, piece in enumerate(hi_lo):
-        a_s[:, n * chans : (n + 1) * chans] = piece
-    a_val = a_s[:, 0 : 6 * chans].astype(BF16)
-    for at in range(sites):
-        rows = slice(at * chans, (at + 1) * chans)
-        real_hi, real_lo = split(site_s[0, rows, :], 2)
-        imag_hi, imag_lo = split(site_s[1, rows, :], 2)
-        right_real = jnp.concatenate(
-            [real_hi, real_lo, real_hi, -imag_hi, -imag_lo, -imag_hi], axis=0
-        )
-        right_imag = jnp.concatenate(
-            [imag_hi, imag_lo, imag_hi, real_hi, real_lo, real_hi], axis=0
-        )
-        p_s[at, 0] = mm(a_val, right_real)
-        p_s[at, 1] = mm(a_val, right_imag)
-
     occupied = corr_s[width + sites : width + sites + 1, :]
 
     for i in range(sites):
@@ -396,67 +486,89 @@
         pair_row = corr_s[width + i : width + i + 1, :]
         on_diag = iota((chans, width), 0) + i * chans == iota((chans, width), 1)
         for part in range(2):
-            total = None
-            for at in range(sites):
-                gap = int(place_diff[i, at])
-                scale = corr_s[at * sites + i : at * sites + i + 1, :]
-                term = scale * p_s[at, part, gap * chans : (gap + 1) * chans, :]
-                total = term if total is None else total + term
+            halves = []
+            for side in range(2):
+                lanes = slice(side * half, (side + 1) * half)
+                total = None
+                for at in range(sites):
+                    gap = int(place_diff[i, at])
+                    above, cell = divmod(at, cells)
+                    if side == 1 and above == 0:
+                        cell = cell ^ (cells - 1)
+                    scale = corr_s[at * sites + i : at * sites + i + 1, lanes]
+                    term = scale * p_s[cell, side ^ above, part, gap * chans : (gap + 1) * chans, :]
+                    total = term if total is None else total + term
+                halves.append(total)
+            total = jnp.concatenate(halves, axis=1)
             lead = pair_row * site_s[part, rows, :]
             if part == 0:
                 lead = lead - jnp.where(on_diag, occupied, 0.0)
             n_s[part, after, :] = lead
             n_s[part, rows, :] = lead + pair_row * site_s[part, after, :] - total
 
-    def site_rows(n):
-        start = base + n * rows_n
-        return (site_s[0, start : start + rows_n, :], site_s[1, start : start + rows_n, :])
-
-    def kernel_of(n):
-        rows = slice(n * width, (n + 1) * width)
-        return (site_s[0, rows, :], site_s[1, rows, :])
-
     mid = [(n_s[0, n * width : (n + 1) * width, :], n_s[1, n * width : (n + 1) * width, :]) for n in range(2)]
-    lead_rows = [site_rows(n) for n in range(4)]
-    minus = -occupied
-    q_zero = cadd(cmul(lead_rows[1], mid[0]), cmul(lead_rows[2], mid[1]), cscale(lead_rows[3], minus))
-    q_one = cadd(cmul(lead_rows[1], mid[1]), cscale(lead_rows[2], minus))
-    q_two = cscale(lead_rows[1], minus)
-    result = cadd(
-        lead_rows[0],
-        cmul(q_zero, kernel_of(0)),
-        cmul(q_one, kernel_of(1)),
-        cmul(q_two, kernel_of(2)),
-    )
-
-    back_val = (back[0], back[1])
-    means = []
-    for n in range(2):
-        moved = cmul(mid[n], back_val, functools.partial(mm_exact, pieces=2))
-        total = None
-        for i in range(sites):
-            rows = slice(i * chans, (i + 1) * chans)
-            phase = (phases[0, i : i + 1, :], phases[1, i : i + 1, :])
-            real, imag = moved[0][rows], moved[1][rows]
-            term = (phase[0] * real + phase[1] * imag, phase[0] * imag - phase[1] * real)
-            total = term if total is None else cadd(total, term)
-        means.append(total)
-    mean_diag = [tuple(block_diag(v, chans) for v in pair_val) for pair_val in means]
-    kern_diag = [tuple(block_diag(v, chans) for v in pair_val) for pair_val in kern]
+    stack = []
+    for value in mid:
+        for part in range(2):
+            low = [value[part][c * chans : (c + 1) * chans] for c in range(cells)]
+            high = [value[part][half + c * chans : half + (c + 1) * chans] for c in range(cells)]
+            stack.append(
+                sum_cells([low[c][:, :half] + high[c][:, half:] for c in range(cells)], chans)
+            )
+            crossed = sum_cells([low[c][:, half:] for c in range(cells)], chans)
+            for bit in (1, 2, 4):
+                crossed = flip_cells(crossed, bit * chans)
+            stack.append(sum_cells([high[c][:, :half] for c in range(cells)], chans) + crossed)
+    moved = mm_exact(jnp.concatenate(stack, axis=0), from_cells[...], pieces=2)
+    moved = [moved[n * chans : (n + 1) * chans] for n in range(8)]
+    means = [
+        cadd(
+            (moved[4 * n], moved[4 * n + 2]),
+            turned((moved[4 * n + 1], moved[4 * n + 3]), turns, back=True),
+        )
+        for n in range(2)
+    ]
+    kern_diag = [tuple(block_diag(v, chans) for v in pair_val) for pair_val in kern[:2]]
     filled = -jnp.mean(occupied, axis=1, keepdims=True)
-    u_zero = cadd(
-        cmul(series[0], mean_diag[0]), cmul(series[1], mean_diag[1]), cscale(series[2], filled)
-    )
-    u_one = cadd(cmul(series[0], mean_diag[1]), cscale(series[1], filled))
-    u_two = cscale(series[0], filled)
+    mean_zero, mean_one, last = rows_by([means[0], means[1], series[2]], kern_diag[0])
+    (mean_next,) = rows_by([means[1]], kern_diag[1])
+    v_zero = cadd(mean_zero, mean_next, cscale(kern[2], filled))
+    v_one = cadd(mean_one, cscale(kern[1], filled))
     change = cadd(
         series[1],
         series[2],
         series[3],
-        cmul(u_zero, kern_diag[0]),
-        cmul(u_one, kern_diag[1]),
-        cmul(u_two, kern_diag[2]),
-    )
+        cmul(series[0], tuple(block_diag(v, chans) for v in v_zero)),
+        cmul(series[1], tuple(block_diag(v, chans) for v in v_one)),
+        cscale(last, filled),
+    )
+
+    def site_rows(n):
+        start = base + n * rows_n
+        return (site_s[0, start : start + rows_n, :], site_s[1, start : start + rows_n, :])
+
+    def side_by_side(*values):
+        return tuple(jnp.concatenate([v[part] for v in values], axis=1) for part in range(2))
+
+    lead_rows = [site_rows(n) for n in range(4)]
+    minus = -occupied
+    q_zero = cadd(
+        cmul(side_by_side(lead_rows[1], lead_rows[2]), (n_s[0], n_s[1]), mm3_deep),
+        cscale(lead_rows[3], minus),
+    )
+    q_one = cadd(cmul(lead_rows[1], mid[1], mm3_deep), cscale(lead_rows[2], minus))
+    q_two = cscale(lead_rows[1], minus)
+    kernels = (site_s[0, 0 : 3 * width, :], site_s[1, 0 : 3 * width, :])
+    q_all = side_by_side(q_zero, q_one, q_two)
+    parts = []
+    for group in range(2):
+        rows = slice(group * own_rows, (group + 1) * own_rows)
+        parts.append(cmul(tuple(v[rows] for v in q_all), kernels, mm3_deep))
+    result = cadd(
+        lead_rows[0],
+        tuple(jnp.concatenate([p[part] for p in parts], axis=0) for part in range(2)),
+    )
+
     for ref, start in ((keep, 0), (send, own_rows)):
         for part in range(2):
             ref[part * own_rows : (part + 1) * own_rows, :] = result[part][start : start + own_rows]
@@ -554,10 +666,9 @@
     chip_rows = 2 * own_rows
     slot_rows = -(-count_cfg * SLOT // width)
     sum_rows = 2 * chans + -(-slot_rows // 8) * 8
-    fwd, back, phases, place_diff = phase_constants(sites, chans)
+    *tables, place_diff = phase_constants(sites, chans)
 
     cfg_at = lax.axis_index("cfg").astype(jnp.int32).reshape(1)
-    phases = jnp.asarray(phases)
     kmap_row = kmap.reshape(1, count_k)
 
     place = lax.axis_index(("ka", "cfg")).astype(jnp.int32).reshape(1)
@@ -622,17 +733,16 @@
         for value in arrived:
             summed = summed + value
     out_rows = 2 * own_rows + 4 * chans
-    lhs_rows = 3 * width + 4 * chip_rows
     kept, sent = call(
         functools.partial(cluster_kernel, per_moment, own_rows, place_diff),
         (shape_of(out_rows, width), shape_of(out_rows, width)),
         [
-            pltpu.VMEM((2, lhs_rows, width), F32),
-            pltpu.VMEM((2, lhs_rows, width), F32),
+            pltpu.VMEM((2, 3 * width + 4 * chip_rows, width), F32),
             pltpu.VMEM((width + sites + PAD_ROWS, width), F32),
-            pltpu.VMEM((sites, 2, width, width), F32),
+            pltpu.VMEM((sites // 2, 2, 2, width, width // 2), F32),
             pltpu.VMEM((width, 128), F32),
             pltpu.VMEM((2, 2 * width, width), F32),
+            pltpu.VMEM((4, 2, 2, sites // 2, chans, width // 2), F32),
         ],
         1,
         (
@@ -641,9 +751,7 @@
             y_row,
             shift_a,
             shift_b,
-            jnp.asarray(fwd, BF16),
-            jnp.asarray(back, BF16),
-            phases,
+            *tables,
         ),
         1 << 26,
     )

time: 38.4 us -> 37 us (0.964)
  Pallas kernels: 16.5 us -> 15 us
    pallas_call x6, Pallas kernels: 16.5 us -> 15 us  [call(): pl.pallas_call(body, out_shape=outs, in_specs=[SMEM_SPEC] * scalars + [sp...]
  transfers between devices with their start and end apart: 8 -> 8, of which waited for: 5 -> 5; matrix products, arithmetic and copies ran while one was open for 0% -> 0% of each run, Pallas kernels for 11% -> 12%
where the time goes in v3:
time: 37 us; the launch traced here: 36.8 us
  Pallas kernels  15 us (41%)
  waiting for transfers between devices  10.5 us (28%)
  starting transfers between devices  9.17 us (25%)
  between operations  1.43 us (4%)
  local copies, waits for them, and re-layouts  0.67 us (2%)
    pallas_call x6, Pallas kernels, call(): pl.pallas_call(body, out_shape=outs, in_specs=[SMEM_SPEC] * scalars + [sp...  15 us
    ppermute x8, waiting for transfers between devices, swap(): lax.ppermute(value, ('ka', 'cfg'), [(i, i ^ mask) for i in range(total)])  10.5 us
    ppermute x8, starting transfers between devices, swap(): lax.ppermute(value, ('ka', 'cfg'), [(i, i ^ mask) for i in range(total)])  9.17 us
  transfers between devices with their start and end apart: 8, of which 5 were waited for; matrix products, arithmetic and copies ran while one was open for 0% of the time, Pallas kernels for 12%

profile of v3, /device:TPU:0, one launch (start us, length us, event | category | flops | bytes accessed | tf_op | source)
XLA Modules:
  0.0 36.8 jit_solution(18414345668758417345)
XLA Ops:
  1.3 2.9 %shard_map.121 = (f32[40,256]{1,0:T(8,128)S(1)}, f32[2,256,128]{2,1,0:T(8,128)S(1)}, f32[2,256,128]{2,1,0:T(8,128)S(1)}, f32[2,256,16]{2,1,0:T(8,128)S(1)}, f32[...) custom-call(s32[1]{0:T(128)} %bitcast.1.place, f32[1]{0:T(128)S(6)} %copy.13.weight, f32[2,2,256,16]{3,2,1,0:T(8,128)} %bitcast.8, ...), custom_call_target="tpu_custom_call" | custom-call | flops 8388608 | bytes 131072 | tf_op jit(solution)/shard_map/pallas_call | solution.py:625
  4.2 0.6 %collective-permute-start = (f32[40,256]{1,0:T(8,128)S(1)}, f32[40,256]{1,0:T(8,128)S(1)}, u32[]{:S(2)}, u32[]{:S(2)}) collective-permute-start(f32[40,256]{1,0:T(8,128)S(1)} %get-tuple-element.18.sent), channel_id=1, source_target_pairs={{0,1},{1,0},{2,3},{3,2},{4,5},{5,4},{6,7},{7,6},{8,9},{9,8},{10,11... | collective-permute-start | bytes 122888 | tf_op jit(solution)/shard_map/ppermute | solution.py:651
  4.7 2.0 %shard_map.122 = (f32[40,256]{1,0:T(8,128)S(1)}, f32[2,256,128]{2,1,0:T(8,128)S(1)}, f32[2,256,128]{2,1,0:T(8,128)S(1)}, f32[2,16,256]{2,1,0:T(8,128)S(1)}) custom-call(f32[40,256]{1,0:T(8,128)S(1)} %get-tuple-element.18.sent, f32[2,256,16]{2,1,0:T(8,128)S(1)} %get-tuple-element.19.medium, f32[2,256,128]{2,1,0:T(8,128)S(1)} %get-tuple-element.20.structure, ...), custom_call_target="tpu_custom_call" | custom-call | flops 8388608 | bytes 131072 | tf_op jit(solution)/shard_map/pallas_call | solution.py:625
  6.8 2.6 %collective-permute-start.1 = (f32[40,256]{1,0:T(8,128)S(1)}, f32[40,256]{1,0:T(8,128)S(1)}, u32[]{:S(2)}, u32[]{:S(2)}) collective-permute-start(f32[40,256]{1,0:T(8,128)S(1)} %add.25), channel_id=1, source_target_pairs={{0,2},{1,3},{2,0},{3,1},{4,6},{5,7},{6,4},{7,5},{8,10},{9,11},{10,... | collective-permute-start | bytes 122888 | tf_op jit(solution)/shard_map/ppermute | solution.py:651
  9.3 1.5 %collective-permute-start.2 = (f32[40,256]{1,0:T(8,128)S(1)}, f32[40,256]{1,0:T(8,128)S(1)}, u32[]{:S(2)}, u32[]{:S(2)}) collective-permute-start(f32[40,256]{1,0:T(8,128)S(1)} %add.25), channel_id=1, source_target_pairs={{0,4},{1,5},{2,6},{3,7},{4,0},{5,1},{6,2},{7,3},{8,12},{9,13},{10,... | collective-permute-start | bytes 122888 | tf_op jit(solution)/shard_map/ppermute | solution.py:651
  10.8 0.0 collective-permute-start.3
  10.9 0.7 %collective-permute-done.1 = f32[40,256]{1,0:T(8,128)S(1)} collective-permute-done((f32[40,256]{1,0:T(8,128)S(1)}, f32[40,256]{1,0:T(8,128)S(1)}, u32[]{:S(2)}, u32[]{:S(2)}) %collective-permute-start.1) | collective-permute-done | bytes 40992 | tf_op jit(solution)/shard_map/ppermute | solution.py:651
  11.5 1.8 %collective-permute-done.2 = f32[40,256]{1,0:T(8,128)S(1)} collective-permute-done((f32[40,256]{1,0:T(8,128)S(1)}, f32[40,256]{1,0:T(8,128)S(1)}, u32[]{:S(2)}, u32[]{:S(2)}) %collective-permute-start.2) | collective-permute-done | bytes 40992 | tf_op jit(solution)/shard_map/ppermute | solution.py:651
  13.3 2.4 %collective-permute-done.3 = f32[40,256]{1,0:T(8,128)S(1)} collective-permute-done((f32[40,256]{1,0:T(8,128)S(1)}, f32[40,256]{1,0:T(8,128)S(1)}, u32[]{:S(2)}, u32[]{:S(2)}) %collective-permute-start.3) | collective-permute-done | bytes 40992 | tf_op jit(solution)/shard_map/ppermute | solution.py:651
  15.8 0.0 copy-start
  15.8 0.0 copy-start.1
  15.8 0.0 copy-start.2
  15.8 0.0 copy-start.3
  15.8 1.6 %collective-permute-start.4 = (f32[40,256]{1,0:T(8,128)S(1)}, f32[40,256]{1,0:T(8,128)S(1)}, u32[]{:S(2)}, u32[]{:S(2)}) collective-permute-start(f32[40,256]{1,0:T(8,128)S(1)} %add_add_fusion.1), channel_id=1, source_target_pairs={{0,8},{1,9},{2,10},{3,11},{4,12},{5,13},{6,14},{7,15},{8,0},{9,1},... | collective-permute-start | bytes 122888 | tf_op jit(solution)/shard_map/ppermute | solution.py:651
  17.5 2.6 %collective-permute-start.5 = (f32[40,256]{1,0:T(8,128)S(1)}, f32[40,256]{1,0:T(8,128)S(1)}, u32[]{:S(2)}, u32[]{:S(2)}) collective-permute-start(f32[40,256]{1,0:T(8,128)S(1)} %add_add_fusion.1), channel_id=1, source_target_pairs={{0,16},{1,17},{2,18},{3,19},{4,20},{5,21},{6,22},{7,23},{8,24},{9,... | collective-permute-start | bytes 122888 | tf_op jit(solution)/shard_map/ppermute | solution.py:651
  20.0 0.2 collective-permute-start.6
  20.3 2.9 %collective-permute-done.5 = f32[40,256]{1,0:T(8,128)S(1)} collective-permute-done((f32[40,256]{1,0:T(8,128)S(1)}, f32[40,256]{1,0:T(8,128)S(1)}, u32[]{:S(2)}, u32[]{:S(2)}) %collective-permute-start.5) | collective-permute-done | bytes 40992 | tf_op jit(solution)/shard_map/ppermute | solution.py:651
  23.2 2.6 %collective-permute-done.6 = f32[40,256]{1,0:T(8,128)S(1)} collective-permute-done((f32[40,256]{1,0:T(8,128)S(1)}, f32[40,256]{1,0:T(8,128)S(1)}, u32[]{:S(2)}, u32[]{:S(2)}) %collective-permute-start.6) | collective-permute-done | bytes 40992 | tf_op jit(solution)/shard_map/ppermute | solution.py:651
  25.9 5.8 %shard_map.123 = (f32[192,256]{1,0:T(8,128)S(1)}, f32[192,256]{1,0:T(8,128)S(1)}) custom-call(s32[1]{0:T(128)} %bitcast.cfg_at, f32[40,256]{1,0:T(8,128)S(1)} %add_add_fusion.summed, f32[2,16,256]{2,1,0:T(8,128)S(1)} %get-tuple-element.23.y_row, f32[2,2,16,16]{3,2,1,0:T(8,128)S(1)} %copy-done.2, f32[2,2,16,16]{3,2,1,0:T(8,128)S(1)} %copy-done.3, ...), custom_call_target="tpu_custom_call" | custom-call | flops 67108864 | bytes 1048576 | tf_op jit(solution)/shard_map/pallas_call | solution.py:625
  31.7 0.1 collective-permute-start.7
  31.8 1.2 %shard_map.124.square_own = f32[2,256,128]{2,1,0:T(8,128)S(1)} custom-call(f32[2,256,128]{2,1,0:T(8,128)S(1)} %get-tuple-element.26.y_in, f32[2,256,128]{2,1,0:T(8,128)S(1)} %get-tuple-element.27.z_in), custom_call_target="tpu_custom_call" | custom-call | flops 16777216 | bytes 262144 | tf_op jit(solution)/shard_map/pallas_call | solution.py:625
  32.9 1.1 %shard_map.125.square_other = f32[2,256,128]{2,1,0:T(8,128)S(1)} custom-call(f32[2,256,128]{2,1,0:T(8,128)S(1)} %get-tuple-element.28.y_in, f32[2,256,128]{2,1,0:T(8,128)S(1)} %get-tuple-element.29.z_in), custom_call_target="tpu_custom_call" | custom-call | flops 16777216 | bytes 262144 | tf_op jit(solution)/shard_map/pallas_call | solution.py:625
  34.1 0.6 %copy-done.5 = s32[128]{0:T(128)S(1)} copy-done((s32[128]{0:T(128)S(1)}, s32[128]{0:T(128)}, u32[]{:S(2)}) %copy-start.5) | copy-done | bytes 536
  34.7 2.1 %shard_map.126 = (f32[2,2,64,256]{3,2,1,0:T(8,128)}, f32[2,2,256,16]{3,2,1,0:T(8,128)}, f32[2,2,128]{2,1,0:T(2,128)}) custom-call(s32[1]{0:T(128)} %bitcast.cfg_at, f32[192,256]{1,0:T(8,128)S(1)} %get-tuple-element.24.kept, f32[192,256]{1,0:T(8,128)S(1)} %collective-permute-done.7.got, s32[1,128]{1,0:T(1,128)S(1)} %bitcast.7, ...), custom_call_target="tpu_custom_call" | custom-call | flops 4194304 | bytes 65536 | tf_op jit(solution)/shard_map/pallas_call | solution.py:625
  (13 shorter events, 0.1 us)
Async XLA Ops:
  4.2 2.6 %collective-permute-start = (f32[40,256]{1,0:T(8,128)S(1)}, f32[40,256]{1,0:T(8,128)S(1)}, u32[]{:S(2)}, u32[]{:S(2)}) collective-permute-start(f32[40,256]{1,0:T(8,128)S(1)} %get-tuple-element.18.sent), channel_id=1, source_target_pairs={{0,1},{1,0},{2,3},{3,2},{4,5},{5,4},{6,7},{7,6},{8,9},{9,8},{10,11... | collective-permute-start | bytes 122888 | tf_op jit(solution)/shard_map/ppermute | solution.py:651
  6.8 4.8 %collective-permute-start.1 = (f32[40,256]{1,0:T(8,128)S(1)}, f32[40,256]{1,0:T(8,128)S(1)}, u32[]{:S(2)}, u32[]{:S(2)}) collective-permute-start(f32[40,256]{1,0:T(8,128)S(1)} %add.25), channel_id=1, source_target_pairs={{0,2},{1,3},{2,0},{3,1},{4,6},{5,7},{6,4},{7,5},{8,10},{9,11},{10,... | collective-permute-start | bytes 122888 | tf_op jit(solution)/shard_map/ppermute | solution.py:651
  9.3 4.0 %collective-permute-start.2 = (f32[40,256]{1,0:T(8,128)S(1)}, f32[40,256]{1,0:T(8,128)S(1)}, u32[]{:S(2)}, u32[]{:S(2)}) collective-permute-start(f32[40,256]{1,0:T(8,128)S(1)} %add.25), channel_id=1, source_target_pairs={{0,4},{1,5},{2,6},{3,7},{4,0},{5,1},{6,2},{7,3},{8,12},{9,13},{10,... | collective-permute-start | bytes 122888 | tf_op jit(solution)/shard_map/ppermute | solution.py:651
  10.8 4.9 %collective-permute-start.3 = (f32[40,256]{1,0:T(8,128)S(1)}, f32[40,256]{1,0:T(8,128)S(1)}, u32[]{:S(2)}, u32[]{:S(2)}) collective-permute-start(f32[40,256]{1,0:T(8,128)S(1)} %add.25), channel_id=1, source_target_pairs={{0,6},{1,7},{2,4},{3,5},{4,2},{5,3},{6,0},{7,1},{8,14},{9,15},{10,... | collective-permute-start | bytes 122888 | tf_op jit(solution)/shard_map/ppermute | solution.py:651
  15.7 10.1 %copy-start.4 = (f32[16,256]{1,0:T(8,128)S(1)}, f32[16,256]{1,0:T(8,128)}, u32[]{:S(2)}) copy-start(f32[16,256]{1,0:T(8,128)} %constant.19.clone.turn_rows) | copy-start | bytes 49156
  15.8 10.1 %copy-start = (bf16[256,128]{1,0:T(8,128)(2,1)S(1)}, bf16[256,128]{1,0:T(8,128)(2,1)}, u32[]{:S(2)}) copy-start(bf16[256,128]{1,0:T(8,128)(2,1)} %constant.17.clone.to_cells) | copy-start | bytes 196612
  15.8 10.1 %copy-start.1 = (bf16[128,256]{1,0:T(8,128)(2,1)S(1)}, bf16[128,256]{1,0:T(8,128)(2,1)}, u32[]{:S(2)}) copy-start(bf16[128,256]{1,0:T(8,128)(2,1)} %constant.18.clone.from_cells) | copy-start | bytes 196612
  15.8 10.1 %copy-start.2 = (f32[2,2,16,16]{3,2,1,0:T(8,128)S(1)}, f32[2,2,16,16]{3,2,1,0:T(8,128)}, u32[]{:S(2)}) copy-start(f32[2,2,16,16]{3,2,1,0:T(8,128)} %shift_a.1) | copy-start | bytes 12292
  15.8 10.1 %copy-start.3 = (f32[2,2,16,16]{3,2,1,0:T(8,128)S(1)}, f32[2,2,16,16]{3,2,1,0:T(8,128)}, u32[]{:S(2)}) copy-start(f32[2,2,16,16]{3,2,1,0:T(8,128)} %shift_b.1) | copy-start | bytes 12292
  15.8 4.5 %collective-permute-start.4 = (f32[40,256]{1,0:T(8,128)S(1)}, f32[40,256]{1,0:T(8,128)S(1)}, u32[]{:S(2)}, u32[]{:S(2)}) collective-permute-start(f32[40,256]{1,0:T(8,128)S(1)} %add_add_fusion.1), channel_id=1, source_target_pairs={{0,8},{1,9},{2,10},{3,11},{4,12},{5,13},{6,14},{7,15},{8,0},{9,1},... | collective-permute-start | bytes 122888 | tf_op jit(solution)/shard_map/ppermute | solution.py:651
  17.5 5.8 %collective-permute-start.5 = (f32[40,256]{1,0:T(8,128)S(1)}, f32[40,256]{1,0:T(8,128)S(1)}, u32[]{:S(2)}, u32[]{:S(2)}) collective-permute-start(f32[40,256]{1,0:T(8,128)S(1)} %add_add_fusion.1), channel_id=1, source_target_pairs={{0,16},{1,17},{2,18},{3,19},{4,20},{5,21},{6,22},{7,23},{8,24},{9,... | collective-permute-start | bytes 122888 | tf_op jit(solution)/shard_map/ppermute | solution.py:651
  20.0 5.8 %collective-permute-start.6 = (f32[40,256]{1,0:T(8,128)S(1)}, f32[40,256]{1,0:T(8,128)S(1)}, u32[]{:S(2)}, u32[]{:S(2)}) collective-permute-start(f32[40,256]{1,0:T(8,128)S(1)} %add_add_fusion.1), channel_id=1, source_target_pairs={{0,24},{1,25},{2,26},{3,27},{4,28},{5,29},{6,30},{7,31},{8,16},{9,... | collective-permute-start | bytes 122888 | tf_op jit(solution)/shard_map/ppermute | solution.py:651
  31.7 2.4 %collective-permute-start.7 = (f32[192,256]{1,0:T(8,128)S(1)}, f32[192,256]{1,0:T(8,128)S(1)}, u32[]{:S(2)}, u32[]{:S(2)}) collective-permute-start(f32[192,256]{1,0:T(8,128)S(1)} %get-tuple-element.25), channel_id=1, source_target_pairs={{0,1},{1,0},{2,3},{3,2},{4,5},{5,4},{6,7},{7,6},{8,9},{9,8},{10,11... | collective-permute-start | bytes 589832 | tf_op jit(solution)/shard_map/ppermute | solution.py:651
  34.1 0.7 %copy-start.5 = (s32[128]{0:T(128)S(1)}, s32[128]{0:T(128)}, u32[]{:S(2)}) copy-start(s32[128]{0:T(128)} %param.12) | copy-start | bytes 1540

commit v4 on v3

--- a/solution.py
+++ b/solution.py
@@ -428,13 +428,72 @@
     others = [whole] + series[:3]
     sides_of = to_differences(kern[1:] + others)
     kern_to_sites(1, sides_of[0])
-    kern_to_sites(2, sides_of[1])
     base = 3 * width
-    for n, sides in enumerate(sides_of[2:]):
+    slots = summed[2 * chans :, :]
+    groups = width // SLOT
+    slot_of = iota(slots.shape, 1) // SLOT
+    unpacked = jnp.concatenate([jnp.where(slot_of == n, slots, 0.0) for n in range(groups)], axis=0)
+    place_in = iota((width, width), 0) % SLOT
+    col = iota((width, width), 1)
+    row_l = mm(unpacked.astype(BF16), (place_in == col // sites).astype(BF16))
+    row_j = mm(unpacked.astype(BF16), (place_in == col % sites).astype(BF16))
+    sites_in = (iota((sites, width), 1) % SLOT == iota((sites, width), 0)).astype(BF16)
+    filled_t = mm_nt(sites_in, unpacked.astype(BF16)).astype(BF16)
+    weights = jnp.sum(
+        jnp.where(iota(unpacked.shape, 1) % SLOT == sites, unpacked, 0.0), axis=1, keepdims=True
+    )
+    norm = 1.0 / jnp.sum(weights, axis=0, keepdims=True)
+    pieces = split(weights * (row_l * row_j), 3)
+    triple = mm(filled_t, pieces[2]) + mm(filled_t, pieces[1]) + mm(filled_t, pieces[0])
+    triple = triple * norm
+    lane_l = iota((sites, width), 1) // sites
+    lane_j = iota((sites, width), 1) % sites
+    row_i = iota((sites, width), 0)
+    pair = jnp.where(lane_l == row_i, triple, 0.0)
+    single = jnp.sum(jnp.where(lane_j == row_i, pair, 0.0), axis=0, keepdims=True)
+    stack = jnp.concatenate(
+        [block_diag(triple, sites), pair, jnp.broadcast_to(single, (PAD_ROWS, width))], axis=0
+    )
+    spread_j = (
+        iota((width, width), 0) % sites == iota((width, width), 1) // chans
+    ).astype(BF16)
+    corr_s[...] = mm_exact(stack, spread_j)
+
+    occupied = corr_s[width + sites : width + sites + 1, :]
+
+    pending = [(n, side, part) for n in range(4) for side in range(2) for part in range(2)]
+    for i in range(sites):
+        rows = slice(i * chans, (i + 1) * chans)
+        after = slice(width + i * chans, width + (i + 1) * chans)
+        pair_row = corr_s[width + i : width + i + 1, :]
+        on_diag = iota((chans, width), 0) + i * chans == iota((chans, width), 1)
+        halves = []
         for side in range(2):
-            for part in range(2):
-                for c, value in enumerate(cell_orders(sides[side][part], chans)):
-                    c_s[n, side, part, c] = value
+            lanes = slice(side * half, (side + 1) * half)
+            totals = [None, None]
+            for at in range(sites):
+                gap = int(place_diff[i, at])
+                above, cell = divmod(at, cells)
+                if side == 1 and above == 0:
+                    cell = cell ^ (cells - 1)
+                scale = corr_s[at * sites + i : at * sites + i + 1, lanes]
+                scale = jnp.broadcast_to(scale, (chans, half))
+                for part in range(2):
+                    term = scale * p_s[cell, side ^ above, part, gap * chans : (gap + 1) * chans, :]
+                    totals[part] = term if totals[part] is None else totals[part] + term
+            halves.append(totals)
+        for part in range(2):
+            total = jnp.concatenate([halves[0][part], halves[1][part]], axis=1)
+            lead = pair_row * site_s[part, rows, :]
+            if part == 0:
+                lead = lead - jnp.where(on_diag, occupied, 0.0)
+            n_s[part, after, :] = lead
+            n_s[part, rows, :] = lead + pair_row * site_s[part, after, :] - total
+        if i == sites // 2:
+            kern_to_sites(2, sides_of[1])
+        for n, side, part in pending[i * len(pending) // sites : (i + 1) * len(pending) // sites]:
+            for c, value in enumerate(cell_orders(sides_of[2 + n][side][part], chans)):
+                c_s[n, side, part, c] = value
     for group, first_site in enumerate((own_start, other_start)):
         for i in range(own_sites):
             cell = (first_site + i) % cells
@@ -448,65 +507,22 @@
                         n, 1 - above, part, turned_cell
                     ]
 
-    slots = summed[2 * chans :, :]
-    groups = width // SLOT
-    slot_of = iota(slots.shape, 1) // SLOT
-    unpacked = jnp.concatenate([jnp.where(slot_of == n, slots, 0.0) for n in range(groups)], axis=0)
-    place_in = iota((width, width), 0) % SLOT
-    col = iota((width, width), 1)
-    row_l = mm(unpacked.astype(BF16), (place_in == col // sites).astype(BF16))
-    row_j = mm(unpacked.astype(BF16), (place_in == col % sites).astype(BF16))
-    sites_in = (iota((sites, width), 1) % SLOT == iota((sites, width), 0)).astype(BF16)
-    filled_t = mm_nt(sites_in, unpacked.astype(BF16)).astype(BF16)
-    weights = jnp.sum(
-        jnp.where(iota(unpacked.shape, 1) % SLOT == sites, unpacked, 0.0), axis=1, keepdims=True
-    )
-    norm = 1.0 / jnp.sum(weights, axis=0, keepdims=True)
-    pieces = split(weights * (row_l * row_j), 3)
-    triple = mm(filled_t, pieces[2]) + mm(filled_t, pieces[1]) + mm(filled_t, pieces[0])
-    triple = triple * norm
-    lane_l = iota((sites, width), 1) // sites
-    lane_j = iota((sites, width), 1) % sites
-    row_i = iota((sites, width), 0)
-    pair = jnp.where(lane_l == row_i, triple, 0.0)
-    single = jnp.sum(jnp.where(lane_j == row_i, pair, 0.0), axis=0, keepdims=True)
-    stack = jnp.concatenate(
-        [block_diag(triple, sites), pair, jnp.broadcast_to(single, (PAD_ROWS, width))], axis=0
-    )
-    spread_j = (
-        iota((width, width), 0) % sites == iota((width, width), 1) // chans
-    ).astype(BF16)
-    corr_s[...] = mm_exact(stack, spread_j)
-
-    occupied = corr_s[width + sites : width + sites + 1, :]
-
-    for i in range(sites):
-        rows = slice(i * chans, (i + 1) * chans)
-        after = slice(width + i * chans, width + (i + 1) * chans)
-        pair_row = corr_s[width + i : width + i + 1, :]
-        on_diag = iota((chans, width), 0) + i * chans == iota((chans, width), 1)
-        for part in range(2):
-            halves = []
-            for side in range(2):
-                lanes = slice(side * half, (side + 1) * half)
-                total = None
-                for at in range(sites):
-                    gap = int(place_diff[i, at])
-                    above, cell = divmod(at, cells)
-                    if side == 1 and above == 0:
-                        cell = cell ^ (cells - 1)
-                    scale = corr_s[at * sites + i : at * sites + i + 1, lanes]
-                    term = scale * p_s[cell, side ^ above, part, gap * chans : (gap + 1) * chans, :]
-                    total = term if total is None else total + term
-                halves.append(total)
-            total = jnp.concatenate(halves, axis=1)
-            lead = pair_row * site_s[part, rows, :]
-            if part == 0:
-                lead = lead - jnp.where(on_diag, occupied, 0.0)
-            n_s[part, after, :] = lead
-            n_s[part, rows, :] = lead + pair_row * site_s[part, after, :] - total
-
     mid = [(n_s[0, n * width : (n + 1) * width, :], n_s[1, n * width : (n + 1) * width, :]) for n in range(2)]
+
+    def site_rows(n):
+        start = base + n * rows_n
+        return (site_s[0, start : start + rows_n, :], site_s[1, start : start + rows_n, :])
+
+    def side_by_side(*values):
+        return tuple(jnp.concatenate([v[part] for v in values], axis=1) for part in range(2))
+
+    lead_rows = [site_rows(n) for n in range(4)]
+    minus = -occupied
+    q_zero = cadd(
+        cmul(side_by_side(lead_rows[1], lead_rows[2]), (n_s[0], n_s[1]), mm3_deep),
+        cscale(lead_rows[3], minus),
+    )
+    q_one = cadd(cmul(lead_rows[1], mid[1], mm3_deep), cscale(lead_rows[2], minus))
     stack = []
     for value in mid:
         for part in range(2):
@@ -542,21 +558,6 @@
         cmul(series[1], tuple(block_diag(v, chans) for v in v_one)),
         cscale(last, filled),
     )
-
-    def site_rows(n):
-        start = base + n * rows_n
-        return (site_s[0, start : start + rows_n, :], site_s[1, start : start + rows_n, :])
-
-    def side_by_side(*values):
-        return tuple(jnp.concatenate([v[part] for v in values], axis=1) for part in range(2))
-
-    lead_rows = [site_rows(n) for n in range(4)]
-    minus = -occupied
-    q_zero = cadd(
-        cmul(side_by_side(lead_rows[1], lead_rows[2]), (n_s[0], n_s[1]), mm3_deep),
-        cscale(lead_rows[3], minus),
-    )
-    q_one = cadd(cmul(lead_rows[1], mid[1], mm3_deep), cscale(lead_rows[2], minus))
     q_two = cscale(lead_rows[1], minus)
     kernels = (site_s[0, 0 : 3 * width, :], site_s[1, 0 : 3 * width, :])
     q_all = side_by_side(q_zero, q_one, q_two)
@@ -577,40 +578,61 @@
                 ref[at : at + chans, :] = value[part]
 
 
-def last_kernel(
-    own_rows, cfg_at, kept, got, kmap, square_own, square_other, avg, coarse, correction
-):
-    own = cfg_at[0] % 2
-    chans = (kept.shape[0] - 2 * own_rows) // 4
-    width = kept.shape[1]
-    flat = coarse.shape[2]
-    count_m = coarse.shape[3]
+def finish_energy(own_rows, ref, kmap, square, coarse, correction):
+    chans = (ref.shape[0] - 2 * own_rows) // 4
+    width = ref.shape[1]
+    flat, count_m = coarse.shape[1:]
     count_k = kmap.shape[1]
     onehot = kmap[...] == iota((count_m, count_k), 0)
     spread_b = (iota((chans, flat), 0) == iota((chans, flat), 1) % chans).astype(BF16)
     same_b = iota((width, flat), 0) % chans == iota((width, flat), 1) // chans
     pick_m = (iota((width, count_m), 0) // chans == iota((width, count_m), 1)).astype(BF16)
     same_c = iota((flat, width), 0) % chans == iota((flat, width), 1) % chans
-    for at_slot, (ref, energy) in enumerate(((kept, own), (got, 1 - own))):
-        moved = []
+    moved = []
+    for part in range(2):
+        at = 2 * own_rows + part * chans
+        wide = mm_exact(ref[at : at + chans, :].T, spread_b)
+        wide = jnp.where(same_b, wide, 0.0).reshape(count_m, chans, flat)
+        moved.append(jnp.sum(wide, axis=1))
+    real, imag = cmul(tuple(moved), (square[0], square[1]))
+    correction[0:1, :] = jnp.sum(jnp.where(onehot, real, 0.0), axis=0, keepdims=True)
+    correction[1:2, :] = jnp.sum(jnp.where(onehot, imag, 0.0), axis=0, keepdims=True)
+    for part in range(2):
+        at = 2 * own_rows + (2 + part) * chans
+        row = ref[at : at + chans, :]
+        tall = jnp.broadcast_to(row[:, None, :], (chans, chans, width)).reshape(flat, width)
+        coarse[part] = mm_exact(jnp.where(same_c, tall, 0.0), pick_m)
+
+
+def own_kernel(own_rows, kept, kmap, square, coarse, correction):
+    finish_energy(own_rows, kept, kmap, square, coarse, correction)
+
+
+def other_kernel(
+    own_rows,
+    cfg_at, kept, got, kmap, square, coarse_own, correction_own,
+    avg, coarse, correction,
+    coarse_s, correction_s, sems,
+):
+    own = cfg_at[0] % 2
+    copies = []
+
+    def send_out(source, target):
+        copy = pltpu.make_async_copy(source, target, sems.at[len(copies)])
+        copy.start()
+        copies.append(copy)
+
+    for ref, energy in ((got, 1 - own), (kept, own)):
         for part in range(2):
-            avg[energy, part] = ref[part * own_rows : (part + 1) * own_rows, :]
-            at = 2 * own_rows + part * chans
-            turned = mm_exact(ref[at : at + chans, :].T, spread_b)
-            turned = jnp.where(same_b, turned, 0.0).reshape(count_m, chans, flat)
-            moved.append(jnp.sum(turned, axis=1))
-            at = 2 * own_rows + (2 + part) * chans
-            row = ref[at : at + chans, :]
-            tall = jnp.broadcast_to(row[:, None, :], (chans, chans, width)).reshape(flat, width)
-            coarse[energy, part] = mm_exact(jnp.where(same_c, tall, 0.0), pick_m)
-        both = jnp.concatenate(moved, axis=0)
-        square = (square_own, square_other)[at_slot]
-        by_real = mm3(both, square[0])
-        by_imag = mm3(both, square[1])
-        real = by_real[:count_m] - by_imag[count_m:]
-        imag = by_imag[:count_m] + by_real[count_m:]
-        correction[energy, 0:1, :] = jnp.sum(jnp.where(onehot, real, 0.0), axis=0, keepdims=True)
-        correction[energy, 1:2, :] = jnp.sum(jnp.where(onehot, imag, 0.0), axis=0, keepdims=True)
+            rows = pl.ds(part * own_rows, own_rows)
+            send_out(ref.at[rows], avg.at[energy, part])
+    send_out(coarse_own, coarse.at[own])
+    send_out(correction_own, correction.at[own])
+    finish_energy(own_rows, got, kmap, square, coarse_s, correction_s)
+    send_out(coarse_s, coarse.at[1 - own])
+    send_out(correction_s, correction.at[1 - own])
+    for copy in copies:
+        copy.wait()
 
 
 def shape_of(*extent):
@@ -621,12 +643,12 @@
 VMEM_SPEC = pl.BlockSpec(memory_space=pltpu.VMEM)
 
 
-def call(body, outs, scratch, scalars, args, cost, spec=None):
+def call(body, outs, scratch, scalars, args, cost, spec=None, out_spec=VMEM_SPEC):
     return pl.pallas_call(
         body,
         out_shape=outs,
         in_specs=[SMEM_SPEC] * scalars + [spec or VMEM_SPEC] * (len(args) - scalars),
-        out_specs=jax.tree.map(lambda _: VMEM_SPEC, outs),
+        out_specs=jax.tree.map(lambda _: out_spec, outs),
         scratch_shapes=scratch,
         compiler_params=pltpu.CompilerParams(vmem_limit_bytes=KERNEL_VMEM),
         cost_estimate=pl.CostEstimate(flops=cost, bytes_accessed=cost // 64, transcendentals=0),
@@ -756,17 +778,30 @@
         1 << 26,
     )
     got = swap(sent, 1, total)
+    coarse_own, correction_own = call(
+        functools.partial(own_kernel, own_rows),
+        (shape_of(2, flat, count_m), shape_of(2, count_k)),
+        [],
+        0,
+        (kept, own[2], squares[0]),
+        1 << 22,
+    )
     avg, coarse, correction = call(
-        functools.partial(last_kernel, own_rows),
+        functools.partial(other_kernel, own_rows),
         (
             shape_of(ENERGIES, 2, own_rows, width),
             shape_of(ENERGIES, 2, flat, count_m),
             shape_of(ENERGIES, 2, count_k),
         ),
-        [],
+        [
+            pltpu.VMEM((2, flat, count_m), F32),
+            pltpu.VMEM((2, count_k), F32),
+            pltpu.SemaphoreType.DMA((8,)),
+        ],
         1,
-        (cfg_at, kept, got, kmap_row, *squares),
+        (cfg_at, kept, got, own[2], squares[1], coarse_own, correction_own),
         1 << 22,
+        out_spec=pl.BlockSpec(memory_space=pltpu.HBM),
     )
     return (coarse.reshape(ENERGIES, 2, chans, chans, count_m), avg, correction)
 

time: 37 us -> 36.2 us (0.978)
  local copies, waits for them, and re-layouts: 0.67 us -> 0.03 us
    unnamed x12 -> x10, local copies, waits for them, and re-layouts: 0.67 us -> 0.03 us
    pallas_call x6 -> x7, Pallas kernels: 15 us -> 14.9 us  [call(): pl.pallas_call(body, out_shape=outs, in_specs=[SMEM_SPEC] * scalars + [sp...]
  transfers between devices with their start and end apart: 8 -> 8, of which waited for: 5 -> 5; matrix products, arithmetic and copies ran while one was open for 0% -> 0% of each run, Pallas kernels for 12% -> 14%
where the time goes in v4:
time: 36.2 us; the launch traced here: 36.1 us
  Pallas kernels  14.9 us (41%)
  waiting for transfers between devices  10.5 us (29%)
  starting transfers between devices  9.17 us (25%)
  between operations  1.43 us (4%)
    pallas_call x7, Pallas kernels, call(): pl.pallas_call(body, out_shape=outs, in_specs=[SMEM_SPEC] * scalars + [sp...  14.9 us
    ppermute x8, waiting for transfers between devices, swap(): lax.ppermute(value, ('ka', 'cfg'), [(i, i ^ mask) for i in range(total)])  10.5 us
    ppermute x8, starting transfers between devices, swap(): lax.ppermute(value, ('ka', 'cfg'), [(i, i ^ mask) for i in range(total)])  9.17 us
  transfers between devices with their start and end apart: 8, of which 5 were waited for; matrix products, arithmetic and copies ran while one was open for 0% of the time, Pallas kernels for 14%

profile of v4, /device:TPU:0, one launch (start us, length us, event | category | flops | bytes accessed | tf_op | source)
XLA Modules:
  0.0 36.1 jit_solution(11602040784353575521)
XLA Ops:
  1.3 2.9 %shard_map.121 = (f32[40,256]{1,0:T(8,128)S(1)}, f32[2,256,128]{2,1,0:T(8,128)S(1)}, f32[2,256,128]{2,1,0:T(8,128)S(1)}, f32[2,256,16]{2,1,0:T(8,128)S(1)}, f32[...) custom-call(s32[1]{0:T(128)} %bitcast.1.place, f32[1]{0:T(128)S(6)} %copy.13.weight, f32[2,2,256,16]{3,2,1,0:T(8,128)} %bitcast.6, ...), custom_call_target="tpu_custom_call" | custom-call | flops 8388608 | bytes 131072 | tf_op jit(solution)/shard_map/pallas_call | solution.py:647
  4.2 0.6 %collective-permute-start = (f32[40,256]{1,0:T(8,128)S(1)}, f32[40,256]{1,0:T(8,128)S(1)}, u32[]{:S(2)}, u32[]{:S(2)}) collective-permute-start(f32[40,256]{1,0:T(8,128)S(1)} %get-tuple-element.20.sent), channel_id=1, source_target_pairs={{0,1},{1,0},{2,3},{3,2},{4,5},{5,4},{6,7},{7,6},{8,9},{9,8},{10,11... | collective-permute-start | bytes 122888 | tf_op jit(solution)/shard_map/ppermute | solution.py:673
  4.7 2.0 %shard_map.122 = (f32[40,256]{1,0:T(8,128)S(1)}, f32[2,256,128]{2,1,0:T(8,128)S(1)}, f32[2,256,128]{2,1,0:T(8,128)S(1)}, f32[2,16,256]{2,1,0:T(8,128)S(1)}) custom-call(f32[40,256]{1,0:T(8,128)S(1)} %get-tuple-element.20.sent, f32[2,256,16]{2,1,0:T(8,128)S(1)} %get-tuple-element.21.medium, f32[2,256,128]{2,1,0:T(8,128)S(1)} %get-tuple-element.22.structure, ...), custom_call_target="tpu_custom_call" | custom-call | flops 8388608 | bytes 131072 | tf_op jit(solution)/shard_map/pallas_call | solution.py:647
  6.8 2.6 %collective-permute-start.1 = (f32[40,256]{1,0:T(8,128)S(1)}, f32[40,256]{1,0:T(8,128)S(1)}, u32[]{:S(2)}, u32[]{:S(2)}) collective-permute-start(f32[40,256]{1,0:T(8,128)S(1)} %add.25), channel_id=1, source_target_pairs={{0,2},{1,3},{2,0},{3,1},{4,6},{5,7},{6,4},{7,5},{8,10},{9,11},{10,... | collective-permute-start | bytes 122888 | tf_op jit(solution)/shard_map/ppermute | solution.py:673
  9.3 1.5 %collective-permute-start.2 = (f32[40,256]{1,0:T(8,128)S(1)}, f32[40,256]{1,0:T(8,128)S(1)}, u32[]{:S(2)}, u32[]{:S(2)}) collective-permute-start(f32[40,256]{1,0:T(8,128)S(1)} %add.25), channel_id=1, source_target_pairs={{0,4},{1,5},{2,6},{3,7},{4,0},{5,1},{6,2},{7,3},{8,12},{9,13},{10,... | collective-permute-start | bytes 122888 | tf_op jit(solution)/shard_map/ppermute | solution.py:673
  10.8 0.0 collective-permute-start.3
  10.9 0.7 %collective-permute-done.1 = f32[40,256]{1,0:T(8,128)S(1)} collective-permute-done((f32[40,256]{1,0:T(8,128)S(1)}, f32[40,256]{1,0:T(8,128)S(1)}, u32[]{:S(2)}, u32[]{:S(2)}) %collective-permute-start.1) | collective-permute-done | bytes 40992 | tf_op jit(solution)/shard_map/ppermute | solution.py:673
  11.6 1.8 %collective-permute-done.2 = f32[40,256]{1,0:T(8,128)S(1)} collective-permute-done((f32[40,256]{1,0:T(8,128)S(1)}, f32[40,256]{1,0:T(8,128)S(1)}, u32[]{:S(2)}, u32[]{:S(2)}) %collective-permute-start.2) | collective-permute-done | bytes 40992 | tf_op jit(solution)/shard_map/ppermute | solution.py:673
  13.3 2.4 %collective-permute-done.3 = f32[40,256]{1,0:T(8,128)S(1)} collective-permute-done((f32[40,256]{1,0:T(8,128)S(1)}, f32[40,256]{1,0:T(8,128)S(1)}, u32[]{:S(2)}, u32[]{:S(2)}) %collective-permute-start.3) | collective-permute-done | bytes 40992 | tf_op jit(solution)/shard_map/ppermute | solution.py:673
  15.8 0.0 copy-start
  15.8 0.0 copy-start.1
  15.8 0.0 copy-start.2
  15.8 0.0 copy-start.3
  15.8 1.6 %collective-permute-start.4 = (f32[40,256]{1,0:T(8,128)S(1)}, f32[40,256]{1,0:T(8,128)S(1)}, u32[]{:S(2)}, u32[]{:S(2)}) collective-permute-start(f32[40,256]{1,0:T(8,128)S(1)} %add_add_fusion.1), channel_id=1, source_target_pairs={{0,8},{1,9},{2,10},{3,11},{4,12},{5,13},{6,14},{7,15},{8,0},{9,1},... | collective-permute-start | bytes 122888 | tf_op jit(solution)/shard_map/ppermute | solution.py:673
  17.5 2.6 %collective-permute-start.5 = (f32[40,256]{1,0:T(8,128)S(1)}, f32[40,256]{1,0:T(8,128)S(1)}, u32[]{:S(2)}, u32[]{:S(2)}) collective-permute-start(f32[40,256]{1,0:T(8,128)S(1)} %add_add_fusion.1), channel_id=1, source_target_pairs={{0,16},{1,17},{2,18},{3,19},{4,20},{5,21},{6,22},{7,23},{8,24},{9,... | collective-permute-start | bytes 122888 | tf_op jit(solution)/shard_map/ppermute | solution.py:673
  20.1 0.2 collective-permute-start.6
  20.3 3.0 %collective-permute-done.5 = f32[40,256]{1,0:T(8,128)S(1)} collective-permute-done((f32[40,256]{1,0:T(8,128)S(1)}, f32[40,256]{1,0:T(8,128)S(1)}, u32[]{:S(2)}, u32[]{:S(2)}) %collective-permute-start.5) | collective-permute-done | bytes 40992 | tf_op jit(solution)/shard_map/ppermute | solution.py:673
  23.2 2.6 %collective-permute-done.6 = f32[40,256]{1,0:T(8,128)S(1)} collective-permute-done((f32[40,256]{1,0:T(8,128)S(1)}, f32[40,256]{1,0:T(8,128)S(1)}, u32[]{:S(2)}, u32[]{:S(2)}) %collective-permute-start.6) | collective-permute-done | bytes 40992 | tf_op jit(solution)/shard_map/ppermute | solution.py:673
  25.9 5.3 %shard_map.123 = (f32[192,256]{1,0:T(8,128)S(1)}, f32[192,256]{1,0:T(8,128)S(1)}) custom-call(s32[1]{0:T(128)} %bitcast.cfg_at, f32[40,256]{1,0:T(8,128)S(1)} %add_add_fusion.summed, f32[2,16,256]{2,1,0:T(8,128)S(1)} %get-tuple-element.25.y_row, f32[2,2,16,16]{3,2,1,0:T(8,128)S(1)} %copy-done.2, f32[2,2,16,16]{3,2,1,0:T(8,128)S(1)} %copy-done.3, ...), custom_call_target="tpu_custom_call" | custom-call | flops 67108864 | bytes 1048576 | tf_op jit(solution)/shard_map/pallas_call | solution.py:647
  31.2 0.1 collective-permute-start.7
  31.3 1.2 %shard_map.125.square = f32[2,256,128]{2,1,0:T(8,128)S(1)} custom-call(f32[2,256,128]{2,1,0:T(8,128)S(1)} %get-tuple-element.30.y_in, f32[2,256,128]{2,1,0:T(8,128)S(1)} %get-tuple-element.31.z_in), custom_call_target="tpu_custom_call" | custom-call | flops 16777216 | bytes 262144 | tf_op jit(solution)/shard_map/pallas_call | solution.py:647
  32.4 1.1 %shard_map.124.square = f32[2,256,128]{2,1,0:T(8,128)S(1)} custom-call(f32[2,256,128]{2,1,0:T(8,128)S(1)} %get-tuple-element.28.y_in, f32[2,256,128]{2,1,0:T(8,128)S(1)} %get-tuple-element.29.z_in), custom_call_target="tpu_custom_call" | custom-call | flops 16777216 | bytes 262144 | tf_op jit(solution)/shard_map/pallas_call | solution.py:647
  33.6 0.8 %shard_map.126 = (f32[2,256,16]{2,1,0:T(8,128)S(1)}, f32[2,128]{1,0:T(2,128)S(1)}) custom-call(f32[192,256]{1,0:T(8,128)S(1)} %get-tuple-element.26.kept, s32[1,128]{1,0:T(1,128)S(1)} %get-tuple-element.23.kmap, f32[2,256,128]{2,1,0:T(8,128)S(1)} %shard_map.125.square), custom_call_target="tpu_custom_call" | custom-call | flops 4194304 | bytes 65536 | tf_op jit(solution)/shard_map/pallas_call | solution.py:647
  34.4 1.6 %shard_map.127 = (f32[2,2,64,256]{3,2,1,0:T(8,128)}, f32[2,2,256,16]{3,2,1,0:T(8,128)}, f32[2,2,128]{2,1,0:T(2,128)}) custom-call(s32[1]{0:T(128)} %bitcast.cfg_at, f32[192,256]{1,0:T(8,128)S(1)} %get-tuple-element.26.kept, f32[192,256]{1,0:T(8,128)S(1)} %collective-permute-done.7.got, s32[1,128]{1,0:T(1,128)S(1)} %get-tuple-element.23.kmap, ...), custom_call_target="tpu_custom_call" | custom-call | flops 4194304 | bytes 65536 | tf_op jit(solution)/shard_map/pallas_call | solution.py:647
  (12 shorter events, 0.1 us)
Async XLA Ops:
  4.2 2.6 %collective-permute-start = (f32[40,256]{1,0:T(8,128)S(1)}, f32[40,256]{1,0:T(8,128)S(1)}, u32[]{:S(2)}, u32[]{:S(2)}) collective-permute-start(f32[40,256]{1,0:T(8,128)S(1)} %get-tuple-element.20.sent), channel_id=1, source_target_pairs={{0,1},{1,0},{2,3},{3,2},{4,5},{5,4},{6,7},{7,6},{8,9},{9,8},{10,11... | collective-permute-start | bytes 122888 | tf_op jit(solution)/shard_map/ppermute | solution.py:673
  6.8 4.8 %collective-permute-start.1 = (f32[40,256]{1,0:T(8,128)S(1)}, f32[40,256]{1,0:T(8,128)S(1)}, u32[]{:S(2)}, u32[]{:S(2)}) collective-permute-start(f32[40,256]{1,0:T(8,128)S(1)} %add.25), channel_id=1, source_target_pairs={{0,2},{1,3},{2,0},{3,1},{4,6},{5,7},{6,4},{7,5},{8,10},{9,11},{10,... | collective-permute-start | bytes 122888 | tf_op jit(solution)/shard_map/ppermute | solution.py:673
  9.3 4.0 %collective-permute-start.2 = (f32[40,256]{1,0:T(8,128)S(1)}, f32[40,256]{1,0:T(8,128)S(1)}, u32[]{:S(2)}, u32[]{:S(2)}) collective-permute-start(f32[40,256]{1,0:T(8,128)S(1)} %add.25), channel_id=1, source_target_pairs={{0,4},{1,5},{2,6},{3,7},{4,0},{5,1},{6,2},{7,3},{8,12},{9,13},{10,... | collective-permute-start | bytes 122888 | tf_op jit(solution)/shard_map/ppermute | solution.py:673
  10.8 4.9 %collective-permute-start.3 = (f32[40,256]{1,0:T(8,128)S(1)}, f32[40,256]{1,0:T(8,128)S(1)}, u32[]{:S(2)}, u32[]{:S(2)}) collective-permute-start(f32[40,256]{1,0:T(8,128)S(1)} %add.25), channel_id=1, source_target_pairs={{0,6},{1,7},{2,4},{3,5},{4,2},{5,3},{6,0},{7,1},{8,14},{9,15},{10,... | collective-permute-start | bytes 122888 | tf_op jit(solution)/shard_map/ppermute | solution.py:673
  15.7 10.1 %copy-start.4 = (f32[16,256]{1,0:T(8,128)S(1)}, f32[16,256]{1,0:T(8,128)}, u32[]{:S(2)}) copy-start(f32[16,256]{1,0:T(8,128)} %constant.19.clone.turn_rows) | copy-start | bytes 49156
  15.8 10.1 %copy-start = (bf16[256,128]{1,0:T(8,128)(2,1)S(1)}, bf16[256,128]{1,0:T(8,128)(2,1)}, u32[]{:S(2)}) copy-start(bf16[256,128]{1,0:T(8,128)(2,1)} %constant.17.clone.to_cells) | copy-start | bytes 196612
  15.8 10.1 %copy-start.1 = (bf16[128,256]{1,0:T(8,128)(2,1)S(1)}, bf16[128,256]{1,0:T(8,128)(2,1)}, u32[]{:S(2)}) copy-start(bf16[128,256]{1,0:T(8,128)(2,1)} %constant.18.clone.from_cells) | copy-start | bytes 196612
  15.8 10.1 %copy-start.2 = (f32[2,2,16,16]{3,2,1,0:T(8,128)S(1)}, f32[2,2,16,16]{3,2,1,0:T(8,128)}, u32[]{:S(2)}) copy-start(f32[2,2,16,16]{3,2,1,0:T(8,128)} %shift_a.1) | copy-start | bytes 12292
  15.8 10.1 %copy-start.3 = (f32[2,2,16,16]{3,2,1,0:T(8,128)S(1)}, f32[2,2,16,16]{3,2,1,0:T(8,128)}, u32[]{:S(2)}) copy-start(f32[2,2,16,16]{3,2,1,0:T(8,128)} %shift_b.1) | copy-start | bytes 12292
  15.8 4.5 %collective-permute-start.4 = (f32[40,256]{1,0:T(8,128)S(1)}, f32[40,256]{1,0:T(8,128)S(1)}, u32[]{:S(2)}, u32[]{:S(2)}) collective-permute-start(f32[40,256]{1,0:T(8,128)S(1)} %add_add_fusion.1), channel_id=1, source_target_pairs={{0,8},{1,9},{2,10},{3,11},{4,12},{5,13},{6,14},{7,15},{8,0},{9,1},... | collective-permute-start | bytes 122888 | tf_op jit(solution)/shard_map/ppermute | solution.py:673
  17.5 5.8 %collective-permute-start.5 = (f32[40,256]{1,0:T(8,128)S(1)}, f32[40,256]{1,0:T(8,128)S(1)}, u32[]{:S(2)}, u32[]{:S(2)}) collective-permute-start(f32[40,256]{1,0:T(8,128)S(1)} %add_add_fusion.1), channel_id=1, source_target_pairs={{0,16},{1,17},{2,18},{3,19},{4,20},{5,21},{6,22},{7,23},{8,24},{9,... | collective-permute-start | bytes 122888 | tf_op jit(solution)/shard_map/ppermute | solution.py:673
  20.1 5.8 %collective-permute-start.6 = (f32[40,256]{1,0:T(8,128)S(1)}, f32[40,256]{1,0:T(8,128)S(1)}, u32[]{:S(2)}, u32[]{:S(2)}) collective-permute-start(f32[40,256]{1,0:T(8,128)S(1)} %add_add_fusion.1), channel_id=1, source_target_pairs={{0,24},{1,25},{2,26},{3,27},{4,28},{5,29},{6,30},{7,31},{8,16},{9,... | collective-permute-start | bytes 122888 | tf_op jit(solution)/shard_map/ppermute | solution.py:673
  31.2 3.2 %collective-permute-start.7 = (f32[192,256]{1,0:T(8,128)S(1)}, f32[192,256]{1,0:T(8,128)S(1)}, u32[]{:S(2)}, u32[]{:S(2)}) collective-permute-start(f32[192,256]{1,0:T(8,128)S(1)} %get-tuple-element.27), channel_id=1, source_target_pairs={{0,1},{1,0},{2,3},{3,2},{4,5},{5,4},{6,7},{7,6},{8,9},{9,8},{10,11... | collective-permute-start | bytes 589832 | tf_op jit(solution)/shard_map/ppermute | solution.py:673

commit v5 on v4

--- a/solution.py
+++ b/solution.py
@@ -167,7 +167,7 @@
 
 
 def batch_mul(left, right, write, chans):
-    group = 4
+    group = 8
 
     def body(step, carry):
         base = step * (group * chans)
@@ -195,7 +195,7 @@
     ref[2, rows, :] = real + imag
 
 
-def kpoint_energy(medium, kmap, packed, z_out, y_out, y_s, g_s, f_s):
+def kpoint_energy(medium, kmap, packed, z_out, y_out, y_s, g_s, f_s, ready=None):
     flat, count_m = medium[0].shape
     count_k = kmap.shape[1]
     chans = math.isqrt(flat)
@@ -212,6 +212,8 @@
         y_s[part] = value
         y_out[part] = value
     y_s[2] = y_s[0] + y_s[1]
+    if ready is not None:
+        ready()
     g_s[2] = g_s[0] + g_s[1]
     batch_mul(y_s, g_s, lambda base, real, imag: put3(f_s, base, chans, real, imag), chans)
 
@@ -222,11 +224,9 @@
 
     batch_mul(f_s, f_s, write_z, chans)
     for part in range(2):
-        parts = split(z_out[part], 3)
-        total = mm_nt(parts[2], wide) + mm_nt(parts[1], wide) + mm_nt(parts[0], wide)
+        parts = split(z_out[part], 2)
+        total = mm_nt(parts[1], wide) + mm_nt(parts[0], wide)
         packed[part * chans : (part + 1) * chans, :] = fold(total)
-
-    return fold
 
 
 def occupation_slots(place, occupation, weight, rows, width):
@@ -264,11 +264,16 @@
     copies = [pltpu.make_async_copy(src, dst, sems.at[n]) for n, (src, dst) in enumerate(copies)]
     for copy in copies:
         copy.start()
-    for copy in copies[:5]:
-        copy.wait()
+    half = 2 * math.isqrt(medium_s.shape[1])
+    copies[0].wait()
+    copies[1].wait()
+
+    def ready():
+        for copy in copies[2:5]:
+            copy.wait()
+
     medium_val = (medium_s[0], medium_s[1])
-    kpoint_energy(medium_val, kmap_own[...], packed, z_out, y_out, y_s, g_s, f_s)
-    half = 2 * math.isqrt(medium_s.shape[1])
+    kpoint_energy(medium_val, kmap_own[...], packed, z_out, y_out, y_s, g_s, f_s, ready)
     packed[half:, :] = occupation_slots(
         place[0], occupation_s[...], weight, packed.shape[0] - half, packed.shape[1]
     )
@@ -276,17 +281,13 @@
         copy.wait()
 
 
-def keep_kernel(sent, medium, structure, kmap, packed, z_out, y_out, y_row, y_s, g_s, f_s):
+def keep_kernel(sent, medium, structure, kmap, packed, z_out, y_out, y_s, g_s, f_s):
     for part in range(2):
         g_s[part] = structure[part]
     medium_val = (medium[0], medium[1])
-    fold = kpoint_energy(medium_val, kmap[...], packed, z_out, y_out, y_s, g_s, f_s)
-    half = 2 * y_row.shape[1]
+    kpoint_energy(medium_val, kmap[...], packed, z_out, y_out, y_s, g_s, f_s)
+    half = 2 * math.isqrt(medium.shape[1])
     packed[half:, :] = sent[half:, :]
-    count_m, width = medium.shape[2], packed.shape[1]
-    lanes_of = (iota((count_m, width), 0) == iota((count_m, width), 1) * count_m // width).astype(BF16)
-    for part in range(2):
-        y_row[part] = fold(mm_exact(medium_val[part], lanes_of))
 
 
 def square_kernel(y_in, z_in, out, y_s, z_s, t_s):
@@ -310,6 +311,17 @@
         out[1, rows, :] = imag
 
     batch_mul(t_s, t_s, write_o, chans)
+
+
+def square_own_kernel(y_in, z_in, medium, out, y_row, y_s, z_s, t_s):
+    square_kernel(y_in, z_in, out, y_s, z_s, t_s)
+    flat, count_m = medium.shape[1:]
+    chans, width = y_row.shape[1:]
+    lanes_of = (iota((count_m, width), 0) == iota((count_m, width), 1) // chans).astype(BF16)
+    same = iota((flat, width), 0) % chans == iota((flat, width), 1) % chans
+    for part in range(2):
+        value = jnp.where(same, mm_exact(medium[part], lanes_of), 0.0)
+        y_row[part] = jnp.sum(value.reshape(chans, chans, width), axis=1)
 
 
 def cluster_kernel(
@@ -457,7 +469,7 @@
     spread_j = (
         iota((width, width), 0) % sites == iota((width, width), 1) // chans
     ).astype(BF16)
-    corr_s[...] = mm_exact(stack, spread_j)
+    corr_s[...] = mm_exact(stack, spread_j, pieces=2)
 
     occupied = corr_s[width + sites : width + sites + 1, :]
 
@@ -591,7 +603,7 @@
     moved = []
     for part in range(2):
         at = 2 * own_rows + part * chans
-        wide = mm_exact(ref[at : at + chans, :].T, spread_b)
+        wide = mm_exact(ref[at : at + chans, :].T, spread_b, pieces=2)
         wide = jnp.where(same_b, wide, 0.0).reshape(count_m, chans, flat)
         moved.append(jnp.sum(wide, axis=1))
     real, imag = cmul(tuple(moved), (square[0], square[1]))
@@ -601,7 +613,7 @@
         at = 2 * own_rows + (2 + part) * chans
         row = ref[at : at + chans, :]
         tall = jnp.broadcast_to(row[:, None, :], (chans, chans, width)).reshape(flat, width)
-        coarse[part] = mm_exact(jnp.where(same_c, tall, 0.0), pick_m)
+        coarse[part] = mm_exact(jnp.where(same_c, tall, 0.0), pick_m, pieces=2)
 
 
 def own_kernel(own_rows, kept, kmap, square, coarse, correction):
@@ -731,23 +743,23 @@
         spec=pl.BlockSpec(memory_space=pltpu.HBM),
     )
     arrived = swap(send, 1, total)
-    keep, z_own, y_own, y_row = call(
-        keep_kernel, outs + (shape_of(2, chans, width),), work, 0, (send, *own), 1 << 23
-    )
+    keep, z_own, y_own = call(keep_kernel, outs, work, 0, (send, *own), 1 << 23)
     summed = keep + arrived
     y_z = ((y_own, z_own), (y_other, z_other))
     squares = []
     for energy in range(ENERGIES):
-        squares.append(
-            call(
-                square_kernel,
-                shape_of(2, flat, count_k),
-                [pltpu.VMEM((3, flat, count_k), F32)] * 3,
+        if energy == 0:
+            square, y_row = call(
+                square_own_kernel,
+                (shape_of(2, flat, count_k), shape_of(2, chans, width)),
+                work,
                 0,
-                y_z[energy],
+                (*y_z[energy], own[0]),
                 1 << 24,
             )
-        )
+        else:
+            square = call(square_kernel, shape_of(2, flat, count_k), work, 0, y_z[energy], 1 << 24)
+        squares.append(square)
     for stage in exchange_stages(ka_size, cfg_size):
         arrived = []
         for mask in stage:

time: 36.2 us -> 31.7 us (0.88)
  waiting for transfers between devices: 10.5 us -> 6.46 us
  Pallas kernels: 14.9 us -> 14.3 us
    ppermute x8, waiting for transfers between devices: 10.5 us -> 6.46 us  [swap(): lax.ppermute(value, ('ka', 'cfg'), [(i, i ^ mask) for i in range(total)])]
    pallas_call x7, Pallas kernels: 14.9 us -> 14.3 us  [call(): pl.pallas_call(body, out_shape=outs, in_specs=[SMEM_SPEC] * scalars + [sp...]
  transfers between devices with their start and end apart: 8 -> 8, of which waited for: 5 -> 4; matrix products, arithmetic and copies ran while one was open for 0% -> 0% of each run, Pallas kernels for 14% -> 15%
where the time goes in v5:
time: 31.7 us; the launch traced here: 31.5 us
  Pallas kernels  14.3 us (45%)
  starting transfers between devices  9.24 us (29%)
  waiting for transfers between devices  6.46 us (20%)
  between operations  1.45 us (5%)
    pallas_call x7, Pallas kernels, call(): pl.pallas_call(body, out_shape=outs, in_specs=[SMEM_SPEC] * scalars + [sp...  14.3 us
    ppermute x8, starting transfers between devices, swap(): lax.ppermute(value, ('ka', 'cfg'), [(i, i ^ mask) for i in range(total)])  9.24 us
    ppermute x8, waiting for transfers between devices, swap(): lax.ppermute(value, ('ka', 'cfg'), [(i, i ^ mask) for i in range(total)])  6.46 us
  transfers between devices with their start and end apart: 8, of which 4 were waited for; matrix products, arithmetic and copies ran while one was open for 0% of the time, Pallas kernels for 15%

profile of v5, /device:TPU:0, one launch (start us, length us, event | category | flops | bytes accessed | tf_op | source)
XLA Modules:
  0.0 31.5 jit_solution(14290560907626924705)
XLA Ops:
  1.3 2.7 %shard_map.121 = (f32[40,256]{1,0:T(8,128)S(1)}, f32[2,256,128]{2,1,0:T(8,128)S(1)}, f32[2,256,128]{2,1,0:T(8,128)S(1)}, f32[2,256,16]{2,1,0:T(8,128)S(1)}, f32[...) custom-call(s32[1]{0:T(128)} %bitcast.1.place, f32[1]{0:T(128)S(6)} %copy.13.weight, f32[2,2,256,16]{3,2,1,0:T(8,128)} %bitcast.6, ...), custom_call_target="tpu_custom_call" | custom-call | flops 8388608 | bytes 131072 | tf_op jit(solution)/shard_map/pallas_call | solution.py:659
  4.0 0.6 %collective-permute-start = (f32[40,256]{1,0:T(8,128)S(1)}, f32[40,256]{1,0:T(8,128)S(1)}, u32[]{:S(2)}, u32[]{:S(2)}) collective-permute-start(f32[40,256]{1,0:T(8,128)S(1)} %get-tuple-element.21.sent), channel_id=1, source_target_pairs={{0,1},{1,0},{2,3},{3,2},{4,5},{5,4},{6,7},{7,6},{8,9},{9,8},{10,11... | collective-permute-start | bytes 122888 | tf_op jit(solution)/shard_map/ppermute | solution.py:685
  4.5 1.6 %shard_map.122 = (f32[40,256]{1,0:T(8,128)S(1)}, f32[2,256,128]{2,1,0:T(8,128)S(1)}, f32[2,256,128]{2,1,0:T(8,128)S(1)}) custom-call(f32[40,256]{1,0:T(8,128)S(1)} %get-tuple-element.21.sent, f32[2,256,16]{2,1,0:T(8,128)S(1)} %get-tuple-element.22.medium, f32[2,256,128]{2,1,0:T(8,128)S(1)} %get-tuple-element.23.structure, s32[1,128]{1,0:T(1,128)S(1)} %get-tuple-element.24.kmap), custom_call_target="tpu_custom_call" | custom-call | flops 8388608 | bytes 131072 | tf_op jit(solution)/shard_map/pallas_call | solution.py:659
  6.2 0.0 collective-permute-done
  6.2 3.5 %collective-permute-start.3 = (f32[40,256]{1,0:T(8,128)S(1)}, f32[40,256]{1,0:T(8,128)S(1)}, u32[]{:S(2)}, u32[]{:S(2)}) collective-permute-start(f32[40,256]{1,0:T(8,128)S(1)} %add.25), channel_id=1, source_target_pairs={{0,6},{1,7},{2,4},{3,5},{4,2},{5,3},{6,0},{7,1},{8,14},{9,15},{10,... | collective-permute-start | bytes 122888 | tf_op jit(solution)/shard_map/ppermute | solution.py:685
  9.7 0.5 %collective-permute-start.2 = (f32[40,256]{1,0:T(8,128)S(1)}, f32[40,256]{1,0:T(8,128)S(1)}, u32[]{:S(2)}, u32[]{:S(2)}) collective-permute-start(f32[40,256]{1,0:T(8,128)S(1)} %add.25), channel_id=1, source_target_pairs={{0,4},{1,5},{2,6},{3,7},{4,0},{5,1},{6,2},{7,3},{8,12},{9,13},{10,... | collective-permute-start | bytes 122888 | tf_op jit(solution)/shard_map/ppermute | solution.py:685
  10.2 0.1 collective-permute-start.1
  10.3 1.6 %collective-permute-done.3 = f32[40,256]{1,0:T(8,128)S(1)} collective-permute-done((f32[40,256]{1,0:T(8,128)S(1)}, f32[40,256]{1,0:T(8,128)S(1)}, u32[]{:S(2)}, u32[]{:S(2)}) %collective-permute-start.3) | collective-permute-done | bytes 40992 | tf_op jit(solution)/shard_map/ppermute | solution.py:685
  11.9 1.8 %collective-permute-done.2 = f32[40,256]{1,0:T(8,128)S(1)} collective-permute-done((f32[40,256]{1,0:T(8,128)S(1)}, f32[40,256]{1,0:T(8,128)S(1)}, u32[]{:S(2)}, u32[]{:S(2)}) %collective-permute-start.2) | collective-permute-done | bytes 40992 | tf_op jit(solution)/shard_map/ppermute | solution.py:685
  13.7 0.5 %collective-permute-done.1 = f32[40,256]{1,0:T(8,128)S(1)} collective-permute-done((f32[40,256]{1,0:T(8,128)S(1)}, f32[40,256]{1,0:T(8,128)S(1)}, u32[]{:S(2)}, u32[]{:S(2)}) %collective-permute-start.1) | collective-permute-done | bytes 40992 | tf_op jit(solution)/shard_map/ppermute | solution.py:685
  14.2 3.6 %collective-permute-start.6 = (f32[40,256]{1,0:T(8,128)S(1)}, f32[40,256]{1,0:T(8,128)S(1)}, u32[]{:S(2)}, u32[]{:S(2)}) collective-permute-start(f32[40,256]{1,0:T(8,128)S(1)} %add_add_fusion.1), channel_id=1, source_target_pairs={{0,24},{1,25},{2,26},{3,27},{4,28},{5,29},{6,30},{7,31},{8,16},{9,... | collective-permute-start | bytes 122888 | tf_op jit(solution)/shard_map/ppermute | solution.py:685
  17.9 0.0 collective-permute-start.5
  17.9 0.8 %collective-permute-start.4 = (f32[40,256]{1,0:T(8,128)S(1)}, f32[40,256]{1,0:T(8,128)S(1)}, u32[]{:S(2)}, u32[]{:S(2)}) collective-permute-start(f32[40,256]{1,0:T(8,128)S(1)} %add_add_fusion.1), channel_id=1, source_target_pairs={{0,8},{1,9},{2,10},{3,11},{4,12},{5,13},{6,14},{7,15},{8,0},{9,1},... | collective-permute-start | bytes 122888 | tf_op jit(solution)/shard_map/ppermute | solution.py:685
  18.7 1.4 %shard_map.123 = (f32[2,256,128]{2,1,0:T(8,128)S(1)}, f32[2,16,256]{2,1,0:T(8,128)S(1)}) custom-call(f32[2,256,128]{2,1,0:T(8,128)S(1)} %get-tuple-element.26.y_in, f32[2,256,128]{2,1,0:T(8,128)S(1)} %get-tuple-element.27.z_in, f32[2,256,16]{2,1,0:T(8,128)S(1)} %get-tuple-element.22.medium), custom_call_target="tpu_custom_call" | custom-call | flops 16777216 | bytes 262144 | tf_op jit(solution)/shard_map/pallas_call | solution.py:659
  20.2 0.0 copy-start
  20.2 0.0 copy-start.1
  20.2 0.0 copy-start.2
  20.2 0.0 copy-start.3
  20.2 2.6 %collective-permute-done.5 = f32[40,256]{1,0:T(8,128)S(1)} collective-permute-done((f32[40,256]{1,0:T(8,128)S(1)}, f32[40,256]{1,0:T(8,128)S(1)}, u32[]{:S(2)}, u32[]{:S(2)}) %collective-permute-start.5) | collective-permute-done | bytes 40992 | tf_op jit(solution)/shard_map/ppermute | solution.py:685
  22.9 5.3 %shard_map.124 = (f32[192,256]{1,0:T(8,128)S(1)}, f32[192,256]{1,0:T(8,128)S(1)}) custom-call(s32[1]{0:T(128)} %bitcast.cfg_at, f32[40,256]{1,0:T(8,128)S(1)} %add_add_fusion.summed, f32[2,16,256]{2,1,0:T(8,128)S(1)} %get-tuple-element.28.y_row, f32[2,2,16,16]{3,2,1,0:T(8,128)S(1)} %copy-done.2, f32[2,2,16,16]{3,2,1,0:T(8,128)S(1)} %copy-done.3, ...), custom_call_target="tpu_custom_call" | custom-call | flops 67108864 | bytes 1048576 | tf_op jit(solution)/shard_map/pallas_call | solution.py:659
  28.1 0.1 collective-permute-start.7
  28.2 1.1 %shard_map.125.square = f32[2,256,128]{2,1,0:T(8,128)S(1)} custom-call(f32[2,256,128]{2,1,0:T(8,128)S(1)} %get-tuple-element.31.y_in, f32[2,256,128]{2,1,0:T(8,128)S(1)} %get-tuple-element.32.z_in), custom_call_target="tpu_custom_call" | custom-call | flops 16777216 | bytes 262144 | tf_op jit(solution)/shard_map/pallas_call | solution.py:659
  29.3 0.7 %shard_map.126 = (f32[2,256,16]{2,1,0:T(8,128)S(1)}, f32[2,128]{1,0:T(2,128)S(1)}) custom-call(f32[192,256]{1,0:T(8,128)S(1)} %get-tuple-element.29.kept, s32[1,128]{1,0:T(1,128)S(1)} %get-tuple-element.24.kmap, f32[2,256,128]{2,1,0:T(8,128)S(1)} %get-tuple-element.33.square), custom_call_target="tpu_custom_call" | custom-call | flops 4194304 | bytes 65536 | tf_op jit(solution)/shard_map/pallas_call | solution.py:659
  30.0 1.5 %shard_map.127 = (f32[2,2,64,256]{3,2,1,0:T(8,128)}, f32[2,2,256,16]{3,2,1,0:T(8,128)}, f32[2,2,128]{2,1,0:T(2,128)}) custom-call(s32[1]{0:T(128)} %bitcast.cfg_at, f32[192,256]{1,0:T(8,128)S(1)} %get-tuple-element.29.kept, f32[192,256]{1,0:T(8,128)S(1)} %collective-permute-done.7.got, s32[1,128]{1,0:T(1,128)S(1)} %get-tuple-element.24.kmap, ...), custom_call_target="tpu_custom_call" | custom-call | flops 4194304 | bytes 65536 | tf_op jit(solution)/shard_map/pallas_call | solution.py:659
  (12 shorter events, 0.1 us)
Async XLA Ops:
  4.0 2.2 %collective-permute-start = (f32[40,256]{1,0:T(8,128)S(1)}, f32[40,256]{1,0:T(8,128)S(1)}, u32[]{:S(2)}, u32[]{:S(2)}) collective-permute-start(f32[40,256]{1,0:T(8,128)S(1)} %get-tuple-element.21.sent), channel_id=1, source_target_pairs={{0,1},{1,0},{2,3},{3,2},{4,5},{5,4},{6,7},{7,6},{8,9},{9,8},{10,11... | collective-permute-start | bytes 122888 | tf_op jit(solution)/shard_map/ppermute | solution.py:685
  6.2 5.7 %collective-permute-start.3 = (f32[40,256]{1,0:T(8,128)S(1)}, f32[40,256]{1,0:T(8,128)S(1)}, u32[]{:S(2)}, u32[]{:S(2)}) collective-permute-start(f32[40,256]{1,0:T(8,128)S(1)} %add.25), channel_id=1, source_target_pairs={{0,6},{1,7},{2,4},{3,5},{4,2},{5,3},{6,0},{7,1},{8,14},{9,15},{10,... | collective-permute-start | bytes 122888 | tf_op jit(solution)/shard_map/ppermute | solution.py:685
  9.7 4.0 %collective-permute-start.2 = (f32[40,256]{1,0:T(8,128)S(1)}, f32[40,256]{1,0:T(8,128)S(1)}, u32[]{:S(2)}, u32[]{:S(2)}) collective-permute-start(f32[40,256]{1,0:T(8,128)S(1)} %add.25), channel_id=1, source_target_pairs={{0,4},{1,5},{2,6},{3,7},{4,0},{5,1},{6,2},{7,3},{8,12},{9,13},{10,... | collective-permute-start | bytes 122888 | tf_op jit(solution)/shard_map/ppermute | solution.py:685
  10.2 4.0 %collective-permute-start.1 = (f32[40,256]{1,0:T(8,128)S(1)}, f32[40,256]{1,0:T(8,128)S(1)}, u32[]{:S(2)}, u32[]{:S(2)}) collective-permute-start(f32[40,256]{1,0:T(8,128)S(1)} %add.25), channel_id=1, source_target_pairs={{0,2},{1,3},{2,0},{3,1},{4,6},{5,7},{6,4},{7,5},{8,10},{9,11},{10,... | collective-permute-start | bytes 122888 | tf_op jit(solution)/shard_map/ppermute | solution.py:685
  14.2 6.0 %collective-permute-start.6 = (f32[40,256]{1,0:T(8,128)S(1)}, f32[40,256]{1,0:T(8,128)S(1)}, u32[]{:S(2)}, u32[]{:S(2)}) collective-permute-start(f32[40,256]{1,0:T(8,128)S(1)} %add_add_fusion.1), channel_id=1, source_target_pairs={{0,24},{1,25},{2,26},{3,27},{4,28},{5,29},{6,30},{7,31},{8,16},{9,... | collective-permute-start | bytes 122888 | tf_op jit(solution)/shard_map/ppermute | solution.py:685
  17.9 4.9 %collective-permute-start.5 = (f32[40,256]{1,0:T(8,128)S(1)}, f32[40,256]{1,0:T(8,128)S(1)}, u32[]{:S(2)}, u32[]{:S(2)}) collective-permute-start(f32[40,256]{1,0:T(8,128)S(1)} %add_add_fusion.1), channel_id=1, source_target_pairs={{0,16},{1,17},{2,18},{3,19},{4,20},{5,21},{6,22},{7,23},{8,24},{9,... | collective-permute-start | bytes 122888 | tf_op jit(solution)/shard_map/ppermute | solution.py:685
  17.9 4.9 %collective-permute-start.4 = (f32[40,256]{1,0:T(8,128)S(1)}, f32[40,256]{1,0:T(8,128)S(1)}, u32[]{:S(2)}, u32[]{:S(2)}) collective-permute-start(f32[40,256]{1,0:T(8,128)S(1)} %add_add_fusion.1), channel_id=1, source_target_pairs={{0,8},{1,9},{2,10},{3,11},{4,12},{5,13},{6,14},{7,15},{8,0},{9,1},... | collective-permute-start | bytes 122888 | tf_op jit(solution)/shard_map/ppermute | solution.py:685
  18.7 4.1 %copy-start.4 = (f32[16,256]{1,0:T(8,128)S(1)}, f32[16,256]{1,0:T(8,128)}, u32[]{:S(2)}) copy-start(f32[16,256]{1,0:T(8,128)} %constant.19.clone.turn_rows) | copy-start | bytes 49156
  20.2 2.7 %copy-start = (bf16[128,256]{1,0:T(8,128)(2,1)S(1)}, bf16[128,256]{1,0:T(8,128)(2,1)}, u32[]{:S(2)}) copy-start(bf16[128,256]{1,0:T(8,128)(2,1)} %constant.18.clone.from_cells) | copy-start | bytes 196612
  20.2 2.7 %copy-start.1 = (bf16[256,128]{1,0:T(8,128)(2,1)S(1)}, bf16[256,128]{1,0:T(8,128)(2,1)}, u32[]{:S(2)}) copy-start(bf16[256,128]{1,0:T(8,128)(2,1)} %constant.17.clone.to_cells) | copy-start | bytes 196612
  20.2 2.7 %copy-start.2 = (f32[2,2,16,16]{3,2,1,0:T(8,128)S(1)}, f32[2,2,16,16]{3,2,1,0:T(8,128)}, u32[]{:S(2)}) copy-start(f32[2,2,16,16]{3,2,1,0:T(8,128)} %shift_a.1) | copy-start | bytes 12292
  20.2 2.7 %copy-start.3 = (f32[2,2,16,16]{3,2,1,0:T(8,128)S(1)}, f32[2,2,16,16]{3,2,1,0:T(8,128)}, u32[]{:S(2)}) copy-start(f32[2,2,16,16]{3,2,1,0:T(8,128)} %shift_b.1) | copy-start | bytes 12292
  28.1 1.9 %collective-permute-start.7 = (f32[192,256]{1,0:T(8,128)S(1)}, f32[192,256]{1,0:T(8,128)S(1)}, u32[]{:S(2)}, u32[]{:S(2)}) collective-permute-start(f32[192,256]{1,0:T(8,128)S(1)} %get-tuple-element.30), channel_id=1, source_target_pairs={{0,1},{1,0},{2,3},{3,2},{4,5},{5,4},{6,7},{7,6},{8,9},{9,8},{10,11... | collective-permute-start | bytes 589832 | tf_op jit(solution)/shard_map/ppermute | solution.py:685

commit v6 on v5

--- a/solution.py
+++ b/solution.py
@@ -139,6 +139,18 @@
         values = [values[n] + flip_cells(values[n + bit], bit * chans) for n in range(bit)]
         bit //= 2
     return values[0]
+
+
+def by_momentum(row, chans, inner_first):
+    width = row.shape[1]
+    flat = chans * chans
+    outer, inner = iota((chans, flat), 1) // chans, iota((chans, flat), 1) % chans
+    at = inner if inner_first else outer
+    wide = mm_exact(row.T, (iota((chans, flat), 0) == at).astype(BF16), pieces=2)
+    lane = iota((width, flat), 1)
+    lane = lane // chans if inner_first else lane % chans
+    wide = jnp.where(iota((width, flat), 0) % chans == lane, wide, 0.0)
+    return jnp.sum(wide.reshape(width // chans, chans, flat), axis=1)
 
 
 def turned(value, turns, back=False):
@@ -199,7 +211,7 @@
     flat, count_m = medium[0].shape
     count_k = kmap.shape[1]
     chans = math.isqrt(flat)
-    width = packed.shape[1]
+    width = 2 * packed.shape[1]
     onehot = (kmap == iota((count_m, count_k), 0)).astype(BF16)
     wide = (kmap == iota((width, count_k), 0) // chans).astype(BF16)
     same = iota((flat, width), 0) % chans == iota((flat, width), 1) % chans
@@ -226,7 +238,10 @@
     for part in range(2):
         parts = split(z_out[part], 2)
         total = mm_nt(parts[1], wide) + mm_nt(parts[0], wide)
-        packed[part * chans : (part + 1) * chans, :] = fold(total)
+        folded = fold(total)
+        for side in range(2):
+            at = (2 * side + part) * chans
+            packed[at : at + chans, :] = folded[:, side * width // 2 : (side + 1) * width // 2]
 
 
 def occupation_slots(place, occupation, weight, rows, width):
@@ -264,7 +279,7 @@
     copies = [pltpu.make_async_copy(src, dst, sems.at[n]) for n, (src, dst) in enumerate(copies)]
     for copy in copies:
         copy.start()
-    half = 2 * math.isqrt(medium_s.shape[1])
+    half = 4 * math.isqrt(medium_s.shape[1])
     copies[0].wait()
     copies[1].wait()
 
@@ -286,7 +301,7 @@
         g_s[part] = structure[part]
     medium_val = (medium[0], medium[1])
     kpoint_energy(medium_val, kmap[...], packed, z_out, y_out, y_s, g_s, f_s)
-    half = 2 * math.isqrt(medium.shape[1])
+    half = 4 * math.isqrt(medium.shape[1])
     packed[half:, :] = sent[half:, :]
 
 
@@ -331,7 +346,7 @@
 ):
     own = cfg_at[0] % 2
     chans = shift_a.shape[2]
-    width = summed.shape[1]
+    width = 2 * summed.shape[1]
     sites = width // turn_rows.shape[0]
     cells = sites // 2
     half = cells * chans
@@ -340,13 +355,20 @@
     rows_n = 2 * own_rows
     own_start = cfg_at[0] * own_sites
     other_start = (cfg_at[0] + 1 - 2 * own) * own_sites
-    cols = (slice(0, chans), slice(chans, 2 * chans))
 
     y_val = (y_row[0], y_row[1])
-    z_val = (summed[cols[0], :], summed[cols[1], :])
+    z_val = tuple(
+        jnp.concatenate(
+            [summed[(2 * side + part) * chans : (2 * side + part + 1) * chans, :] for side in range(2)],
+            axis=1,
+        )
+        for part in range(2)
+    )
     y_diag = tuple(block_diag(v, chans) for v in y_val)
     coarse = cadd(y_val, cscale(cmul(z_val, y_diag), 1.0 / per_moment))
 
+    coarse_rows = tuple(by_momentum(value, chans, False) for value in coarse)
+    count_m = width // chans
     base_t = (shift_b[own, 0], shift_b[own, 1])
     step_t = (shift_a[own, 0] - base_t[0], shift_a[own, 1] - base_t[1])
 
@@ -441,15 +463,16 @@
     sides_of = to_differences(kern[1:] + others)
     kern_to_sites(1, sides_of[0])
     base = 3 * width
-    slots = summed[2 * chans :, :]
-    groups = width // SLOT
+    slots = summed[4 * chans :, :]
+    lanes_n = slots.shape[1]
+    groups = lanes_n // SLOT
     slot_of = iota(slots.shape, 1) // SLOT
     unpacked = jnp.concatenate([jnp.where(slot_of == n, slots, 0.0) for n in range(groups)], axis=0)
-    place_in = iota((width, width), 0) % SLOT
-    col = iota((width, width), 1)
+    place_in = iota((lanes_n, width), 0) % SLOT
+    col = iota((lanes_n, width), 1)
     row_l = mm(unpacked.astype(BF16), (place_in == col // sites).astype(BF16))
     row_j = mm(unpacked.astype(BF16), (place_in == col % sites).astype(BF16))
-    sites_in = (iota((sites, width), 1) % SLOT == iota((sites, width), 0)).astype(BF16)
+    sites_in = (iota((sites, lanes_n), 1) % SLOT == iota((sites, lanes_n), 0)).astype(BF16)
     filled_t = mm_nt(sites_in, unpacked.astype(BF16)).astype(BF16)
     weights = jnp.sum(
         jnp.where(iota(unpacked.shape, 1) % SLOT == sites, unpacked, 0.0), axis=1, keepdims=True
@@ -570,6 +593,7 @@
         cmul(series[1], tuple(block_diag(v, chans) for v in v_one)),
         cscale(last, filled),
     )
+    change_rows = tuple(by_momentum(value, chans, True) for value in change)
     q_two = cscale(lead_rows[1], minus)
     kernels = (site_s[0, 0 : 3 * width, :], site_s[1, 0 : 3 * width, :])
     q_all = side_by_side(q_zero, q_one, q_two)
@@ -585,35 +609,21 @@
     for ref, start in ((keep, 0), (send, own_rows)):
         for part in range(2):
             ref[part * own_rows : (part + 1) * own_rows, :] = result[part][start : start + own_rows]
-            for n, value in enumerate((change, coarse)):
-                at = 2 * own_rows + (2 * n + part) * chans
-                ref[at : at + chans, :] = value[part]
+            for n, value in enumerate((change_rows, coarse_rows)):
+                at = 2 * own_rows + (2 * n + part) * count_m
+                ref[at : at + count_m, :] = value[part]
 
 
 def finish_energy(own_rows, ref, kmap, square, coarse, correction):
-    chans = (ref.shape[0] - 2 * own_rows) // 4
-    width = ref.shape[1]
-    flat, count_m = coarse.shape[1:]
+    count_m = coarse.shape[2]
     count_k = kmap.shape[1]
     onehot = kmap[...] == iota((count_m, count_k), 0)
-    spread_b = (iota((chans, flat), 0) == iota((chans, flat), 1) % chans).astype(BF16)
-    same_b = iota((width, flat), 0) % chans == iota((width, flat), 1) // chans
-    pick_m = (iota((width, count_m), 0) // chans == iota((width, count_m), 1)).astype(BF16)
-    same_c = iota((flat, width), 0) % chans == iota((flat, width), 1) % chans
-    moved = []
+    blocks = [ref[2 * own_rows + n * count_m : 2 * own_rows + (n + 1) * count_m, :] for n in range(4)]
     for part in range(2):
-        at = 2 * own_rows + part * chans
-        wide = mm_exact(ref[at : at + chans, :].T, spread_b, pieces=2)
-        wide = jnp.where(same_b, wide, 0.0).reshape(count_m, chans, flat)
-        moved.append(jnp.sum(wide, axis=1))
-    real, imag = cmul(tuple(moved), (square[0], square[1]))
+        coarse[part] = blocks[2 + part].T
+    real, imag = cmul((blocks[0], blocks[1]), (square[0], square[1]))
     correction[0:1, :] = jnp.sum(jnp.where(onehot, real, 0.0), axis=0, keepdims=True)
     correction[1:2, :] = jnp.sum(jnp.where(onehot, imag, 0.0), axis=0, keepdims=True)
-    for part in range(2):
-        at = 2 * own_rows + (2 + part) * chans
-        row = ref[at : at + chans, :]
-        tall = jnp.broadcast_to(row[:, None, :], (chans, chans, width)).reshape(flat, width)
-        coarse[part] = mm_exact(jnp.where(same_c, tall, 0.0), pick_m, pieces=2)
 
 
 def own_kernel(own_rows, kept, kmap, square, coarse, correction):
@@ -698,8 +708,8 @@
     own_sites = sites // cfg_size
     own_rows = own_sites * chans
     chip_rows = 2 * own_rows
-    slot_rows = -(-count_cfg * SLOT // width)
-    sum_rows = 2 * chans + -(-slot_rows // 8) * 8
+    slot_rows = -(-count_cfg * SLOT // (width // 2))
+    sum_rows = 4 * chans + -(-slot_rows // 8) * 8
     *tables, place_diff = phase_constants(sites, chans)
 
     cfg_at = lax.axis_index("cfg").astype(jnp.int32).reshape(1)
@@ -718,7 +728,7 @@
         pltpu.with_memory_space_constraint(value, pltpu.HBM) for value in inputs[2:]
     )
     outs = (
-        shape_of(sum_rows, width),
+        shape_of(sum_rows, width // 2),
         shape_of(2, flat, count_k),
         shape_of(2, flat, count_k),
     )
@@ -766,10 +776,10 @@
             arrived.append(swap(summed, mask, total))
         for value in arrived:
             summed = summed + value
-    out_rows = 2 * own_rows + 4 * chans
+    out_rows = 2 * own_rows + 4 * count_m
     kept, sent = call(
         functools.partial(cluster_kernel, per_moment, own_rows, place_diff),
-        (shape_of(out_rows, width), shape_of(out_rows, width)),
+        (shape_of(out_rows, flat), shape_of(out_rows, flat)),
         [
             pltpu.VMEM((2, 3 * width + 4 * chip_rows, width), F32),
             pltpu.VMEM((width + sites + PAD_ROWS, width), F32),

time: 31.7 us -> 31.4 us (level)
  transfers between devices with their start and end apart: 8 -> 8, of which waited for: 4 -> 5; matrix products, arithmetic and copies ran while one was open for 0% -> 0% of each run, Pallas kernels for 15% -> 14%
where the time goes in v6:
time: 31.4 us; the launch traced here: 31.3 us
  Pallas kernels  14 us (45%)
  starting transfers between devices  9.23 us (29%)
  waiting for transfers between devices  6.53 us (21%)
  between operations  1.44 us (5%)
    pallas_call x7, Pallas kernels, call(): pl.pallas_call(body, out_shape=outs, in_specs=[SMEM_SPEC] * scalars + [sp...  14 us
    ppermute x8, starting transfers between devices, swap(): lax.ppermute(value, ('ka', 'cfg'), [(i, i ^ mask) for i in range(total)])  9.23 us
    ppermute x8, waiting for transfers between devices, swap(): lax.ppermute(value, ('ka', 'cfg'), [(i, i ^ mask) for i in range(total)])  6.53 us
  transfers between devices with their start and end apart: 8, of which 5 were waited for; matrix products, arithmetic and copies ran while one was open for 0% of the time, Pallas kernels for 14%

profile of v6, /device:TPU:0, one launch (start us, length us, event | category | flops | bytes accessed | tf_op | source)
XLA Modules:
  0.0 31.3 jit_solution(12404570373610254431)
XLA Ops:
  1.3 2.7 %shard_map.121 = (f32[72,128]{1,0:T(8,128)S(1)}, f32[2,256,128]{2,1,0:T(8,128)S(1)}, f32[2,256,128]{2,1,0:T(8,128)S(1)}, f32[2,256,16]{2,1,0:T(8,128)S(1)}, f32[...) custom-call(s32[1]{0:T(128)} %bitcast.1.place, f32[1]{0:T(128)S(6)} %copy.13.weight, f32[2,2,256,16]{3,2,1,0:T(8,128)} %bitcast.6, ...), custom_call_target="tpu_custom_call" | custom-call | flops 8388608 | bytes 131072 | tf_op jit(solution)/shard_map/pallas_call | solution.py:669
  4.0 0.6 %collective-permute-start = (f32[72,128]{1,0:T(8,128)S(1)}, f32[72,128]{1,0:T(8,128)S(1)}, u32[]{:S(2)}, u32[]{:S(2)}) collective-permute-start(f32[72,128]{1,0:T(8,128)S(1)} %get-tuple-element.21.sent), channel_id=1, source_target_pairs={{0,1},{1,0},{2,3},{3,2},{4,5},{5,4},{6,7},{7,6},{8,9},{9,8},{10,11... | collective-permute-start | bytes 110600 | tf_op jit(solution)/shard_map/ppermute | solution.py:695
  4.5 1.6 %shard_map.122 = (f32[72,128]{1,0:T(8,128)S(1)}, f32[2,256,128]{2,1,0:T(8,128)S(1)}, f32[2,256,128]{2,1,0:T(8,128)S(1)}) custom-call(f32[72,128]{1,0:T(8,128)S(1)} %get-tuple-element.21.sent, f32[2,256,16]{2,1,0:T(8,128)S(1)} %get-tuple-element.22.medium, f32[2,256,128]{2,1,0:T(8,128)S(1)} %get-tuple-element.23.structure, s32[1,128]{1,0:T(1,128)S(1)} %get-tuple-element.24.kmap), custom_call_target="tpu_custom_call" | custom-call | flops 8388608 | bytes 131072 | tf_op jit(solution)/shard_map/pallas_call | solution.py:669
  6.2 3.5 %collective-permute-start.3 = (f32[72,128]{1,0:T(8,128)S(1)}, f32[72,128]{1,0:T(8,128)S(1)}, u32[]{:S(2)}, u32[]{:S(2)}) collective-permute-start(f32[72,128]{1,0:T(8,128)S(1)} %add.25), channel_id=1, source_target_pairs={{0,6},{1,7},{2,4},{3,5},{4,2},{5,3},{6,0},{7,1},{8,14},{9,15},{10,... | collective-permute-start | bytes 110600 | tf_op jit(solution)/shard_map/ppermute | solution.py:695
  9.7 0.5 %collective-permute-start.2 = (f32[72,128]{1,0:T(8,128)S(1)}, f32[72,128]{1,0:T(8,128)S(1)}, u32[]{:S(2)}, u32[]{:S(2)}) collective-permute-start(f32[72,128]{1,0:T(8,128)S(1)} %add.25), channel_id=1, source_target_pairs={{0,4},{1,5},{2,6},{3,7},{4,0},{5,1},{6,2},{7,3},{8,12},{9,13},{10,... | collective-permute-start | bytes 110600 | tf_op jit(solution)/shard_map/ppermute | solution.py:695
  10.2 0.1 collective-permute-start.1
  10.3 1.5 %collective-permute-done.3 = f32[72,128]{1,0:T(8,128)S(1)} collective-permute-done((f32[72,128]{1,0:T(8,128)S(1)}, f32[72,128]{1,0:T(8,128)S(1)}, u32[]{:S(2)}, u32[]{:S(2)}) %collective-permute-start.3) | collective-permute-done | bytes 36896 | tf_op jit(solution)/shard_map/ppermute | solution.py:695
  11.8 1.8 %collective-permute-done.2 = f32[72,128]{1,0:T(8,128)S(1)} collective-permute-done((f32[72,128]{1,0:T(8,128)S(1)}, f32[72,128]{1,0:T(8,128)S(1)}, u32[]{:S(2)}, u32[]{:S(2)}) %collective-permute-start.2) | collective-permute-done | bytes 36896 | tf_op jit(solution)/shard_map/ppermute | solution.py:695
  13.6 0.5 %collective-permute-done.1 = f32[72,128]{1,0:T(8,128)S(1)} collective-permute-done((f32[72,128]{1,0:T(8,128)S(1)}, f32[72,128]{1,0:T(8,128)S(1)}, u32[]{:S(2)}, u32[]{:S(2)}) %collective-permute-start.1) | collective-permute-done | bytes 36896 | tf_op jit(solution)/shard_map/ppermute | solution.py:695
  14.2 3.7 %collective-permute-start.6 = (f32[72,128]{1,0:T(8,128)S(1)}, f32[72,128]{1,0:T(8,128)S(1)}, u32[]{:S(2)}, u32[]{:S(2)}) collective-permute-start(f32[72,128]{1,0:T(8,128)S(1)} %add_add_fusion.1), channel_id=1, source_target_pairs={{0,24},{1,25},{2,26},{3,27},{4,28},{5,29},{6,30},{7,31},{8,16},{9,... | collective-permute-start | bytes 110600 | tf_op jit(solution)/shard_map/ppermute | solution.py:695
  17.8 0.0 collective-permute-start.5
  17.8 0.8 %collective-permute-start.4 = (f32[72,128]{1,0:T(8,128)S(1)}, f32[72,128]{1,0:T(8,128)S(1)}, u32[]{:S(2)}, u32[]{:S(2)}) collective-permute-start(f32[72,128]{1,0:T(8,128)S(1)} %add_add_fusion.1), channel_id=1, source_target_pairs={{0,8},{1,9},{2,10},{3,11},{4,12},{5,13},{6,14},{7,15},{8,0},{9,1},... | collective-permute-start | bytes 110600 | tf_op jit(solution)/shard_map/ppermute | solution.py:695
  18.6 1.4 %shard_map.123 = (f32[2,256,128]{2,1,0:T(8,128)S(1)}, f32[2,16,256]{2,1,0:T(8,128)S(1)}) custom-call(f32[2,256,128]{2,1,0:T(8,128)S(1)} %get-tuple-element.26.y_in, f32[2,256,128]{2,1,0:T(8,128)S(1)} %get-tuple-element.27.z_in, f32[2,256,16]{2,1,0:T(8,128)S(1)} %get-tuple-element.22.medium), custom_call_target="tpu_custom_call" | custom-call | flops 16777216 | bytes 262144 | tf_op jit(solution)/shard_map/pallas_call | solution.py:669
  20.1 0.0 copy-start
  20.1 0.0 copy-start.1
  20.1 0.0 copy-start.2
  20.1 0.0 copy-start.4
  20.1 2.6 %collective-permute-done.5 = f32[72,128]{1,0:T(8,128)S(1)} collective-permute-done((f32[72,128]{1,0:T(8,128)S(1)}, f32[72,128]{1,0:T(8,128)S(1)}, u32[]{:S(2)}, u32[]{:S(2)}) %collective-permute-start.5) | collective-permute-done | bytes 36896 | tf_op jit(solution)/shard_map/ppermute | solution.py:695
  22.8 6.0 %shard_map.124 = (f32[192,256]{1,0:T(8,128)S(1)}, f32[192,256]{1,0:T(8,128)S(1)}) custom-call(s32[1]{0:T(128)} %bitcast.cfg_at, f32[72,128]{1,0:T(8,128)S(1)} %add_add_fusion.summed, f32[2,16,256]{2,1,0:T(8,128)S(1)} %get-tuple-element.28.y_row, f32[2,2,16,16]{3,2,1,0:T(8,128)S(1)} %copy-done.2, f32[2,2,16,16]{3,2,1,0:T(8,128)S(1)} %copy-done.3, ...), custom_call_target="tpu_custom_call" | custom-call | flops 67108864 | bytes 1048576 | tf_op jit(solution)/shard_map/pallas_call | solution.py:669
  28.8 0.1 collective-permute-start.7
  28.9 1.1 %shard_map.125.square = f32[2,256,128]{2,1,0:T(8,128)S(1)} custom-call(f32[2,256,128]{2,1,0:T(8,128)S(1)} %get-tuple-element.31.y_in, f32[2,256,128]{2,1,0:T(8,128)S(1)} %get-tuple-element.32.z_in), custom_call_target="tpu_custom_call" | custom-call | flops 16777216 | bytes 262144 | tf_op jit(solution)/shard_map/pallas_call | solution.py:669
  29.9 0.2 shard_map.126
  30.1 0.1 collective-permute-done.7.got
  30.3 1.0 %shard_map.127 = (f32[2,2,64,256]{3,2,1,0:T(8,128)}, f32[2,2,256,16]{3,2,1,0:T(8,128)}, f32[2,2,128]{2,1,0:T(2,128)}) custom-call(s32[1]{0:T(128)} %bitcast.cfg_at, f32[192,256]{1,0:T(8,128)S(1)} %get-tuple-element.29.kept, f32[192,256]{1,0:T(8,128)S(1)} %collective-permute-done.7.got, s32[1,128]{1,0:T(1,128)S(1)} %get-tuple-element.24.kmap, ...), custom_call_target="tpu_custom_call" | custom-call | flops 4194304 | bytes 65536 | tf_op jit(solution)/shard_map/pallas_call | solution.py:669
  (12 shorter events, 0.1 us)
Async XLA Ops:
  4.0 2.2 %collective-permute-start = (f32[72,128]{1,0:T(8,128)S(1)}, f32[72,128]{1,0:T(8,128)S(1)}, u32[]{:S(2)}, u32[]{:S(2)}) collective-permute-start(f32[72,128]{1,0:T(8,128)S(1)} %get-tuple-element.21.sent), channel_id=1, source_target_pairs={{0,1},{1,0},{2,3},{3,2},{4,5},{5,4},{6,7},{7,6},{8,9},{9,8},{10,11... | collective-permute-start | bytes 110600 | tf_op jit(solution)/shard_map/ppermute | solution.py:695
  6.2 5.7 %collective-permute-start.3 = (f32[72,128]{1,0:T(8,128)S(1)}, f32[72,128]{1,0:T(8,128)S(1)}, u32[]{:S(2)}, u32[]{:S(2)}) collective-permute-start(f32[72,128]{1,0:T(8,128)S(1)} %add.25), channel_id=1, source_target_pairs={{0,6},{1,7},{2,4},{3,5},{4,2},{5,3},{6,0},{7,1},{8,14},{9,15},{10,... | collective-permute-start | bytes 110600 | tf_op jit(solution)/shard_map/ppermute | solution.py:695
  9.7 4.0 %collective-permute-start.2 = (f32[72,128]{1,0:T(8,128)S(1)}, f32[72,128]{1,0:T(8,128)S(1)}, u32[]{:S(2)}, u32[]{:S(2)}) collective-permute-start(f32[72,128]{1,0:T(8,128)S(1)} %add.25), channel_id=1, source_target_pairs={{0,4},{1,5},{2,6},{3,7},{4,0},{5,1},{6,2},{7,3},{8,12},{9,13},{10,... | collective-permute-start | bytes 110600 | tf_op jit(solution)/shard_map/ppermute | solution.py:695
  10.2 4.0 %collective-permute-start.1 = (f32[72,128]{1,0:T(8,128)S(1)}, f32[72,128]{1,0:T(8,128)S(1)}, u32[]{:S(2)}, u32[]{:S(2)}) collective-permute-start(f32[72,128]{1,0:T(8,128)S(1)} %add.25), channel_id=1, source_target_pairs={{0,2},{1,3},{2,0},{3,1},{4,6},{5,7},{6,4},{7,5},{8,10},{9,11},{10,... | collective-permute-start | bytes 110600 | tf_op jit(solution)/shard_map/ppermute | solution.py:695
  14.2 6.0 %collective-permute-start.6 = (f32[72,128]{1,0:T(8,128)S(1)}, f32[72,128]{1,0:T(8,128)S(1)}, u32[]{:S(2)}, u32[]{:S(2)}) collective-permute-start(f32[72,128]{1,0:T(8,128)S(1)} %add_add_fusion.1), channel_id=1, source_target_pairs={{0,24},{1,25},{2,26},{3,27},{4,28},{5,29},{6,30},{7,31},{8,16},{9,... | collective-permute-start | bytes 110600 | tf_op jit(solution)/shard_map/ppermute | solution.py:695
  17.8 4.9 %collective-permute-start.5 = (f32[72,128]{1,0:T(8,128)S(1)}, f32[72,128]{1,0:T(8,128)S(1)}, u32[]{:S(2)}, u32[]{:S(2)}) collective-permute-start(f32[72,128]{1,0:T(8,128)S(1)} %add_add_fusion.1), channel_id=1, source_target_pairs={{0,16},{1,17},{2,18},{3,19},{4,20},{5,21},{6,22},{7,23},{8,24},{9,... | collective-permute-start | bytes 110600 | tf_op jit(solution)/shard_map/ppermute | solution.py:695
  17.8 4.9 %collective-permute-start.4 = (f32[72,128]{1,0:T(8,128)S(1)}, f32[72,128]{1,0:T(8,128)S(1)}, u32[]{:S(2)}, u32[]{:S(2)}) collective-permute-start(f32[72,128]{1,0:T(8,128)S(1)} %add_add_fusion.1), channel_id=1, source_target_pairs={{0,8},{1,9},{2,10},{3,11},{4,12},{5,13},{6,14},{7,15},{8,0},{9,1},... | collective-permute-start | bytes 110600 | tf_op jit(solution)/shard_map/ppermute | solution.py:695
  18.6 4.1 %copy-start.3 = (f32[2,2,16,16]{3,2,1,0:T(8,128)S(1)}, f32[2,2,16,16]{3,2,1,0:T(8,128)}, u32[]{:S(2)}) copy-start(f32[2,2,16,16]{3,2,1,0:T(8,128)} %shift_b.1) | copy-start | bytes 12292
  20.1 2.7 %copy-start = (bf16[128,256]{1,0:T(8,128)(2,1)S(1)}, bf16[128,256]{1,0:T(8,128)(2,1)}, u32[]{:S(2)}) copy-start(bf16[128,256]{1,0:T(8,128)(2,1)} %constant.18.clone.from_cells) | copy-start | bytes 196612
  20.1 2.6 %copy-start.1 = (bf16[256,128]{1,0:T(8,128)(2,1)S(1)}, bf16[256,128]{1,0:T(8,128)(2,1)}, u32[]{:S(2)}) copy-start(bf16[256,128]{1,0:T(8,128)(2,1)} %constant.17.clone.to_cells) | copy-start | bytes 196612
  20.1 2.6 %copy-start.2 = (f32[2,2,16,16]{3,2,1,0:T(8,128)S(1)}, f32[2,2,16,16]{3,2,1,0:T(8,128)}, u32[]{:S(2)}) copy-start(f32[2,2,16,16]{3,2,1,0:T(8,128)} %shift_a.1) | copy-start | bytes 12292
  20.1 2.6 %copy-start.4 = (f32[16,256]{1,0:T(8,128)S(1)}, f32[16,256]{1,0:T(8,128)}, u32[]{:S(2)}) copy-start(f32[16,256]{1,0:T(8,128)} %constant.19.clone.turn_rows) | copy-start | bytes 49156
  28.8 1.5 %collective-permute-start.7 = (f32[192,256]{1,0:T(8,128)S(1)}, f32[192,256]{1,0:T(8,128)S(1)}, u32[]{:S(2)}, u32[]{:S(2)}) collective-permute-start(f32[192,256]{1,0:T(8,128)S(1)} %get-tuple-element.30), channel_id=1, source_target_pairs={{0,1},{1,0},{2,3},{3,2},{4,5},{5,4},{6,7},{7,6},{8,9},{9,8},{10,11... | collective-permute-start | bytes 589832 | tf_op jit(solution)/shard_map/ppermute | solution.py:695

commit v7 on v6

--- a/solution.py
+++ b/solution.py
@@ -141,16 +141,27 @@
     return values[0]
 
 
-def by_momentum(row, chans, inner_first):
-    width = row.shape[1]
-    flat = chans * chans
-    outer, inner = iota((chans, flat), 1) // chans, iota((chans, flat), 1) % chans
-    at = inner if inner_first else outer
-    wide = mm_exact(row.T, (iota((chans, flat), 0) == at).astype(BF16), pieces=2)
-    lane = iota((width, flat), 1)
-    lane = lane // chans if inner_first else lane % chans
-    wide = jnp.where(iota((width, flat), 0) % chans == lane, wide, 0.0)
-    return jnp.sum(wide.reshape(width // chans, chans, flat), axis=1)
+def by_momentum(row, chans):
+    high, wide = row.shape[0] // 2, row.shape[1] // 2
+    tiles = [[row[i * high : (i + 1) * high, j * wide : (j + 1) * wide] for j in range(2)] for i in range(2)]
+    tiles[0][1], tiles[1][0] = tiles[1][0], tiles[0][1]
+    bit = high // 2
+    while bit:
+        step = bit * chans
+        low_row = iota((high, wide), 0) // bit % 2 == 0
+        low_lane = iota((high, wide), 1) // step % 2 == 0
+        for i in range(2):
+            for j in range(2):
+                tile = tiles[i][j]
+                ahead = pltpu.roll(pltpu.roll(tile, high - bit, 0), step, 1)
+                if 2 * bit == high:
+                    behind = ahead
+                else:
+                    behind = pltpu.roll(pltpu.roll(tile, bit, 0), wide - step, 1)
+                moved = jnp.where(low_row, ahead, behind)
+                tiles[i][j] = jnp.where(low_row == low_lane, tile, moved)
+        bit //= 2
+    return jnp.concatenate([jnp.concatenate(line, axis=1) for line in tiles], axis=0)
 
 
 def turned(value, turns, back=False):
@@ -322,10 +333,13 @@
 
     def write_o(base, real, imag):
         rows = pl.ds(pl.multiple_of(base, chans), chans)
-        out[0, rows, :] = real
-        out[1, rows, :] = imag
+        y_s[0, rows, :] = real
+        y_s[1, rows, :] = imag
 
     batch_mul(t_s, t_s, write_o, chans)
+    for part in range(2):
+        for col in range(chans):
+            out[part, col * chans : (col + 1) * chans, :] = y_s[part, pl.ds(col, chans, stride=chans), :]
 
 
 def square_own_kernel(y_in, z_in, medium, out, y_row, y_s, z_s, t_s):
@@ -367,7 +381,7 @@
     y_diag = tuple(block_diag(v, chans) for v in y_val)
     coarse = cadd(y_val, cscale(cmul(z_val, y_diag), 1.0 / per_moment))
 
-    coarse_rows = tuple(by_momentum(value, chans, False) for value in coarse)
+    coarse_rows = tuple(by_momentum(value, chans) for value in coarse)
     count_m = width // chans
     base_t = (shift_b[own, 0], shift_b[own, 1])
     step_t = (shift_a[own, 0] - base_t[0], shift_a[own, 1] - base_t[1])
@@ -593,7 +607,7 @@
         cmul(series[1], tuple(block_diag(v, chans) for v in v_one)),
         cscale(last, filled),
     )
-    change_rows = tuple(by_momentum(value, chans, True) for value in change)
+    change_rows = tuple(by_momentum(value, chans) for value in change)
     q_two = cscale(lead_rows[1], minus)
     kernels = (site_s[0, 0 : 3 * width, :], site_s[1, 0 : 3 * width, :])
     q_all = side_by_side(q_zero, q_one, q_two)

time: 31.4 us -> 30.7 us (0.978)
  Pallas kernels: 14 us -> 13.3 us
    pallas_call x7, Pallas kernels: 14 us -> 13.3 us  [call(): pl.pallas_call(body, out_shape=outs, in_specs=[SMEM_SPEC] * scalars + [sp...]
where the time goes in v7:
time: 30.7 us; the launch traced here: 30.5 us
  Pallas kernels  13.3 us (43%)
  starting transfers between devices  9.23 us (30%)
  waiting for transfers between devices  6.48 us (21%)
  between operations  1.44 us (5%)
    pallas_call x7, Pallas kernels, call(): pl.pallas_call(body, out_shape=outs, in_specs=[SMEM_SPEC] * scalars + [sp...  13.3 us
    ppermute x8, starting transfers between devices, swap(): lax.ppermute(value, ('ka', 'cfg'), [(i, i ^ mask) for i in range(total)])  9.23 us
    ppermute x8, waiting for transfers between devices, swap(): lax.ppermute(value, ('ka', 'cfg'), [(i, i ^ mask) for i in range(total)])  6.48 us
  transfers between devices with their start and end apart: 8, of which 5 were waited for; matrix products, arithmetic and copies ran while one was open for 0% of the time, Pallas kernels for 14%

profile of v7, /device:TPU:0, one launch (start us, length us, event | category | flops | bytes accessed | tf_op | source)
XLA Modules:
  0.0 30.5 jit_solution(13007937896925457389)
XLA Ops:
  1.3 2.7 %shard_map.121 = (f32[72,128]{1,0:T(8,128)S(1)}, f32[2,256,128]{2,1,0:T(8,128)S(1)}, f32[2,256,128]{2,1,0:T(8,128)S(1)}, f32[2,256,16]{2,1,0:T(8,128)S(1)}, f32[...) custom-call(s32[1]{0:T(128)} %bitcast.1.place, f32[1]{0:T(128)S(6)} %copy.13.weight, f32[2,2,256,16]{3,2,1,0:T(8,128)} %bitcast.6, ...), custom_call_target="tpu_custom_call" | custom-call | flops 8388608 | bytes 131072 | tf_op jit(solution)/shard_map/pallas_call | solution.py:683
  4.0 0.6 %collective-permute-start = (f32[72,128]{1,0:T(8,128)S(1)}, f32[72,128]{1,0:T(8,128)S(1)}, u32[]{:S(2)}, u32[]{:S(2)}) collective-permute-start(f32[72,128]{1,0:T(8,128)S(1)} %get-tuple-element.21.sent), channel_id=1, source_target_pairs={{0,1},{1,0},{2,3},{3,2},{4,5},{5,4},{6,7},{7,6},{8,9},{9,8},{10,11... | collective-permute-start | bytes 110600 | tf_op jit(solution)/shard_map/ppermute | solution.py:709
  4.5 1.6 %shard_map.122 = (f32[72,128]{1,0:T(8,128)S(1)}, f32[2,256,128]{2,1,0:T(8,128)S(1)}, f32[2,256,128]{2,1,0:T(8,128)S(1)}) custom-call(f32[72,128]{1,0:T(8,128)S(1)} %get-tuple-element.21.sent, f32[2,256,16]{2,1,0:T(8,128)S(1)} %get-tuple-element.22.medium, f32[2,256,128]{2,1,0:T(8,128)S(1)} %get-tuple-element.23.structure, s32[1,128]{1,0:T(1,128)S(1)} %get-tuple-element.24.kmap), custom_call_target="tpu_custom_call" | custom-call | flops 8388608 | bytes 131072 | tf_op jit(solution)/shard_map/pallas_call | solution.py:683
  6.2 3.5 %collective-permute-start.3 = (f32[72,128]{1,0:T(8,128)S(1)}, f32[72,128]{1,0:T(8,128)S(1)}, u32[]{:S(2)}, u32[]{:S(2)}) collective-permute-start(f32[72,128]{1,0:T(8,128)S(1)} %add.25), channel_id=1, source_target_pairs={{0,6},{1,7},{2,4},{3,5},{4,2},{5,3},{6,0},{7,1},{8,14},{9,15},{10,... | collective-permute-start | bytes 110600 | tf_op jit(solution)/shard_map/ppermute | solution.py:709
  9.7 0.5 %collective-permute-start.2 = (f32[72,128]{1,0:T(8,128)S(1)}, f32[72,128]{1,0:T(8,128)S(1)}, u32[]{:S(2)}, u32[]{:S(2)}) collective-permute-start(f32[72,128]{1,0:T(8,128)S(1)} %add.25), channel_id=1, source_target_pairs={{0,4},{1,5},{2,6},{3,7},{4,0},{5,1},{6,2},{7,3},{8,12},{9,13},{10,... | collective-permute-start | bytes 110600 | tf_op jit(solution)/shard_map/ppermute | solution.py:709
  10.2 0.1 collective-permute-start.1
  10.3 1.5 %collective-permute-done.3 = f32[72,128]{1,0:T(8,128)S(1)} collective-permute-done((f32[72,128]{1,0:T(8,128)S(1)}, f32[72,128]{1,0:T(8,128)S(1)}, u32[]{:S(2)}, u32[]{:S(2)}) %collective-permute-start.3) | collective-permute-done | bytes 36896 | tf_op jit(solution)/shard_map/ppermute | solution.py:709
  11.8 1.8 %collective-permute-done.2 = f32[72,128]{1,0:T(8,128)S(1)} collective-permute-done((f32[72,128]{1,0:T(8,128)S(1)}, f32[72,128]{1,0:T(8,128)S(1)}, u32[]{:S(2)}, u32[]{:S(2)}) %collective-permute-start.2) | collective-permute-done | bytes 36896 | tf_op jit(solution)/shard_map/ppermute | solution.py:709
  13.6 0.5 %collective-permute-done.1 = f32[72,128]{1,0:T(8,128)S(1)} collective-permute-done((f32[72,128]{1,0:T(8,128)S(1)}, f32[72,128]{1,0:T(8,128)S(1)}, u32[]{:S(2)}, u32[]{:S(2)}) %collective-permute-start.1) | collective-permute-done | bytes 36896 | tf_op jit(solution)/shard_map/ppermute | solution.py:709
  14.2 3.7 %collective-permute-start.6 = (f32[72,128]{1,0:T(8,128)S(1)}, f32[72,128]{1,0:T(8,128)S(1)}, u32[]{:S(2)}, u32[]{:S(2)}) collective-permute-start(f32[72,128]{1,0:T(8,128)S(1)} %add_add_fusion.1), channel_id=1, source_target_pairs={{0,24},{1,25},{2,26},{3,27},{4,28},{5,29},{6,30},{7,31},{8,16},{9,... | collective-permute-start | bytes 110600 | tf_op jit(solution)/shard_map/ppermute | solution.py:709
  17.8 0.0 collective-permute-start.5
  17.8 0.8 %collective-permute-start.4 = (f32[72,128]{1,0:T(8,128)S(1)}, f32[72,128]{1,0:T(8,128)S(1)}, u32[]{:S(2)}, u32[]{:S(2)}) collective-permute-start(f32[72,128]{1,0:T(8,128)S(1)} %add_add_fusion.1), channel_id=1, source_target_pairs={{0,8},{1,9},{2,10},{3,11},{4,12},{5,13},{6,14},{7,15},{8,0},{9,1},... | collective-permute-start | bytes 110600 | tf_op jit(solution)/shard_map/ppermute | solution.py:709
  18.6 1.5 %shard_map.123 = (f32[2,256,128]{2,1,0:T(8,128)S(1)}, f32[2,16,256]{2,1,0:T(8,128)S(1)}) custom-call(f32[2,256,128]{2,1,0:T(8,128)S(1)} %get-tuple-element.26.y_in, f32[2,256,128]{2,1,0:T(8,128)S(1)} %get-tuple-element.27.z_in, f32[2,256,16]{2,1,0:T(8,128)S(1)} %get-tuple-element.22.medium), custom_call_target="tpu_custom_call" | custom-call | flops 16777216 | bytes 262144 | tf_op jit(solution)/shard_map/pallas_call | solution.py:683
  20.1 0.0 copy-start
  20.1 0.0 copy-start.1
  20.1 0.0 copy-start.2
  20.1 0.0 copy-start.4
  20.2 2.5 %collective-permute-done.5 = f32[72,128]{1,0:T(8,128)S(1)} collective-permute-done((f32[72,128]{1,0:T(8,128)S(1)}, f32[72,128]{1,0:T(8,128)S(1)}, u32[]{:S(2)}, u32[]{:S(2)}) %collective-permute-start.5) | collective-permute-done | bytes 36896 | tf_op jit(solution)/shard_map/ppermute | solution.py:709
  22.8 5.2 %shard_map.124 = (f32[192,256]{1,0:T(8,128)S(1)}, f32[192,256]{1,0:T(8,128)S(1)}) custom-call(s32[1]{0:T(128)} %bitcast.cfg_at, f32[72,128]{1,0:T(8,128)S(1)} %add_add_fusion.summed, f32[2,16,256]{2,1,0:T(8,128)S(1)} %get-tuple-element.28.y_row, f32[2,2,16,16]{3,2,1,0:T(8,128)S(1)} %copy-done.2, f32[2,2,16,16]{3,2,1,0:T(8,128)S(1)} %copy-done.3, ...), custom_call_target="tpu_custom_call" | custom-call | flops 67108864 | bytes 1048576 | tf_op jit(solution)/shard_map/pallas_call | solution.py:683
  28.0 0.1 collective-permute-start.7
  28.1 1.1 %shard_map.125.square = f32[2,256,128]{2,1,0:T(8,128)S(1)} custom-call(f32[2,256,128]{2,1,0:T(8,128)S(1)} %get-tuple-element.31.y_in, f32[2,256,128]{2,1,0:T(8,128)S(1)} %get-tuple-element.32.z_in), custom_call_target="tpu_custom_call" | custom-call | flops 16777216 | bytes 262144 | tf_op jit(solution)/shard_map/pallas_call | solution.py:683
  29.2 0.2 shard_map.126
  29.4 0.1 collective-permute-done.7.got
  29.5 1.0 %shard_map.127 = (f32[2,2,64,256]{3,2,1,0:T(8,128)}, f32[2,2,256,16]{3,2,1,0:T(8,128)}, f32[2,2,128]{2,1,0:T(2,128)}) custom-call(s32[1]{0:T(128)} %bitcast.cfg_at, f32[192,256]{1,0:T(8,128)S(1)} %get-tuple-element.29.kept, f32[192,256]{1,0:T(8,128)S(1)} %collective-permute-done.7.got, s32[1,128]{1,0:T(1,128)S(1)} %get-tuple-element.24.kmap, ...), custom_call_target="tpu_custom_call" | custom-call | flops 4194304 | bytes 65536 | tf_op jit(solution)/shard_map/pallas_call | solution.py:683
  (12 shorter events, 0.1 us)
Async XLA Ops:
  4.0 2.2 %collective-permute-start = (f32[72,128]{1,0:T(8,128)S(1)}, f32[72,128]{1,0:T(8,128)S(1)}, u32[]{:S(2)}, u32[]{:S(2)}) collective-permute-start(f32[72,128]{1,0:T(8,128)S(1)} %get-tuple-element.21.sent), channel_id=1, source_target_pairs={{0,1},{1,0},{2,3},{3,2},{4,5},{5,4},{6,7},{7,6},{8,9},{9,8},{10,11... | collective-permute-start | bytes 110600 | tf_op jit(solution)/shard_map/ppermute | solution.py:709
  6.2 5.7 %collective-permute-start.3 = (f32[72,128]{1,0:T(8,128)S(1)}, f32[72,128]{1,0:T(8,128)S(1)}, u32[]{:S(2)}, u32[]{:S(2)}) collective-permute-start(f32[72,128]{1,0:T(8,128)S(1)} %add.25), channel_id=1, source_target_pairs={{0,6},{1,7},{2,4},{3,5},{4,2},{5,3},{6,0},{7,1},{8,14},{9,15},{10,... | collective-permute-start | bytes 110600 | tf_op jit(solution)/shard_map/ppermute | solution.py:709
  9.7 4.0 %collective-permute-start.2 = (f32[72,128]{1,0:T(8,128)S(1)}, f32[72,128]{1,0:T(8,128)S(1)}, u32[]{:S(2)}, u32[]{:S(2)}) collective-permute-start(f32[72,128]{1,0:T(8,128)S(1)} %add.25), channel_id=1, source_target_pairs={{0,4},{1,5},{2,6},{3,7},{4,0},{5,1},{6,2},{7,3},{8,12},{9,13},{10,... | collective-permute-start | bytes 110600 | tf_op jit(solution)/shard_map/ppermute | solution.py:709
  10.2 4.0 %collective-permute-start.1 = (f32[72,128]{1,0:T(8,128)S(1)}, f32[72,128]{1,0:T(8,128)S(1)}, u32[]{:S(2)}, u32[]{:S(2)}) collective-permute-start(f32[72,128]{1,0:T(8,128)S(1)} %add.25), channel_id=1, source_target_pairs={{0,2},{1,3},{2,0},{3,1},{4,6},{5,7},{6,4},{7,5},{8,10},{9,11},{10,... | collective-permute-start | bytes 110600 | tf_op jit(solution)/shard_map/ppermute | solution.py:709
  14.2 6.0 %collective-permute-start.6 = (f32[72,128]{1,0:T(8,128)S(1)}, f32[72,128]{1,0:T(8,128)S(1)}, u32[]{:S(2)}, u32[]{:S(2)}) collective-permute-start(f32[72,128]{1,0:T(8,128)S(1)} %add_add_fusion.1), channel_id=1, source_target_pairs={{0,24},{1,25},{2,26},{3,27},{4,28},{5,29},{6,30},{7,31},{8,16},{9,... | collective-permute-start | bytes 110600 | tf_op jit(solution)/shard_map/ppermute | solution.py:709
  17.8 4.9 %collective-permute-start.5 = (f32[72,128]{1,0:T(8,128)S(1)}, f32[72,128]{1,0:T(8,128)S(1)}, u32[]{:S(2)}, u32[]{:S(2)}) collective-permute-start(f32[72,128]{1,0:T(8,128)S(1)} %add_add_fusion.1), channel_id=1, source_target_pairs={{0,16},{1,17},{2,18},{3,19},{4,20},{5,21},{6,22},{7,23},{8,24},{9,... | collective-permute-start | bytes 110600 | tf_op jit(solution)/shard_map/ppermute | solution.py:709
  17.8 4.9 %collective-permute-start.4 = (f32[72,128]{1,0:T(8,128)S(1)}, f32[72,128]{1,0:T(8,128)S(1)}, u32[]{:S(2)}, u32[]{:S(2)}) collective-permute-start(f32[72,128]{1,0:T(8,128)S(1)} %add_add_fusion.1), channel_id=1, source_target_pairs={{0,8},{1,9},{2,10},{3,11},{4,12},{5,13},{6,14},{7,15},{8,0},{9,1},... | collective-permute-start | bytes 110600 | tf_op jit(solution)/shard_map/ppermute | solution.py:709
  18.6 4.1 %copy-start.3 = (f32[2,2,16,16]{3,2,1,0:T(8,128)S(1)}, f32[2,2,16,16]{3,2,1,0:T(8,128)}, u32[]{:S(2)}) copy-start(f32[2,2,16,16]{3,2,1,0:T(8,128)} %shift_b.1) | copy-start | bytes 12292
  20.1 2.6 %copy-start = (bf16[128,256]{1,0:T(8,128)(2,1)S(1)}, bf16[128,256]{1,0:T(8,128)(2,1)}, u32[]{:S(2)}) copy-start(bf16[128,256]{1,0:T(8,128)(2,1)} %constant.18.clone.from_cells) | copy-start | bytes 196612
  20.1 2.6 %copy-start.1 = (bf16[256,128]{1,0:T(8,128)(2,1)S(1)}, bf16[256,128]{1,0:T(8,128)(2,1)}, u32[]{:S(2)}) copy-start(bf16[256,128]{1,0:T(8,128)(2,1)} %constant.17.clone.to_cells) | copy-start | bytes 196612
  20.1 2.6 %copy-start.2 = (f32[2,2,16,16]{3,2,1,0:T(8,128)S(1)}, f32[2,2,16,16]{3,2,1,0:T(8,128)}, u32[]{:S(2)}) copy-start(f32[2,2,16,16]{3,2,1,0:T(8,128)} %shift_a.1) | copy-start | bytes 12292
  20.1 2.6 %copy-start.4 = (f32[16,256]{1,0:T(8,128)S(1)}, f32[16,256]{1,0:T(8,128)}, u32[]{:S(2)}) copy-start(f32[16,256]{1,0:T(8,128)} %constant.19.clone.turn_rows) | copy-start | bytes 49156
  28.0 1.5 %collective-permute-start.7 = (f32[192,256]{1,0:T(8,128)S(1)}, f32[192,256]{1,0:T(8,128)S(1)}, u32[]{:S(2)}, u32[]{:S(2)}) collective-permute-start(f32[192,256]{1,0:T(8,128)S(1)} %get-tuple-element.30), channel_id=1, source_target_pairs={{0,1},{1,0},{2,3},{3,2},{4,5},{5,4},{6,7},{7,6},{8,9},{9,8},{10,11... | collective-permute-start | bytes 589832 | tf_op jit(solution)/shard_map/ppermute | solution.py:709
